TPU v7x, 128 devices: a whole 4x4x4 slice. The times are simulated.
128 devices in a mesh: row: 8 (over x, core), col: 16 (over z, y).
Axes of the slice: x: 4, y: 4, z: 4, core: 2. Of those that a mesh axis runs over, the one named last changes fastest.
Arguments:
- luminance: float32 [1024, 8192], P('row', 'col'), may hold values from 0 to 1
- level_gain: float32 [5], replicated, may hold values from 0.5 to 2
Outputs:
- tone_mapped: float32 [1024, 8192], P('row', 'col')
All inputs are finite; a program needn't handle non-finite values.
Results may differ from a plain program's by a relative error of at most 0.00002.
Values sent between devices are 32-bit elements; how exact they have to be, the bound alone decides.
No kernel may reach another device: no remote copies, remote signals or barrier semaphores. Data moves between devices by JAX's collectives and lax.ppermute only.
A program may use at most 64 MiB of HBM per device.

v0:
```python
import jax
import jax.numpy as jnp
from jax import lax
from jax.sharding import PartitionSpec as P

CHANNELS = 16
LEVELS = 6


binomial = (0.0625, 0.25, 0.375, 0.25, 0.0625)
detail_boost = 1.0
base_slope = 0.5
spread_inverse = 1.0 / (2.0 * 0.025 * 0.025)


def with_halo(block, sides, width):
    for axis, dim in sides:
        count = lax.axis_size(axis)
        forward = [(i, i + 1) for i in range(count - 1)]
        forward.append((count - 1, 0))
        backward = [(target, source) for source, target in forward]
        low = lax.ppermute(
            lax.slice_in_dim(block, block.shape[dim] - width, None, axis=dim), axis, forward
        )
        high = lax.ppermute(lax.slice_in_dim(block, 0, width, axis=dim), axis, backward)
        block = jnp.concatenate([low, block, high], axis=dim)
    return block


def remap_tone(values, anchor, switch):
    offset = values - anchor
    return values + switch * (
        (base_slope - 1.0) * offset
        + detail_boost * offset * jnp.exp(-offset * offset * spread_inverse)
    )


def hat_weights(guidance, anchor):
    return jnp.maximum(0.0, 1.0 - jnp.abs(guidance - anchor) * (CHANNELS - 1))


def down_valid(padded):
    out_rows = (padded.shape[-2] - 4) // 2
    blurred = binomial[0] * padded[..., 0 : 2 * out_rows - 1 : 2, :]
    for step in range(1, 5):
        blurred = blurred + binomial[step] * padded[..., step : step + 2 * out_rows - 1 : 2, :]
    out_cols = (padded.shape[-1] - 4) // 2
    result = binomial[0] * blurred[..., 0 : 2 * out_cols - 1 : 2]
    for step in range(1, 5):
        result = result + binomial[step] * blurred[..., step : step + 2 * out_cols - 1 : 2]
    return result


def up_valid(coarse):
    rows_in = coarse.shape[-2]
    even_rows = (
        coarse[..., 0 : rows_in - 2, :]
        + 6.0 * coarse[..., 1 : rows_in - 1, :]
        + coarse[..., 2:rows_in, :]
    ) * 0.125
    odd_rows = (coarse[..., 1 : rows_in - 1, :] + coarse[..., 2:rows_in, :]) * 0.5
    joined = jnp.stack([even_rows, odd_rows], axis=-2)
    joined = joined.reshape(joined.shape[:-3] + (2 * (rows_in - 2), joined.shape[-1]))
    cols_in = joined.shape[-1]
    even_cols = (
        joined[..., 0 : cols_in - 2] + 6.0 * joined[..., 1 : cols_in - 1] + joined[..., 2:cols_in]
    ) * 0.125
    odd_cols = (joined[..., 1 : cols_in - 1] + joined[..., 2:cols_in]) * 0.5
    result = jnp.stack([even_cols, odd_cols], axis=-1)
    return result.reshape(result.shape[:-2] + (2 * (cols_in - 2),))


def trim_edges(values, margin_in, margin_out):
    cut_width = margin_in - margin_out
    if cut_width == 0:
        return values
    return values[
        ..., cut_width : values.shape[-2] - cut_width, cut_width : values.shape[-1] - cut_width
    ]


def channel_start(padded):
    channel_index = jnp.arange(CHANNELS + 1, dtype=jnp.int32)
    anchors = ((channel_index - 1).astype(jnp.float32) / (CHANNELS - 1))[:, None, None]
    switches = (channel_index > 0).astype(jnp.float32)[:, None, None]
    return down_valid(remap_tone(padded[None], anchors, switches))


def rim_levels(channels):
    return with_halo(channels, (("row", 1), ("col", 2)), 2)


def level_term(fine_all, guidance, coarse_channels, coarse_margin, margin_out, gain):
    kept_coarse = (margin_out + 1) // 2 + 1
    anchors = (jnp.arange(CHANNELS, dtype=jnp.int32).astype(jnp.float32) / (CHANNELS - 1))[
        :, None, None
    ]
    widened = up_valid(trim_edges(coarse_channels[1:], coarse_margin, kept_coarse))
    widened = trim_edges(widened, 2 * kept_coarse - 2, margin_out)
    detail = fine_all - widened
    running = jnp.sum(hat_weights(guidance[None], anchors) * detail, axis=0)
    return gain * running


def local(luminance, level_gain):
    padded = with_halo(luminance, (("row", 0), ("col", 1)), 2)
    pyramids = [None]
    margins = [2]
    current = channel_start(padded)
    for level_index in range(1, LEVELS):
        extended = rim_levels(current)
        pyramids.append(extended)
        margins.append(2)
        if level_index < LEVELS - 1:
            current = down_valid(extended)
    kept_margins = [0 for level_index in range(LEVELS)]
    anchors = (jnp.arange(CHANNELS, dtype=jnp.int32).astype(jnp.float32) / (CHANNELS - 1))[
        :, None, None
    ]
    coefficients = []
    for level_index in range(LEVELS - 1):
        margin_out = kept_margins[level_index]
        if level_index == 0:
            guidance = luminance
            fine_all = remap_tone(luminance[None], anchors, 1.0)
        else:
            guidance = trim_edges(pyramids[level_index][0], margins[level_index], margin_out)
            fine_all = trim_edges(pyramids[level_index][1:], margins[level_index], margin_out)
        coefficients.append(
            level_term(
                fine_all,
                guidance,
                pyramids[level_index + 1],
                margins[level_index + 1],
                margin_out,
                level_gain[level_index],
            )
        )
    result = trim_edges(pyramids[LEVELS - 1][0], margins[LEVELS - 1], kept_margins[LEVELS - 1])
    for level_index in reversed(range(LEVELS - 1)):
        widened = up_valid(with_halo(result, (("row", 0), ("col", 1)), 1))
        result = coefficients[level_index] + widened
    return result


def solution(mesh):
    placed = (P("row", "col"), P())
    return jax.shard_map(
        local, mesh=mesh, in_specs=placed, out_specs=P("row", "col"), check_vma=False
    )
```

profile of v0, /device:TPU:1, one launch (start us, length us, event | category | flops | bytes accessed | tf_op | source)
XLA Modules:
  0.0 526.8 jit_solution(2206188700469935484)
XLA Ops:
  0.7 2.6 collective-permute-start
  4.1 2.3 collective-permute-done.1
  8.7 5.0 collective-permute-start.3
  13.7 2.3 collective-permute-done.2
  17.2 2.7 fusion.1
  19.9 3.7 multiply_add_fusion
  23.6 40.6 %slice.617 = f32[17,64,256]{2,0,1:T(8,128)S(1)} slice(f32[17,64,516]{2,0,1:T(8,128)} %multiply_add_fusion), slice={[0:17:1], [0:64:1], [0:511:2]} | slice | bytes 2228224 | tf_op jit(solution)/shard_map/slice | solution.py:48
  64.2 41.0 %slice.618 = f32[17,64,256]{2,0,1:T(8,128)} slice(f32[17,64,516]{2,0,1:T(8,128)} %multiply_add_fusion), slice={[0:17:1], [0:64:1], [1:512:2]} | slice | bytes 2228224 | tf_op jit(solution)/shard_map/slice | solution.py:50
  105.1 41.0 %slice.619 = f32[17,64,256]{2,0,1:T(8,128)} slice(f32[17,64,516]{2,0,1:T(8,128)} %multiply_add_fusion), slice={[0:17:1], [0:64:1], [2:513:2]} | slice | bytes 2228224 | tf_op jit(solution)/shard_map/slice | solution.py:50
  146.1 41.1 %slice.620 = f32[17,64,256]{2,0,1:T(8,128)} slice(f32[17,64,516]{2,0,1:T(8,128)} %multiply_add_fusion), slice={[0:17:1], [0:64:1], [3:514:2]} | slice | bytes 2228224 | tf_op jit(solution)/shard_map/slice | solution.py:50
  187.2 41.0 %slice.621 = f32[17,64,256]{2,0,1:T(8,128)} slice(f32[17,64,516]{2,0,1:T(8,128)} %multiply_add_fusion), slice={[0:17:1], [0:64:1], [4:515:2]} | slice | bytes 2228224 | tf_op jit(solution)/shard_map/slice | solution.py:50
  228.2 3.4 multiply_add_fusion.1
  233.0 2.3 collective-permute-done.5
  238.4 5.7 %collective-permute-start.7 = (f32[17,68,2]{1,2,0:T(2,128)S(1)}, f32[17,68,2]{1,2,0:T(2,128)S(1)}, u32[]{:S(2)}, u32[]{:S(2)}) collective-permute-start(f32[17,68,2]{1,2,0:T(2,128)S(1)} %copy.88), channel_id=1, source_target_pairs={{1,0},{2,1},{3,2},{4,3},{5,4},{6,5},{7,6},{8,7},{9,8},{10,9},{11,1... | collective-permute-start | bytes 27752 | tf_op jit(solution)/shard_map/ppermute | solution.py:25
  247.7 2.8 pad_maximum_fusion.1
  251.8 13.3 %slice.641 = f32[17,32,128]{2,0,1:T(8,128)S(1)} slice(f32[17,32,260]{2,0,1:T(8,128)} %multiply_add_fusion.2), slice={[0:17:1], [0:32:1], [0:255:2]} | slice | bytes 557056 | tf_op jit(solution)/shard_map/slice | solution.py:48
  265.1 13.7 %slice.642 = f32[17,32,128]{2,0,1:T(8,128)} slice(f32[17,32,260]{2,0,1:T(8,128)} %multiply_add_fusion.2), slice={[0:17:1], [0:32:1], [1:256:2]} | slice | bytes 557056 | tf_op jit(solution)/shard_map/slice | solution.py:50
  278.8 13.7 %slice.643 = f32[17,32,128]{2,0,1:T(8,128)} slice(f32[17,32,260]{2,0,1:T(8,128)} %multiply_add_fusion.2), slice={[0:17:1], [0:32:1], [2:257:2]} | slice | bytes 557056 | tf_op jit(solution)/shard_map/slice | solution.py:50
  292.4 14.1 %slice.644 = f32[17,32,128]{2,0,1:T(8,128)} slice(f32[17,32,260]{2,0,1:T(8,128)} %multiply_add_fusion.2), slice={[0:17:1], [0:32:1], [3:258:2]} | slice | bytes 557056 | tf_op jit(solution)/shard_map/slice | solution.py:50
  306.5 13.7 %slice.645 = f32[17,32,128]{2,0,1:T(8,128)} slice(f32[17,32,260]{2,0,1:T(8,128)} %multiply_add_fusion.2), slice={[0:17:1], [0:32:1], [4:259:2]} | slice | bytes 557056 | tf_op jit(solution)/shard_map/slice | solution.py:50
  325.6 4.8 collective-permute-start.11
  331.9 6.0 %collective-permute-done.10 = f32[17,36,2]{2,0,1:T(8,128)S(1)} collective-permute-done((f32[17,36,2]{2,0,1:T(8,128)S(1)}, f32[17,36,2]{2,0,1:T(8,128)S(1)}, u32[]{:S(2)}, u32[]{:S(2)}) %collective-permute-start.10) | collective-permute-done | bytes 4928 | tf_op jit(solution)/shard_map/ppermute | solution.py:22
  340.7 4.1 slice.665
  344.8 4.0 slice.666
  348.8 4.0 slice.667
  352.8 4.0 slice.668
  356.8 4.0 slice.669
  362.1 3.2 collective-permute-start.12
  368.9 5.7 %collective-permute-start.15 = (f32[17,20,2]{2,0,1:T(8,128)S(1)}, f32[17,20,2]{2,0,1:T(8,128)S(1)}, u32[]{:S(2)}, u32[]{:S(2)}) collective-permute-start(f32[17,20,2]{2,0,1:T(8,128)S(1)} %get-tuple-element.30), channel_id=1, source_target_pairs={{1,0},{2,1},{3,2},{4,3},{5,4},{6,5},{7,6},{8,7},{9,8},{10,9},{11,1... | collective-permute-start | bytes 8168 | tf_op jit(solution)/shard_map/ppermute | solution.py:25
  377.6 2.2 collective-permute-done.14
  381.6 2.2 slice.689
  383.8 2.2 slice.690
  385.9 2.2 slice.691
  388.1 2.2 slice.692
  390.3 2.2 slice.693
  398.7 5.7 %collective-permute-start.19 = (f32[17,12,2]{2,0,1:T(8,128)}, f32[17,12,2]{2,0,1:T(8,128)}, u32[]{:S(2)}, u32[]{:S(2)}) collective-permute-start(f32[17,12,2]{2,0,1:T(8,128)} %get-tuple-element.38), channel_id=1, source_target_pairs={{1,0},{2,1},{3,2},{4,3},{5,4},{6,5},{7,6},{8,7},{9,8},{10,9},{11,1... | collective-permute-start | bytes 4904 | tf_op jit(solution)/shard_map/ppermute | solution.py:25
  406.2 2.8 copy.102
  409.0 2.3 copy.103
  416.3 1.6 slice.714
  417.9 1.6 slice.715
  419.6 1.6 slice.716
  421.2 1.6 slice.717
  425.0 2.4 collective-permute-start.21
  429.3 4.8 collective-permute-start.23
  435.6 2.2 copy.107
  437.8 1.9 copy.108
  441.8 1.7 copy.112
  443.5 1.6 copy.113
  446.7 3.3 collective-permute-start.25
  451.7 4.8 collective-permute-start.27
  461.0 4.1 collective-permute-start.29
  465.2 1.7 fusion.41
  467.0 5.1 collective-permute-start.31
  476.1 3.8 collective-permute-start.33
  481.2 5.2 collective-permute-start.35
  488.4 4.0 collective-permute-start.37
  492.4 2.3 pad_maximum_fusion.4
  494.6 4.0 copy.97
  498.7 3.8 copy.98
  502.6 5.5 %collective-permute-start.39 = (f32[34,1]{1,0:T(8,128)S(1)}, f32[34,1]{1,0:T(8,128)S(1)}, u32[]{:S(2)}, u32[]{:S(2)}) collective-permute-start(f32[34,1]{1,0:T(8,128)S(1)} %get-tuple-element.62), channel_id=1, source_target_pairs={{1,0},{2,1},{3,2},{4,3},{5,4},{6,5},{7,6},{8,7},{9,8},{10,9},{11,1... | collective-permute-start | bytes 416 | tf_op jit(solution)/shard_map/ppermute | solution.py:25
  508.1 2.3 fusion.22
  511.6 3.2 collective-permute-start.41
  516.2 4.8 collective-permute-start.43
  520.9 3.3 fusion.9
  (238 shorter events, 73.9 us)
Async XLA Ops:
  0.7 3.4 collective-permute-start
  3.3 3.0 collective-permute-start.1
  7.3 8.7 %collective-permute-start.2 = (f32[132,2]{1,0:T(8,128)S(1)}, f32[132,2]{1,0:T(8,128)S(1)}, u32[]{:S(2)}, u32[]{:S(2)}) collective-permute-start(f32[132,2]{1,0:T(8,128)S(1)} %get-tuple-element.21), channel_id=1, source_target_pairs={{0,1},{1,2},{2,3},{3,4},{4,5},{5,6},{6,7},{7,8},{8,9},{9,10},{10,1... | collective-permute-start | bytes 3176 | tf_op jit(solution)/shard_map/ppermute | solution.py:22
  8.7 7.3 %collective-permute-start.3 = (f32[132,2]{1,0:T(8,128)S(1)}, f32[132,2]{1,0:T(8,128)S(1)}, u32[]{:S(2)}, u32[]{:S(2)}) collective-permute-start(f32[132,2]{1,0:T(8,128)S(1)} %get-tuple-element.22), channel_id=1, source_target_pairs={{1,0},{2,1},{3,2},{4,3},{5,4},{6,5},{7,6},{8,7},{9,8},{10,9},{11,1... | collective-permute-start | bytes 3176 | tf_op jit(solution)/shard_map/ppermute | solution.py:25
  228.2 4.2 copy-start.16
  231.5 5.1 copy-start.1
  231.6 1.5 collective-permute-start.4
  231.8 3.5 collective-permute-start.5
  235.4 8.7 %copy-start.4 = (f32[128,512]{1,0:T(8,128)S(1)}, f32[128,512]{1,0:T(8,128)}, u32[]{:S(2)}) copy-start(f32[128,512]{1,0:T(8,128)} %param.2) | copy-start | bytes 786436
  238.0 7.0 %collective-permute-start.6 = (f32[17,68,2]{1,2,0:T(2,128)S(1)}, f32[17,68,2]{1,2,0:T(2,128)S(1)}, u32[]{:S(2)}, u32[]{:S(2)}) collective-permute-start(f32[17,68,2]{1,2,0:T(2,128)S(1)} %copy.87), channel_id=1, source_target_pairs={{0,1},{1,2},{2,3},{3,4},{4,5},{5,6},{6,7},{7,8},{8,9},{9,10},{10,1... | collective-permute-start | bytes 27752 | tf_op jit(solution)/shard_map/ppermute | solution.py:22
  238.4 8.0 %collective-permute-start.7 = (f32[17,68,2]{1,2,0:T(2,128)S(1)}, f32[17,68,2]{1,2,0:T(2,128)S(1)}, u32[]{:S(2)}, u32[]{:S(2)}) collective-permute-start(f32[17,68,2]{1,2,0:T(2,128)S(1)} %copy.88), channel_id=1, source_target_pairs={{1,0},{2,1},{3,2},{4,3},{5,4},{6,5},{7,6},{8,7},{9,8},{10,9},{11,1... | collective-permute-start | bytes 27752 | tf_op jit(solution)/shard_map/ppermute | solution.py:25
  244.1 205.8 %copy-start.14 = (f32[16]{0:T(128)}, f32[16]{0:T(128)S(1)}, u32[]{:S(2)}) copy-start(f32[16]{0:T(128)S(1)} %convert_multiply_fusion.1) | copy-start | bytes 196
  321.7 3.2 collective-permute-start.8
  322.1 3.3 collective-permute-start.9
  325.6 12.4 %collective-permute-start.10 = (f32[17,36,2]{2,0,1:T(8,128)S(1)}, f32[17,36,2]{2,0,1:T(8,128)S(1)}, u32[]{:S(2)}, u32[]{:S(2)}) collective-permute-start(f32[17,36,2]{2,0,1:T(8,128)S(1)} %get-tuple-element.17), channel_id=1, source_target_pairs={{0,1},{1,2},{2,3},{3,4},{4,5},{5,6},{6,7},{7,8},{8,9},{9,10},{10,1... | collective-permute-start | bytes 14696 | tf_op jit(solution)/shard_map/ppermute | solution.py:22
  325.6 12.3 %collective-permute-start.11 = (f32[17,36,2]{2,0,1:T(8,128)S(1)}, f32[17,36,2]{2,0,1:T(8,128)S(1)}, u32[]{:S(2)}, u32[]{:S(2)}) collective-permute-start(f32[17,36,2]{2,0,1:T(8,128)S(1)} %get-tuple-element.18), channel_id=1, source_target_pairs={{1,0},{2,1},{3,2},{4,3},{5,4},{6,5},{7,6},{8,7},{9,8},{10,9},{11,1... | collective-permute-start | bytes 14696 | tf_op jit(solution)/shard_map/ppermute | solution.py:25
  338.3 1.5 copy-start
  362.1 17.7 %copy-start.3 = (f32[17,16,64]{2,0,1:T(8,128)}, f32[17,16,64]{2,0,1:T(8,128)S(1)}, u32[]{:S(2)}) copy-start(f32[17,16,64]{2,0,1:T(8,128)S(1)} %multiply_add_fusion.5) | copy-start | bytes 208900
  362.1 4.9 collective-permute-start.12
  365.4 3.3 collective-permute-start.13
  368.8 11.1 %collective-permute-start.14 = (f32[17,20,2]{2,0,1:T(8,128)S(1)}, f32[17,20,2]{2,0,1:T(8,128)S(1)}, u32[]{:S(2)}, u32[]{:S(2)}) collective-permute-start(f32[17,20,2]{2,0,1:T(8,128)S(1)} %get-tuple-element.29), channel_id=1, source_target_pairs={{0,1},{1,2},{2,3},{3,4},{4,5},{5,6},{6,7},{7,8},{8,9},{9,10},{10,1... | collective-permute-start | bytes 8168 | tf_op jit(solution)/shard_map/ppermute | solution.py:22
  368.9 11.0 %collective-permute-start.15 = (f32[17,20,2]{2,0,1:T(8,128)S(1)}, f32[17,20,2]{2,0,1:T(8,128)S(1)}, u32[]{:S(2)}, u32[]{:S(2)}) collective-permute-start(f32[17,20,2]{2,0,1:T(8,128)S(1)} %get-tuple-element.30), channel_id=1, source_target_pairs={{1,0},{2,1},{3,2},{4,3},{5,4},{6,5},{7,6},{8,7},{9,8},{10,9},{11,1... | collective-permute-start | bytes 8168 | tf_op jit(solution)/shard_map/ppermute | solution.py:25
  380.1 0.9 copy-start.2
  394.6 3.4 copy-start.6
  394.6 2.3 collective-permute-start.16
  394.7 3.3 collective-permute-start.17
  396.9 8.4 %copy-start.12 = (f32[17,2,32]{2,0,1:T(8,128)}, f32[17,2,32]{2,0,1:T(8,128)S(1)}, u32[]{:S(2)}) copy-start(f32[17,2,32]{2,0,1:T(8,128)S(1)} %collective-permute-done.16) | copy-start | bytes 13060
  397.9 7.3 %copy-start.13 = (f32[17,2,32]{2,0,1:T(8,128)}, f32[17,2,32]{2,0,1:T(8,128)S(1)}, u32[]{:S(2)}) copy-start(f32[17,2,32]{2,0,1:T(8,128)S(1)} %collective-permute-done.17) | copy-start | bytes 13060
  398.7 13.3 %collective-permute-start.18 = (f32[17,12,2]{2,0,1:T(8,128)}, f32[17,12,2]{2,0,1:T(8,128)}, u32[]{:S(2)}, u32[]{:S(2)}) collective-permute-start(f32[17,12,2]{2,0,1:T(8,128)} %get-tuple-element.37), channel_id=1, source_target_pairs={{0,1},{1,2},{2,3},{3,4},{4,5},{5,6},{6,7},{7,8},{8,9},{9,10},{10,1... | collective-permute-start | bytes 4904 | tf_op jit(solution)/shard_map/ppermute | solution.py:22
  398.7 13.3 %collective-permute-start.19 = (f32[17,12,2]{2,0,1:T(8,128)}, f32[17,12,2]{2,0,1:T(8,128)}, u32[]{:S(2)}, u32[]{:S(2)}) collective-permute-start(f32[17,12,2]{2,0,1:T(8,128)} %get-tuple-element.38), channel_id=1, source_target_pairs={{1,0},{2,1},{3,2},{4,3},{5,4},{6,5},{7,6},{8,7},{9,8},{10,9},{11,1... | collective-permute-start | bytes 4904 | tf_op jit(solution)/shard_map/ppermute | solution.py:25
  413.2 0.8 copy-start.5
  424.7 3.9 copy-start.7
  424.7 3.3 collective-permute-start.20
  425.0 3.5 collective-permute-start.21
  428.0 6.8 %copy-start.10 = (f32[17,2,16]{2,0,1:T(8,128)}, f32[17,2,16]{2,0,1:T(8,128)S(1)}, u32[]{:S(2)}) copy-start(f32[17,2,16]{2,0,1:T(8,128)S(1)} %collective-permute-done.20) | copy-start | bytes 6532
  428.5 6.3 %copy-start.11 = (f32[17,2,16]{2,0,1:T(8,128)}, f32[17,2,16]{2,0,1:T(8,128)S(1)}, u32[]{:S(2)}) copy-start(f32[17,2,16]{2,0,1:T(8,128)S(1)} %collective-permute-done.21) | copy-start | bytes 6532
  429.3 10.5 %collective-permute-start.22 = (f32[17,8,2]{2,0,1:T(8,128)}, f32[17,8,2]{2,0,1:T(8,128)}, u32[]{:S(2)}, u32[]{:S(2)}) collective-permute-start(f32[17,8,2]{2,0,1:T(8,128)} %get-tuple-element.45), channel_id=1, source_target_pairs={{0,1},{1,2},{2,3},{3,4},{4,5},{5,6},{6,7},{7,8},{8,9},{9,10},{10,1... | collective-permute-start | bytes 3272 | tf_op jit(solution)/shard_map/ppermute | solution.py:22
  429.3 10.5 %collective-permute-start.23 = (f32[17,8,2]{2,0,1:T(8,128)}, f32[17,8,2]{2,0,1:T(8,128)}, u32[]{:S(2)}, u32[]{:S(2)}) collective-permute-start(f32[17,8,2]{2,0,1:T(8,128)} %get-tuple-element.46), channel_id=1, source_target_pairs={{1,0},{2,1},{3,2},{4,3},{5,4},{6,5},{7,6},{8,7},{9,8},{10,9},{11,1... | collective-permute-start | bytes 3272 | tf_op jit(solution)/shard_map/ppermute | solution.py:25
  446.1 5.5 %collective-permute-start.24 = (f32[1,16]{1,0:T(1,128)S(1)}, f32[1,16]{1,0:T(1,128)S(1)}, u32[]{:S(2)}, u32[]{:S(2)}) collective-permute-start(f32[1,16]{1,0:T(1,128)S(1)} %get-tuple-element.87), channel_id=1, source_target_pairs={{0,16},{16,32},{32,48},{48,64},{64,80},{80,96},{96,112},{112,0},{1... | collective-permute-start | bytes 200 | tf_op jit(solution)/shard_map/ppermute | solution.py:22
  446.7 4.9 collective-permute-start.25
  451.7 5.8 %collective-permute-start.26 = (f32[6,1]{1,0:T(8,128)S(1)}, f32[6,1]{1,0:T(8,128)S(1)}, u32[]{:S(2)}, u32[]{:S(2)}) collective-permute-start(f32[6,1]{1,0:T(8,128)S(1)} %get-tuple-element.85), channel_id=1, source_target_pairs={{0,1},{1,2},{2,3},{3,4},{4,5},{5,6},{6,7},{7,8},{8,9},{9,10},{10,1... | collective-permute-start | bytes 80 | tf_op jit(solution)/shard_map/ppermute | solution.py:22
  451.7 5.8 %collective-permute-start.27 = (f32[6,1]{1,0:T(8,128)S(1)}, f32[6,1]{1,0:T(8,128)S(1)}, u32[]{:S(2)}, u32[]{:S(2)}) collective-permute-start(f32[6,1]{1,0:T(8,128)S(1)} %get-tuple-element.86), channel_id=1, source_target_pairs={{1,0},{2,1},{3,2},{4,3},{5,4},{6,5},{7,6},{8,7},{9,8},{10,9},{11,1... | collective-permute-start | bytes 80 | tf_op jit(solution)/shard_map/ppermute | solution.py:25
  461.0 5.8 %collective-permute-start.28 = (f32[1,32]{1,0:T(1,128)S(1)}, f32[1,32]{1,0:T(1,128)S(1)}, u32[]{:S(2)}, u32[]{:S(2)}) collective-permute-start(f32[1,32]{1,0:T(1,128)S(1)} %get-tuple-element.79), channel_id=1, source_target_pairs={{0,16},{16,32},{32,48},{48,64},{64,80},{80,96},{96,112},{112,0},{1... | collective-permute-start | bytes 392 | tf_op jit(solution)/shard_map/ppermute | solution.py:22
  461.0 5.8 %collective-permute-start.29 = (f32[1,32]{1,0:T(1,128)S(1)}, f32[1,32]{1,0:T(1,128)S(1)}, u32[]{:S(2)}, u32[]{:S(2)}) collective-permute-start(f32[1,32]{1,0:T(1,128)S(1)} %get-tuple-element.80), channel_id=1, source_target_pairs={{16,0},{32,16},{48,32},{64,48},{80,64},{96,80},{112,96},{0,112},{1... | collective-permute-start | bytes 392 | tf_op jit(solution)/shard_map/ppermute | solution.py:25
  467.0 6.1 %collective-permute-start.30 = (f32[10,1]{1,0:T(8,128)S(1)}, f32[10,1]{1,0:T(8,128)S(1)}, u32[]{:S(2)}, u32[]{:S(2)}) collective-permute-start(f32[10,1]{1,0:T(8,128)S(1)} %get-tuple-element.77), channel_id=1, source_target_pairs={{0,1},{1,2},{2,3},{3,4},{4,5},{5,6},{6,7},{7,8},{8,9},{9,10},{10,1... | collective-permute-start | bytes 128 | tf_op jit(solution)/shard_map/ppermute | solution.py:22
  467.0 6.1 %collective-permute-start.31 = (f32[10,1]{1,0:T(8,128)S(1)}, f32[10,1]{1,0:T(8,128)S(1)}, u32[]{:S(2)}, u32[]{:S(2)}) collective-permute-start(f32[10,1]{1,0:T(8,128)S(1)} %get-tuple-element.78), channel_id=1, source_target_pairs={{1,0},{2,1},{3,2},{4,3},{5,4},{6,5},{7,6},{8,7},{9,8},{10,9},{11,1... | collective-permute-start | bytes 128 | tf_op jit(solution)/shard_map/ppermute | solution.py:25
  476.1 4.9 collective-permute-start.32
  476.1 5.0 collective-permute-start.33
  481.2 6.2 %collective-permute-start.34 = (f32[18,1]{1,0:T(8,128)S(1)}, f32[18,1]{1,0:T(8,128)S(1)}, u32[]{:S(2)}, u32[]{:S(2)}) collective-permute-start(f32[18,1]{1,0:T(8,128)S(1)} %get-tuple-element.69), channel_id=1, source_target_pairs={{0,1},{1,2},{2,3},{3,4},{4,5},{5,6},{6,7},{7,8},{8,9},{9,10},{10,1... | collective-permute-start | bytes 224 | tf_op jit(solution)/shard_map/ppermute | solution.py:22
  481.2 6.2 %collective-permute-start.35 = (f32[18,1]{1,0:T(8,128)S(1)}, f32[18,1]{1,0:T(8,128)S(1)}, u32[]{:S(2)}, u32[]{:S(2)}) collective-permute-start(f32[18,1]{1,0:T(8,128)S(1)} %get-tuple-element.70), channel_id=1, source_target_pairs={{1,0},{2,1},{3,2},{4,3},{5,4},{6,5},{7,6},{8,7},{9,8},{10,9},{11,1... | collective-permute-start | bytes 224 | tf_op jit(solution)/shard_map/ppermute | solution.py:25
  488.4 14.1 %collective-permute-start.36 = (f32[1,128]{1,0:T(1,128)S(1)}, f32[1,128]{1,0:T(1,128)S(1)}, u32[]{:S(2)}, u32[]{:S(2)}) collective-permute-start(f32[1,128]{1,0:T(1,128)S(1)} %get-tuple-element.63), channel_id=1, source_target_pairs={{0,16},{16,32},{32,48},{48,64},{64,80},{80,96},{96,112},{112,0},{1... | collective-permute-start | bytes 1544 | tf_op jit(solution)/shard_map/ppermute | solution.py:22
  488.4 14.1 %collective-permute-start.37 = (f32[1,128]{1,0:T(1,128)S(1)}, f32[1,128]{1,0:T(1,128)S(1)}, u32[]{:S(2)}, u32[]{:S(2)}) collective-permute-start(f32[1,128]{1,0:T(1,128)S(1)} %get-tuple-element.64), channel_id=1, source_target_pairs={{16,0},{32,16},{48,32},{64,48},{80,64},{96,80},{112,96},{0,112},{1... | collective-permute-start | bytes 1544 | tf_op jit(solution)/shard_map/ppermute | solution.py:25
  498.7 9.4 %copy-start.9 = (f32[64,256]{1,0:T(8,128)S(1)}, f32[64,256]{1,0:T(8,128)}, u32[]{:S(2)}) copy-start(f32[64,256]{1,0:T(8,128)} %slice.791) | copy-start | bytes 196612
  498.7 9.4 %copy-start.15 = (f32[16]{0:T(128)S(1)}, f32[16]{0:T(128)}, u32[]{:S(2)}) copy-start(f32[16]{0:T(128)} %copy-done.14) | copy-start | bytes 196
  502.6 7.8 %collective-permute-start.38 = (f32[34,1]{1,0:T(8,128)S(1)}, f32[34,1]{1,0:T(8,128)S(1)}, u32[]{:S(2)}, u32[]{:S(2)}) collective-permute-start(f32[34,1]{1,0:T(8,128)S(1)} %get-tuple-element.61), channel_id=1, source_target_pairs={{0,1},{1,2},{2,3},{3,4},{4,5},{5,6},{6,7},{7,8},{8,9},{9,10},{10,1... | collective-permute-start | bytes 416 | tf_op jit(solution)/shard_map/ppermute | solution.py:22
  502.6 7.8 %collective-permute-start.39 = (f32[34,1]{1,0:T(8,128)S(1)}, f32[34,1]{1,0:T(8,128)S(1)}, u32[]{:S(2)}, u32[]{:S(2)}) collective-permute-start(f32[34,1]{1,0:T(8,128)S(1)} %get-tuple-element.62), channel_id=1, source_target_pairs={{1,0},{2,1},{3,2},{4,3},{5,4},{6,5},{7,6},{8,7},{9,8},{10,9},{11,1... | collective-permute-start | bytes 416 | tf_op jit(solution)/shard_map/ppermute | solution.py:25
  511.6 4.4 collective-permute-start.40
  511.6 4.4 collective-permute-start.41
  514.9 6.1 %copy-start.8 = (f32[128,256,2]{1,0,2:T(8,128)S(1)}, f32[128,256,2]{1,0,2:T(8,128)}, u32[]{:S(2)}) copy-start(f32[128,256,2]{1,0,2:T(8,128)} %copy.86) | copy-start | bytes 786436
  516.1 8.1 %collective-permute-start.42 = (f32[66,1]{1,0:T(8,128)S(1)}, f32[66,1]{1,0:T(8,128)S(1)}, u32[]{:S(2)}, u32[]{:S(2)}) collective-permute-start(f32[66,1]{1,0:T(8,128)S(1)} %get-tuple-element.49), channel_id=1, source_target_pairs={{0,1},{1,2},{2,3},{3,4},{4,5},{5,6},{6,7},{7,8},{8,9},{9,10},{10,1... | collective-permute-start | bytes 800 | tf_op jit(solution)/shard_map/ppermute | solution.py:22
  516.2 8.1 %collective-permute-start.43 = (f32[66,1]{1,0:T(8,128)S(1)}, f32[66,1]{1,0:T(8,128)S(1)}, u32[]{:S(2)}, u32[]{:S(2)}) collective-permute-start(f32[66,1]{1,0:T(8,128)S(1)} %get-tuple-element.50), channel_id=1, source_target_pairs={{1,0},{2,1},{3,2},{4,3},{5,4},{6,5},{7,6},{8,7},{9,8},{10,9},{11,1... | collective-permute-start | bytes 800 | tf_op jit(solution)/shard_map/ppermute | solution.py:25
where the time goes:
time: 534 us; the launch traced here: 527 us
  local copies, waits for them, and re-layouts  353 us (66%)
  starting transfers between devices  90.8 us (17%)
  other arithmetic  58.4 us (11%)
  waiting for transfers between devices  23.6 us (4%)
    slice x20, local copies, waits for them, and re-layouts, down_valid(): blurred[..., step:step + 2 * out_cols - 1:2]  250 us
    ppermute x22, starting transfers between devices, with_halo(): lax.ppermute(lax.slice_in_dim(block, 0, width, axis=dim), axis, backward)  81.7 us
    slice x5, local copies, waits for them, and re-layouts, down_valid(): result = binomial[0] * blurred[..., 0:2 * out_cols - 1:2]  61.8 us
    ppermute x22, waiting for transfers between devices, with_halo(): lax.ppermute(lax.slice_in_dim(block, block.shape[dim] - width, None, axis...  15.4 us
    another operation x8, local copies, waits for them, and re-layouts, up_valid(): result = jnp.stack([even_cols, odd_cols], axis=-1)  12.3 us
    reshape x8, local copies, waits for them, and re-layouts, up_valid(): return result.reshape(result.shape[:-2] + (2 * (cols_in - 2),))  11.4 us
  transfers between devices with their start and end apart: 44, of which 16 were waited for; matrix products, arithmetic and copies ran while one was open for 9% of the time, Pallas kernels for 0%

commit v1 on v0

v1 whole, which is shorter than its diff:
```python
import math

import jax
import jax.numpy as jnp
from jax import lax
from jax.experimental import pallas as pl
from jax.experimental.pallas import tpu as pltpu
from jax.sharding import PartitionSpec as P


ROWS = 320
LANES = 128
HALF = 8
STEP = 1.0 / 15.0
BETA = math.sqrt(800.0 * math.log2(math.e))
F32 = jnp.float32


def iota(shape, dim):
    return lax.broadcasted_iota(jnp.int32, shape, dim)


def left(x, n=1):
    return pltpu.roll(x, LANES - n, axis=x.ndim - 1)


def right(x, n=1):
    return pltpu.roll(x, n, axis=x.ndim - 1)


def pick(x, idx):
    return jnp.take_along_axis(x, idx, axis=1)


def select_columns(x, table):
    hi = x.astype(jnp.bfloat16)
    rest = x - hi.astype(F32)
    mid = rest.astype(jnp.bfloat16)
    low = (rest - mid.astype(F32)).astype(jnp.bfloat16)
    dot = lambda part: jnp.dot(part, table, preferred_element_type=F32)
    return dot(hi) + dot(mid) + dot(low)


def spread(ref, *index):
    return ref[index[:-1] + (pl.ds(index[-1], HALF, stride=0), slice(None))]


def fold(y0, y1, y2, y3, y4):
    return (y0 + y4) + 6.0 * y2 + 4.0 * (y1 + y3)


def bump(lum, anchor):
    u = lum - anchor
    return u * jnp.exp2(-(u * u))


def columns_from_four(y):
    y0, y1, y2, y3 = y
    return (
        fold(right(y2), right(y3), y0, y1, y2),
        fold(y0, y1, y2, y3, left(y0)),
    )


def columns_from_two(y):
    y0, y1 = y
    return fold(right(y0), right(y1), y0, y1, left(y0))


def columns_strided(y, n):
    return fold(right(y, 2 * n), right(y, n), y, left(y, n), left(y, 2 * n))


def channel_chain(lum, anchors, d1, d2, d3):
    groups = len(anchors)

    def row(e):
        values = [spread(lum, c, e) for c in range(4)]
        return [[bump(v, a) for v in values] for a in anchors]

    def step(i, state):
        pair, even, odd_before = state
        odd = row(2 * i + 1)
        even_next = row(2 * i + 2)
        new_pair = [[None] * 4 for g in range(groups)]
        for g in range(groups):
            y = []
            for c in range(4):
                new_pair[g][c] = even[g][c] + even_next[g][c]
                y.append(
                    (pair[g][c] + new_pair[g][c])
                    + 4.0 * (even[g][c] + (odd_before[g][c] + odd[g][c]))
                )
            out = columns_from_four(y)
            d1[i, 2 * g] = out[0]
            d1[i, 2 * g + 1] = out[1]
        return new_pair, even_next, odd

    def body(t, state):
        state = step(2 * t + 1, state)
        return step(2 * t + 2, state)

    first = row(0)
    second = row(2)
    pair = [[a + b for a, b in zip(x, y)] for x, y in zip(first, second)]
    lax.fori_loop(0, 79, body, (pair, second, row(1)))

    def second_level(i, carry):
        for g in range(groups):
            y = [fold(*[d1[2 * i + s - 2, 2 * g + c] for s in range(5)]) for c in range(2)]
            d2[i, g] = columns_from_two(y)
        return carry

    lax.fori_loop(2, 79, second_level, 0)

    def third_level(i, carry):
        for g in range(groups):
            d3[i, g] = columns_strided(fold(*[d2[2 * i + s - 2, g] for s in range(5)]), 1)
        return carry

    lax.fori_loop(2, 39, third_level, 0)


def rows_blurred(ref, c, base, count):
    return fold(*[ref[c, pl.ds(base + s - 2, count, stride=2), :] for s in range(5)])


def guide_chain(lum, scale, g1, g2, g3):
    def first(t, carry):
        i = 8 * t + 8
        y = [rows_blurred(lum, c, 2 * i, 8) for c in range(4)]
        out = columns_from_four(y)
        g1[0, pl.ds(i, 8), :] = out[0] * (scale / 256.0)
        g1[1, pl.ds(i, 8), :] = out[1] * (scale / 256.0)
        return carry

    lax.fori_loop(0, 18, first, 0)
    for i in (1, 151):
        y = [rows_blurred(lum, c, 2 * i, 8) for c in range(4)]
        out = columns_from_four(y)
        g1[0, i : i + 8, :] = out[0] * (scale / 256.0)
        g1[1, i : i + 8, :] = out[1] * (scale / 256.0)
    for i in (2, 8, 16, 24, 32, 40, 48, 56, 64, 71):
        y = [rows_blurred(g1, c, 2 * i, 8) for c in range(2)]
        g2[0, i : i + 8, :] = columns_from_two(y) * (1.0 / 256.0)
    for i in (2, 8, 16, 24, 31):
        g3[i : i + 8, :] = columns_strided(rows_blurred(g2, 0, 2 * i, 8), 1) * (1.0 / 256.0)


def anchor_tile(base):
    return (iota((HALF, LANES), 0) + base).astype(F32)


def kernel_a(top, mid, bottom, d1, d2, d3, x15, g1, g2, g3, base_term, lum):
    source = iota((512, 512), 0)
    target = iota((512, 512), 1)
    table = jnp.where(source == 4 * (target % LANES) + target // LANES, 1.0, 0.0).astype(jnp.bfloat16)
    for ref, start, count in ((top, 0, 96), (mid, 96, 128), (bottom, 224, 96)):
        phases = select_columns(ref[...], table)
        for c in range(4):
            part = phases[:, c * LANES : (c + 1) * LANES]
            lum[c, start : start + count, :] = part * BETA
            if start == 96:
                x15[c] = part * 15.0
    guide_chain(lum, 1.0 / BETA, g1, g2, g3)
    anchors = [anchor_tile(HALF * g) * (BETA * STEP) for g in range(2)]
    channel_chain(lum, anchors, d1, d2, d3)

    def natural(t, carry):
        rows = pl.ds(pl.multiple_of(8 * t, 8), 8)
        value = mid[rows, :]
        place = value * 15.0
        lower = jnp.floor(place)
        part = place - lower
        near = value - lower * STEP
        far = value - (lower + 1.0) * STEP
        bend = (1.0 - part) * near * jnp.exp(near * near * -800.0) + part * far * jnp.exp(far * far * -800.0)
        base_term[rows, :] = 0.5 * value + bend
        return carry

    lax.fori_loop(0, 16, natural, 0)


def hat(place, channel):
    return jnp.maximum(0.0, 1.0 - jnp.abs(place - channel))


def total(x):
    return jnp.sum(x, axis=0, keepdims=True)


def rows_up(before, here, after):
    later = here + after
    return here + 0.25 * ((before + here) + later), later


def tiles(ref, index, count):
    return [ref[index + (slice(8 * t, 8 * t + 8), slice(None))] for t in range(count)]


def kernel_b(
    gain_ref, far_left, near_left, near_right, far_right, d1, d2, d3, x15, g1, g2, g3, base_term, out,
    lum, s1, s2, s3, h1, h2, h3, f1, f2, b3, b4, b5, e3, e4, e5,
    c4, c3, c2a, c2s, c1a, c1s, r5, r4, u4, r3, u3, w2, r2a, r2s, wide_a, wide_s, k1, k2, rest,
):
    gains = [gain_ref[i] for i in range(5)]
    lane = iota((HALF, LANES), 1)
    channel = [anchor_tile(HALF * g) for g in range(2)]
    split = anchor_tile(0) + jnp.where(lane >= 64, 8.0, 0.0)

    source = iota((512, 512), 0)
    target = iota((512, 512), 1)
    wanted = 32 + 320 * ((target // 32) % 2) + 4 * (target % 32) + target // LANES
    table = jnp.where(source == wanted, 1.0, 0.0).astype(jnp.bfloat16)
    for start in range(0, ROWS, 160):
        part = slice(start, start + 160)
        natural = jnp.concatenate(
            [far_left[part, :], near_left[part, :], near_right[part, :], far_right[part, :]], axis=1
        )
        phases = select_columns(natural, table)
        for c in range(4):
            lum[c, part, :] = phases[:, c * LANES : (c + 1) * LANES] * BETA
    guide_chain(lum, 1.0 / BETA, h1, h2, h3)
    channel_chain(lum, [split * (BETA * STEP)], s1, s2, s3)

    first, last = lane == 0, lane == 127
    ends = first | last
    low_ends = ends | (lane == 1)
    at = lambda base, table, other: base + sum(
        (jnp.where(lane == k, v - other, 0) for k, v in table.items()), jnp.zeros_like(lane) + other
    )
    one_same = [at(64 * g, {0: 24, 127: 40}, 24) for g in range(2)]
    one_other = [at(64 * g, {0: 23, 127: 39}, 23) for g in range(2)]
    two_same = [at(64 * g, {0: 24, 1: 25, 127: 39}, 24) for g in range(2)]
    two_other = [at(64 * g, {0: 23, 127: 40}, 23) for g in range(2)]

    def edges_one(q0, q1, t0, t1, g):
        a, b = pick(t0, one_same[g]), pick(t1, one_other[g])
        q0 = jnp.where(first, a, q0)
        q1 = jnp.where(last, b, q1)
        return jnp.where(first, b, right(q1)), q0, q1, jnp.where(last, a, left(q0))

    def edges_two(y, t, g):
        a, b = pick(t, two_same[g]), pick(t, two_other[g])
        y = jnp.where(low_ends, a, y)
        return jnp.where(first, b, right(y)), y, jnp.where(last, b, left(y))

    def fix_one(i, carry):
        for g in range(2):
            found = edges_one(d1[i, 2 * g], d1[i, 2 * g + 1], s1[i, 0], s1[i, 1], g)
            for n in range(4):
                f1[i, 4 * g + n] = found[n]
        return carry

    lax.fori_loop(46, 114, fix_one, 0)

    def fix_two(i, carry):
        for g in range(2):
            found = edges_two(d2[i, g], s2[i, 0], g)
            for n in range(3):
                f2[i, 3 * g + n] = found[n]
        return carry

    lax.fori_loop(22, 59, fix_two, 0)

    for t in range(5, 15):
        rows = slice(8 * t, 8 * t + 8)
        m, q0, q1, p = edges_one(g1[0, rows, :], g1[1, rows, :], h1[0, rows, :], h1[1, rows, :], 0)
        k1[0, rows, :], k1[1, rows, :] = q0, q1
    for t in range(2, 8):
        rows = slice(8 * t, 8 * t + 8)
        k2[rows, :] = edges_two(g2[0, rows, :], h2[0, rows, :], 0)[1]

    from_a = (lane >= 14) & (lane <= 74)
    index_a = jnp.clip(2 * (lane - 12), 0, 127)
    index_s = [jnp.clip(64 * g + jnp.where(lane < 14, 2 * lane, 2 * lane - 112), 0, 127) for g in range(2)]

    def merge(i, carry):
        for g in range(2):
            b3[i, g] = jnp.where(from_a, pick(d3[i, g], index_a), pick(s3[i, 0], index_s[g])) * (
                1.0 / (BETA * 2.0**24)
            )
        return carry

    lax.fori_loop(2, 39, merge, 0)
    for t in range(5):
        rows = slice(8 * t, 8 * t + 8)
        e3[rows, :] = jnp.where(from_a, pick(g3[rows, :], index_a), pick(h3[rows, :], index_s[0]))

    def fourth_level(i, carry):
        for g in range(2):
            b4[i, g] = columns_strided(fold(*[b3[2 * i + s - 2, g] for s in range(5)]), 1) * (1.0 / 256.0)
        return carry

    lax.fori_loop(2, 19, fourth_level, 0)

    def fifth_level(i, carry):
        for g in range(2):
            b5[i, g] = columns_strided(fold(*[b4[2 * i + s - 2, g] for s in range(5)]), 2) * (1.0 / 256.0)
        return carry

    lax.fori_loop(2, 9, fifth_level, 0)
    blur = lambda ref, i: fold(*[ref[pl.ds(2 * i + s - 2, 8, stride=2), :] for s in range(5)])
    for i in (2, 8, 11):
        e4[i : i + 8, :] = columns_strided(blur(e3, i), 1) * (1.0 / 256.0)
    e5[2:10, :] = columns_strided(blur(e4, 2), 2) * (1.0 / 256.0)

    def lanes_up(y, n):
        even = 0.125 * (right(y, n) + left(y, n)) + 0.75 * y
        odd = 0.5 * (right(y, n // 2) + left(y, n // 2))
        return even, odd

    def on_grid(y, n, parity):
        even, odd = lanes_up(y, n)
        return jnp.where(parity, odd, even)

    parity_four = (lane % 4) != 0
    parity_three = (lane % 2) != 0

    def coefficient_b(fine, coarse, guide, sums, n, parity):
        def body(i, carry):
            made = []
            for g in range(2):
                made.append(rows_up(coarse[i - 1, g], coarse[i, g], coarse[i + 1, g]))
            for odd in range(2):
                x = 2 * i + odd
                place = spread(guide, x) * 15.0
                acc = None
                for g in range(2):
                    part = hat(place, channel[g]) * (fine[x, g] - 0.5 * on_grid(made[g][odd], n, parity))
                    acc = part if acc is None else acc + part
                sums[pl.ds(x, 1), :] = total(acc)
            return carry

        return body

    lax.fori_loop(2, 8, coefficient_b(b4, b5, e4, c4, 4, parity_four), 0)
    lax.fori_loop(5, 15, coefficient_b(b3, b4, e3, c3, 2, parity_three), 0)

    def raise_rows(src, dst, start, count, index=()):
        above = src[index + (pl.ds(start - 1, count), slice(None))]
        here = src[index + (pl.ds(start, count), slice(None))]
        below = src[index + (pl.ds(start + 1, count), slice(None))]
        even, odd = rows_up(above, here, below)
        dst[index + (pl.ds(2 * start, count, stride=2), slice(None))] = 0.5 * even
        dst[index + (pl.ds(2 * start + 1, count, stride=2), slice(None))] = 0.5 * odd

    r5[...] = e5[...] * (1.0 - 0.5 * gains[4])
    raise_rows(r5, u4, 1, 8)
    for t in range(3):
        rows = slice(8 * t, 8 * t + 8)
        value = gains[4] * (0.5 * e4[rows, :] + c4[rows, :]) + on_grid(u4[rows, :], 4, parity_four)
        r4[rows, :] = value - (0.5 * gains[3]) * e4[rows, :]
    raise_rows(r4, u3, 4, 8)
    raise_rows(r4, u3, 8, 8)
    for t in range(1, 4):
        rows = slice(8 * t, 8 * t + 8)
        value = gains[3] * (0.5 * e3[rows, :] + c3[rows, :]) + on_grid(u3[rows, :], 2, parity_three)
        r3[rows, :] = value - (0.5 * gains[2]) * e3[rows, :]

    base_a = lane // 2 + 12
    column_s = jnp.where((lane // 32) % 2 == 0, lane % 32 - 24 + 256, lane % 32 + 120 + 256)
    base_s = column_s // 2 - 128 + 12
    odd_column = (lane % 2) != 0
    clip = lambda x: jnp.clip(x, 0, 127)
    three_a = [clip(base_a + d) for d in (-1, 0, 1)]
    three_s = [clip(base_s + d) for d in (-1, 0, 1)]
    upper_half = lane >= 64

    def expand(y, three):
        m, c, p = [pick(y, t) for t in three]
        return jnp.where(odd_column, 0.5 * (c + p), 0.125 * (m + p) + 0.75 * c)

    scale_two = 1.0 / (BETA * 2.0**16)

    def coefficient_two(i, carry):
        made = [rows_up(b3[i - 1, g], b3[i, g], b3[i + 1, g]) for g in range(2)]
        for odd in range(2):
            x = 2 * i + odd
            place = spread(k2, x) * 15.0
            acc = None
            for g in range(2):
                part = hat(place, channel[g]) * (
                    f2[x, 3 * g + 1] * scale_two - 0.5 * expand(made[g][odd], three_a)
                )
                acc = part if acc is None else acc + part
            c2a[pl.ds(x, 1), :] = total(acc)
            place = spread(h2, 0, x) * 15.0
            wide = jnp.where(upper_half, expand(made[1][odd], three_s), expand(made[0][odd], three_s))
            acc = hat(place, split) * (s2[x, 0] * scale_two - 0.5 * wide)
            acc = acc + right(acc, 64)
            c2s[pl.ds(x, 1), :] = total(acc)
        return carry

    lax.fori_loop(11, 29, coefficient_two, 0)
    for start in (8, 16, 24):
        raise_rows(r3, w2, start, 8)
    for t in range(2, 8):
        rows = slice(8 * t, 8 * t + 8)
        coarse = w2[rows, :]
        value = gains[2] * (0.5 * k2[rows, :] + c2a[rows, :]) + expand(coarse, three_a)
        r2a[rows, :] = value - (0.5 * gains[1]) * k2[rows, :]
        guide = h2[0, rows, :]
        value = gains[2] * (0.5 * guide + c2s[rows, :]) + expand(coarse, three_s)
        r2s[rows, :] = value - (0.5 * gains[1]) * guide

    def two_phases(m, y, p):
        return y + 0.25 * ((m + y) + (y + p)), y + p

    def coefficient_one(i, carry):
        made = [[rows_up(f2[i - 1, n], f2[i, n], f2[i + 1, n]) for n in range(3 * g, 3 * g + 3)] for g in range(2)]
        made_s = rows_up(s2[i - 1, 0], s2[i, 0], s2[i + 1, 0])
        for odd in range(2):
            x = 2 * i + odd
            places = [spread(k1, c, x) * 15.0 for c in range(2)]
            acc = [None, None]
            for g in range(2):
                ups = two_phases(*[made[g][n][odd] for n in range(3)])
                for c in range(2):
                    part = hat(places[c], channel[g]) * (f1[x, 4 * g + 1 + c] * 1024.0 - ups[c])
                    acc[c] = part if acc[c] is None else acc[c] + part
            for c in range(2):
                c1a[c, pl.ds(x, 1), :] = total(acc[c])
            ups = two_phases(right(made_s[odd]), made_s[odd], left(made_s[odd]))
            for c in range(2):
                part = hat(spread(h1, c, x) * 15.0, split) * (s1[x, c] * 1024.0 - ups[c])
                c1s[c, pl.ds(x, 1), :] = total(part + right(part, 64))
        return carry

    lax.fori_loop(23, 57, coefficient_one, 0)
    scale_one = gains[1] * (1.0 / (BETA * 2.0**18))
    for start in (20, 28, 36, 44, 52):
        raise_rows(r2a, wide_a, start, 8)
        raise_rows(r2s, wide_s, start, 8)

    def collapse_one(t, carry):
        rows = pl.ds(pl.multiple_of(8 * t, 8), 8)
        y, z = wide_a[rows, :], wide_s[rows, :]
        m, y, p = edges_two(y, z, 0)
        ups_a = two_phases(m, y, p)
        ups_s = two_phases(right(z), z, left(z))
        found = []
        for c in range(2):
            guide = k1[c, rows, :]
            found.append(
                (0.5 * (gains[1] - gains[0])) * guide + scale_one * c1a[c, rows, :] + 0.5 * ups_a[c]
            )
        side = []
        for c in range(2):
            guide = h1[c, rows, :]
            side.append((0.5 * (gains[1] - gains[0])) * guide + scale_one * c1s[c, rows, :] + 0.5 * ups_s[c])
        found = edges_one(found[0], found[1], side[0], side[1], 0)
        for n in range(4):
            rest_in[n, rows, :] = found[n]
        return carry

    rest_in = lum
    lax.fori_loop(5, 15, collapse_one, 0)

    scale_zero = gains[0] * (1.0 / (BETA * 2.0**10))

    def four_phases(m, q0, q1, p):
        t0, t1, tm = q0 + q1, q1 + p, m + q0
        return q0 + 0.25 * (tm + t0), t0, q1 + 0.25 * (t0 + t1), t1

    def coefficient_zero(i, carry):
        made = [[rows_up(f1[i - 1, n], f1[i, n], f1[i + 1, n]) for n in range(4 * g, 4 * g + 4)] for g in range(2)]
        for odd in range(2):
            x = 2 * (i - 48) + odd
            ups = [four_phases(*[made[g][n][odd] for n in range(4)]) for g in range(2)]
            for c in range(4):
                place = spread(x15, c, x)
                acc = hat(place, channel[0]) * ups[0][c] + hat(place, channel[1]) * ups[1][c]
                rest[c, pl.ds(x, 1), :] = total(acc)
        return carry

    lax.fori_loop(48, 112, coefficient_zero, 0)

    inverse = jnp.where(target == 4 * (source % LANES) + source // LANES, 1.0, 0.0).astype(jnp.bfloat16)
    for start in range(0, 64, 32):
        above = [rest_in[n, 47 + start : 79 + start, :] for n in range(4)]
        here = [rest_in[n, 48 + start : 80 + start, :] for n in range(4)]
        below = [rest_in[n, 49 + start : 81 + start, :] for n in range(4)]
        made = [rows_up(a, b, c) for a, b, c in zip(above, here, below)]
        for odd in range(2):
            ups = four_phases(*[m[odd] for m in made])
            for c in range(4):
                at_rows = pl.ds(2 * start + odd, 32, stride=2)
                rest[c, at_rows, :] = 0.25 * ups[c] - scale_zero * rest[c, at_rows, :]
    phases = jnp.concatenate([rest[c] for c in range(4)], axis=1)
    out[...] = select_columns(phases, inverse) + gains[0] * base_term[...]


def shape(*dims):
    return jax.ShapeDtypeStruct(dims, F32)


def vmem(*dims):
    return pltpu.VMEM(dims, F32)


def run_a(top, mid, bottom):
    whole = pl.BlockSpec(memory_space=pltpu.VMEM)
    return pl.pallas_call(
        kernel_a,
        out_shape=(
            shape(160, 4, HALF, LANES),
            shape(80, 2, HALF, LANES),
            shape(40, 2, HALF, LANES),
            shape(4, 128, LANES),
            shape(2, 160, LANES),
            shape(1, 80, LANES),
            shape(40, LANES),
            shape(128, 512),
        ),
        in_specs=[whole] * 3,
        out_specs=(whole,) * 8,
        scratch_shapes=[vmem(4, ROWS, LANES)],
        compiler_params=pltpu.CompilerParams(vmem_limit_bytes=40 << 20),
        cost_estimate=pl.CostEstimate(flops=60_000_000, transcendentals=2_600_000, bytes_accessed=6_000_000),
    )(top, mid, bottom)


def run_b(gain, strips, parts):
    whole = pl.BlockSpec(memory_space=pltpu.VMEM)
    return pl.pallas_call(
        kernel_b,
        out_shape=shape(128, 512),
        in_specs=[pl.BlockSpec(memory_space=pltpu.SMEM)] + [whole] * 12,
        out_specs=whole,
        scratch_shapes=[
            vmem(4, ROWS, LANES),
            vmem(160, 2, HALF, LANES),
            vmem(80, 1, HALF, LANES),
            vmem(40, 1, HALF, LANES),
            vmem(2, 160, LANES),
            vmem(1, 80, LANES),
            vmem(40, LANES),
            vmem(160, 8, HALF, LANES),
            vmem(80, 6, HALF, LANES),
            vmem(40, 2, HALF, LANES),
            vmem(24, 2, HALF, LANES),
            vmem(16, 2, HALF, LANES),
            vmem(40, LANES),
            vmem(24, LANES),
            vmem(16, LANES),
            vmem(24, LANES),
            vmem(40, LANES),
            vmem(80, LANES),
            vmem(80, LANES),
            vmem(2, 160, LANES),
            vmem(2, 160, LANES),
            vmem(16, LANES),
            vmem(24, LANES),
            vmem(24, LANES),
            vmem(40, LANES),
            vmem(40, LANES),
            vmem(80, LANES),
            vmem(80, LANES),
            vmem(80, LANES),
            vmem(160, LANES),
            vmem(160, LANES),
            vmem(2, 160, LANES),
            vmem(80, LANES),
            vmem(4, 128, LANES),
        ],
        compiler_params=pltpu.CompilerParams(vmem_limit_bytes=48 << 20),
        cost_estimate=pl.CostEstimate(flops=60_000_000, transcendentals=1_300_000, bytes_accessed=6_000_000),
    )(gain, *strips, *parts)


def ring(axis, shift):
    count = lax.axis_size(axis)
    return [(i, (i + shift) % count) for i in range(count)]


def local(luminance, level_gain):
    top = lax.ppermute(luminance[32:], "row", ring("row", 1))
    bottom = lax.ppermute(luminance[:96], "row", ring("row", -1))
    near = []
    for columns in (slice(0, LANES), slice(512 - LANES, 512)):
        near.append(jnp.concatenate([x[:, columns] for x in (top, luminance, bottom)], axis=0))
    far_left = lax.ppermute(near[1], "col", ring("col", 1))
    far_right = lax.ppermute(near[0], "col", ring("col", -1))
    parts = run_a(top, luminance, bottom)
    return run_b(level_gain, (far_left, near[0], near[1], far_right), parts)


def solution(mesh):
    return jax.shard_map(
        local, mesh=mesh, in_specs=(P("row", "col"), P()), out_specs=P("row", "col"), check_vma=False
    )
```

time: 534 us -> 92.7 us (0.17); the launches traced: 527 us -> 92.5 us
  local copies, waits for them, and re-layouts: 353 us -> 2.89 us
  starting transfers between devices: 90.8 us -> 8.97 us
  Pallas kernels: 0 us -> 76.3 us
  other arithmetic: 58.4 us -> 0.02 us
  waiting for transfers between devices: 23.6 us -> 4.2 us
    slice x58 -> x4, local copies, waits for them, and re-layouts: 324 us -> 1.94 us  [the longest x1 1.05 us: local(): top = lax.ppermute(luminance[32:], 'row', ring('row', 1))]
    ppermute x44 -> x4, starting transfers between devices: 90.8 us -> 8.97 us  [the longest x1 6.28 us: local(): far_right = lax.ppermute(near[0], 'col', ring('col', -1))]
    pallas_call x0 -> x2, Pallas kernels: none -> 76.3 us  [the longest x1 55.7 us: run_b(): pl.pallas_call(kernel_b, out_shape=shape(128, 512), in_specs=[pl.BlockSpe...]
    add x16 -> x0, other arithmetic: 22.6 us -> none  [the longest x5 8.19 us: down_valid(): result + binomial[step] * blurred[..., step:step + 2 * out_cols - 1:2]]
    ppermute x44 -> x4, waiting for transfers between devices: 23.6 us -> 4.2 us  [the longest x1 2.47 us: local(): bottom = lax.ppermute(luminance[:96], 'row', ring('row', -1))]
    another operation x38 -> x0, other arithmetic: 16.5 us -> none  [the longest x18 8.48 us: up_valid(): result = jnp.stack([even_cols, odd_cols], axis=-1)]
    another operation x17 -> x0, local copies, waits for them, and re-layouts: 13.1 us -> none  [the longest x8 12.3 us: up_valid(): result = jnp.stack([even_cols, odd_cols], axis=-1)]
    reshape x10 -> x0, local copies, waits for them, and re-layouts: 11.5 us -> none  [the longest x8 11.4 us: up_valid(): return result.reshape(result.shape[:-2] + (2 * (cols_in - 2),))]
  transfers between devices with their start and end apart: 44 -> 4, of which waited for: 16 -> 2; matrix products, arithmetic and copies ran while one was open for 9% -> 1% of each run, Pallas kernels for 0% -> 22%
where the time goes in v1:
time: 92.7 us; the launch traced here: 92.5 us
  Pallas kernels  76.3 us (82%)
  starting transfers between devices  8.97 us (10%)
  waiting for transfers between devices  4.2 us (5%)
  local copies, waits for them, and re-layouts  2.89 us (3%)
    pallas_call x1, Pallas kernels, run_b(): pl.pallas_call(kernel_b, out_shape=shape(128, 512), in_specs=[pl.BlockSpe...  55.7 us
    pallas_call x1, Pallas kernels, run_a(): pl.pallas_call(kernel_a, out_shape=(shape(160, 4, HALF, LANES), shape(80,...  20.7 us
    ppermute x1, starting transfers between devices, local(): far_right = lax.ppermute(near[0], 'col', ring('col', -1))  6.28 us
    ppermute x1, starting transfers between devices, local(): top = lax.ppermute(luminance[32:], 'row', ring('row', 1))  2.61 us
    ppermute x1, waiting for transfers between devices, local(): bottom = lax.ppermute(luminance[:96], 'row', ring('row', -1))  2.47 us
  transfers between devices with their start and end apart: 4, of which 2 were waited for; matrix products, arithmetic and copies ran while one was open for 1% of the time, Pallas kernels for 22%

profile of v1, /device:TPU:1, one launch (start us, length us, event | category | flops | bytes accessed | tf_op | source)
XLA Modules:
  0.0 92.5 jit_solution(17122923578349577832)
XLA Ops:
  0.0 1.0 %fusion.1 = (f32[96,512]{1,0:T(8,128)S(1)}, f32[96,512]{1,0:T(8,128)S(1)}) fusion(f32[128,512]{1,0:T(8,128)} %mid.1), kind=kLoop, calls=%fused_computation.3 | loop fusion | bytes 786432 | tf_op jit(solution)/shard_map/slice | solution.py:578
  1.1 2.6 %collective-permute-start = (f32[96,512]{1,0:T(8,128)S(1)}, f32[96,512]{1,0:T(8,128)S(1)}, u32[]{:S(2)}, u32[]{:S(2)}) collective-permute-start(f32[96,512]{1,0:T(8,128)S(1)} %get-tuple-element.23), channel_id=1, source_target_pairs={{0,16},{16,32},{32,48},{48,64},{64,80},{80,96},{96,112},{112,0},{1... | collective-permute-start | bytes 589832 | tf_op jit(solution)/shard_map/ppermute | solution.py:578
  3.7 0.0 collective-permute-start.1
  3.7 0.9 fusion
  4.6 1.7 %collective-permute-done.top = f32[96,512]{1,0:T(8,128)S(1)} collective-permute-done((f32[96,512]{1,0:T(8,128)S(1)}, f32[96,512]{1,0:T(8,128)S(1)}, u32[]{:S(2)}, u32[]{:S(2)}) %collective-permute-start) | collective-permute-done | bytes 196640 | tf_op jit(solution)/shard_map/ppermute | solution.py:578
  6.3 2.5 %collective-permute-done.1.bottom = f32[96,512]{1,0:T(8,128)S(1)} collective-permute-done((f32[96,512]{1,0:T(8,128)S(1)}, f32[96,512]{1,0:T(8,128)S(1)}, u32[]{:S(2)}, u32[]{:S(2)}) %collective-permute-start.1) | collective-permute-done | bytes 196640 | tf_op jit(solution)/shard_map/ppermute | solution.py:579
  8.8 6.3 %collective-permute-start.3 = (f32[320,128]{1,0:T(8,128)S(1)}, f32[320,128]{1,0:T(8,128)S(1)}, u32[]{:S(2)}, u32[]{:S(2)}) collective-permute-start(f32[320,128]{1,0:T(8,128)S(1)} %pad_maximum_fusion.1.near_left), channel_id=1, source_target_pairs={{0,15},{1,0},{2,1},{3,2},{4,3},{5,4},{6,5},{7,6},{8,7},{9,8},{10,9... | collective-permute-start | bytes 491528 | tf_op jit(solution)/shard_map/ppermute | solution.py:584
  15.1 0.0 copy-start.1
  15.1 0.1 collective-permute-start.2
  15.2 0.0 copy-start
  15.2 0.9 %copy-done = f32[128,512]{1,0:T(8,128)S(1)} copy-done((f32[128,512]{1,0:T(8,128)S(1)}, f32[128,512]{1,0:T(8,128)}, u32[]{:S(2)}) %copy-start) | copy-done | bytes 262168
  16.1 20.7 %shard_map.28 = (f32[160,4,8,128]{3,2,1,0:T(8,128)S(1)}, f32[80,2,8,128]{3,2,1,0:T(8,128)S(1)}, f32[40,2,8,128]{3,2,1,0:T(8,128)S(1)}, f32[4,128,128]{2,1,0:T(8,...) custom-call(f32[96,512]{1,0:T(8,128)S(1)} %collective-permute-done.t, ...), custom_call_target="tpu_custom_call" | custom-call | flops 60000000 | bytes 6000000 | tf_op jit(solution)/shard_map/pallas_call | solution.py:504
  36.8 0.0 collective-permute-done.3.far_right
  36.8 0.0 collective-permute-done.2.far_left
  36.8 0.0 copy-done.1
  36.8 55.7 %shard_map.29 = f32[128,512]{1,0:T(8,128)} custom-call(f32[5]{0:T(128)S(1)} %copy-done.1, f32[320,128]{1,0:T(8,128)S(1)} %collective-permute-done.2.far_left, f32[320,128]{1,0:T(8,128)S(1)} %pad_maximum_fusion.1.near_left, f32[320,128]{1,0:T(8,128)S(1)} %pad_maximum_fusion.near_right, f32[320,128]{1,0:T(8,128)S(1)} %collective-permute-done.3.far_right, ...), custom_call_target="tpu_custom_call" | custom-call | flops 60000000 | bytes 6000000 | tf_op jit(solution)/shard_map/pallas_call | solution.py:526
  (4 shorter events, 0.0 us)
Async XLA Ops:
  1.1 5.2 %collective-permute-start = (f32[96,512]{1,0:T(8,128)S(1)}, f32[96,512]{1,0:T(8,128)S(1)}, u32[]{:S(2)}, u32[]{:S(2)}) collective-permute-start(f32[96,512]{1,0:T(8,128)S(1)} %get-tuple-element.23), channel_id=1, source_target_pairs={{0,16},{16,32},{32,48},{48,64},{64,80},{80,96},{96,112},{112,0},{1... | collective-permute-start | bytes 589832 | tf_op jit(solution)/shard_map/ppermute | solution.py:578
  3.7 5.1 %collective-permute-start.1 = (f32[96,512]{1,0:T(8,128)S(1)}, f32[96,512]{1,0:T(8,128)S(1)}, u32[]{:S(2)}, u32[]{:S(2)}) collective-permute-start(f32[96,512]{1,0:T(8,128)S(1)} %get-tuple-element.24), channel_id=1, source_target_pairs={{0,112},{16,0},{32,16},{48,32},{64,48},{80,64},{96,80},{112,96},{1... | collective-permute-start | bytes 589832 | tf_op jit(solution)/shard_map/ppermute | solution.py:579
  8.8 28.0 %collective-permute-start.3 = (f32[320,128]{1,0:T(8,128)S(1)}, f32[320,128]{1,0:T(8,128)S(1)}, u32[]{:S(2)}, u32[]{:S(2)}) collective-permute-start(f32[320,128]{1,0:T(8,128)S(1)} %pad_maximum_fusion.1.near_left), channel_id=1, source_target_pairs={{0,15},{1,0},{2,1},{3,2},{4,3},{5,4},{6,5},{7,6},{8,7},{9,8},{10,9... | collective-permute-start | bytes 491528 | tf_op jit(solution)/shard_map/ppermute | solution.py:584
  15.1 21.8 %copy-start.1 = (f32[5]{0:T(128)S(1)}, f32[5]{0:T(128)}, u32[]{:S(2)}) copy-start(f32[5]{0:T(128)} %gain_ref.1) | copy-start | bytes 64
  15.1 21.7 %collective-permute-start.2 = (f32[320,128]{1,0:T(8,128)S(1)}, f32[320,128]{1,0:T(8,128)S(1)}, u32[]{:S(2)}, u32[]{:S(2)}) collective-permute-start(f32[320,128]{1,0:T(8,128)S(1)} %pad_maximum_fusion.near_right), channel_id=1, source_target_pairs={{0,1},{1,2},{2,3},{3,4},{4,5},{5,6},{6,7},{7,8},{8,9},{9,10},{10,1... | collective-permute-start | bytes 491528 | tf_op jit(solution)/shard_map/ppermute | solution.py:583
  15.2 1.0 %copy-start = (f32[128,512]{1,0:T(8,128)S(1)}, f32[128,512]{1,0:T(8,128)}, u32[]{:S(2)}) copy-start(f32[128,512]{1,0:T(8,128)} %mid.1) | copy-start | bytes 786436

commit v2 on v1

--- a/solution.py
+++ b/solution.py
@@ -69,6 +69,20 @@
 
 def columns_strided(y, n):
     return fold(right(y, 2 * n), right(y, n), y, left(y, n), left(y, 2 * n))
+
+
+def loop(low, high, size, body, state=()):
+    whole = (high - low) // size
+
+    def several(t, state):
+        for n in range(size):
+            state = body(low + size * t + n, state)
+        return state
+
+    state = lax.fori_loop(0, whole, several, state)
+    for i in range(low + size * whole, high):
+        state = body(i, state)
+    return state
 
 
 def channel_chain(lum, anchors, d1, d2, d3):
@@ -96,14 +110,10 @@
             d1[i, 2 * g + 1] = out[1]
         return new_pair, even_next, odd
 
-    def body(t, state):
-        state = step(2 * t + 1, state)
-        return step(2 * t + 2, state)
-
-    first = row(0)
-    second = row(2)
+    first = row(2)
+    second = row(4)
     pair = [[a + b for a, b in zip(x, y)] for x, y in zip(first, second)]
-    lax.fori_loop(0, 79, body, (pair, second, row(1)))
+    loop(2, 159, 16 // groups, step, (pair, second, row(3)))
 
     def second_level(i, carry):
         for g in range(groups):
@@ -111,14 +121,14 @@
             d2[i, g] = columns_from_two(y)
         return carry
 
-    lax.fori_loop(2, 79, second_level, 0)
+    loop(2, 79, 16 // groups, second_level)
 
     def third_level(i, carry):
         for g in range(groups):
             d3[i, g] = columns_strided(fold(*[d2[2 * i + s - 2, g] for s in range(5)]), 1)
         return carry
 
-    lax.fori_loop(2, 39, third_level, 0)
+    loop(2, 39, 16 // groups, third_level)
 
 
 def rows_blurred(ref, c, base, count):
@@ -127,14 +137,14 @@
 
 def guide_chain(lum, scale, g1, g2, g3):
     def first(t, carry):
-        i = 8 * t + 8
+        i = pl.multiple_of(8 * t, 8) + 8
         y = [rows_blurred(lum, c, 2 * i, 8) for c in range(4)]
         out = columns_from_four(y)
         g1[0, pl.ds(i, 8), :] = out[0] * (scale / 256.0)
         g1[1, pl.ds(i, 8), :] = out[1] * (scale / 256.0)
         return carry
 
-    lax.fori_loop(0, 18, first, 0)
+    loop(0, 18, 6, first)
     for i in (1, 151):
         y = [rows_blurred(lum, c, 2 * i, 8) for c in range(4)]
         out = columns_from_four(y)
@@ -178,15 +188,25 @@
         base_term[rows, :] = 0.5 * value + bend
         return carry
 
-    lax.fori_loop(0, 16, natural, 0)
+    loop(0, 16, 4, natural)
 
 
 def hat(place, channel):
     return jnp.maximum(0.0, 1.0 - jnp.abs(place - channel))
 
 
-def total(x):
-    return jnp.sum(x, axis=0, keepdims=True)
+def eight_totals(parts):
+    sublane = iota((HALF, LANES), 0)
+
+    def join(a, b, offset, span):
+        mine = (sublane - offset + HALF) % (2 * span) < span
+        return jnp.where(mine, a, b) + pltpu.roll(jnp.where(mine, b, a), HALF - span, axis=0)
+
+    def four(a, b, c, d, offset):
+        return join(join(a, b, offset, 4), join(c, d, offset + 2, 4), offset, 2)
+
+    x = parts
+    return join(four(x[0], x[4], x[2], x[6], 0), four(x[1], x[5], x[3], x[7], 1), 0, 1)
 
 
 def rows_up(before, here, after):
@@ -201,7 +221,7 @@
 def kernel_b(
     gain_ref, far_left, near_left, near_right, far_right, d1, d2, d3, x15, g1, g2, g3, base_term, out,
     lum, s1, s2, s3, h1, h2, h3, f1, f2, b3, b4, b5, e3, e4, e5,
-    c4, c3, c2a, c2s, c1a, c1s, r5, r4, u4, r3, u3, w2, r2a, r2s, wide_a, wide_s, k1, k2, rest,
+    c4, c3, c2a, c2s, c1a, c1s, r5, r4, u4, r3, u3, wide3, w2, r2a, r2s, wide_a, wide_s, k1, k2, rest,
 ):
     gains = [gain_ref[i] for i in range(5)]
     lane = iota((HALF, LANES), 1)
@@ -223,27 +243,23 @@
     guide_chain(lum, 1.0 / BETA, h1, h2, h3)
     channel_chain(lum, [split * (BETA * STEP)], s1, s2, s3)
 
-    first, last = lane == 0, lane == 127
-    ends = first | last
-    low_ends = ends | (lane == 1)
-    at = lambda base, table, other: base + sum(
-        (jnp.where(lane == k, v - other, 0) for k, v in table.items()), jnp.zeros_like(lane) + other
-    )
-    one_same = [at(64 * g, {0: 24, 127: 40}, 24) for g in range(2)]
-    one_other = [at(64 * g, {0: 23, 127: 39}, 23) for g in range(2)]
-    two_same = [at(64 * g, {0: 24, 1: 25, 127: 39}, 24) for g in range(2)]
-    two_other = [at(64 * g, {0: 23, 127: 40}, 23) for g in range(2)]
+    first, last, low_ends = lane == 0, lane == 127, lane <= 1
+    turn = lambda x, source, to: pltpu.roll(x, (to - source) % LANES, axis=1)
 
     def edges_one(q0, q1, t0, t1, g):
-        a, b = pick(t0, one_same[g]), pick(t1, one_other[g])
-        q0 = jnp.where(first, a, q0)
-        q1 = jnp.where(last, b, q1)
-        return jnp.where(first, b, right(q1)), q0, q1, jnp.where(last, a, left(q0))
+        base = 64 * g
+        q0 = jnp.where(first, turn(t0, base + 24, 0), q0)
+        q1 = jnp.where(last, turn(t1, base + 39, 127), q1)
+        before = jnp.where(first, turn(t1, base + 23, 0), right(q1))
+        after = jnp.where(last, turn(t0, base + 40, 127), left(q0))
+        return before, q0, q1, after
 
     def edges_two(y, t, g):
-        a, b = pick(t, two_same[g]), pick(t, two_other[g])
-        y = jnp.where(low_ends, a, y)
-        return jnp.where(first, b, right(y)), y, jnp.where(last, b, left(y))
+        base = 64 * g
+        y = jnp.where(last, turn(t, base + 39, 127), jnp.where(low_ends, turn(t, base + 24, 0), y))
+        before = jnp.where(first, turn(t, base + 23, 0), right(y))
+        after = jnp.where(last, turn(t, base + 40, 127), left(y))
+        return before, y, after
 
     def fix_one(i, carry):
         for g in range(2):
@@ -252,7 +268,7 @@
                 f1[i, 4 * g + n] = found[n]
         return carry
 
-    lax.fori_loop(46, 114, fix_one, 0)
+    loop(46, 114, 4, fix_one)
 
     def fix_two(i, carry):
         for g in range(2):
@@ -261,7 +277,7 @@
                 f2[i, 3 * g + n] = found[n]
         return carry
 
-    lax.fori_loop(22, 59, fix_two, 0)
+    loop(22, 59, 4, fix_two)
 
     for t in range(5, 15):
         rows = slice(8 * t, 8 * t + 8)
@@ -282,7 +298,7 @@
             )
         return carry
 
-    lax.fori_loop(2, 39, merge, 0)
+    loop(2, 39, 8, merge)
     for t in range(5):
         rows = slice(8 * t, 8 * t + 8)
         e3[rows, :] = jnp.where(from_a, pick(g3[rows, :], index_a), pick(h3[rows, :], index_s[0]))
@@ -292,14 +308,14 @@
             b4[i, g] = columns_strided(fold(*[b3[2 * i + s - 2, g] for s in range(5)]), 1) * (1.0 / 256.0)
         return carry
 
-    lax.fori_loop(2, 19, fourth_level, 0)
+    loop(2, 19, 17, fourth_level)
 
     def fifth_level(i, carry):
         for g in range(2):
             b5[i, g] = columns_strided(fold(*[b4[2 * i + s - 2, g] for s in range(5)]), 2) * (1.0 / 256.0)
         return carry
 
-    lax.fori_loop(2, 9, fifth_level, 0)
+    loop(2, 9, 7, fifth_level)
     blur = lambda ref, i: fold(*[ref[pl.ds(2 * i + s - 2, 8, stride=2), :] for s in range(5)])
     for i in (2, 8, 11):
         e4[i : i + 8, :] = columns_strided(blur(e3, i), 1) * (1.0 / 256.0)
@@ -317,25 +333,23 @@
     parity_four = (lane % 4) != 0
     parity_three = (lane % 2) != 0
 
-    def coefficient_b(fine, coarse, guide, sums, n, parity):
-        def body(i, carry):
-            made = []
-            for g in range(2):
-                made.append(rows_up(coarse[i - 1, g], coarse[i, g], coarse[i + 1, g]))
+    def coefficient_b(fine, coarse, guide, sums, start, n, parity):
+        parts = []
+        for i in range(start // 2, start // 2 + 4):
+            made = [rows_up(coarse[i - 1, g], coarse[i, g], coarse[i + 1, g]) for g in range(2)]
             for odd in range(2):
                 x = 2 * i + odd
                 place = spread(guide, x) * 15.0
-                acc = None
-                for g in range(2):
-                    part = hat(place, channel[g]) * (fine[x, g] - 0.5 * on_grid(made[g][odd], n, parity))
-                    acc = part if acc is None else acc + part
-                sums[pl.ds(x, 1), :] = total(acc)
-            return carry
-
-        return body
-
-    lax.fori_loop(2, 8, coefficient_b(b4, b5, e4, c4, 4, parity_four), 0)
-    lax.fori_loop(5, 15, coefficient_b(b3, b4, e3, c3, 2, parity_three), 0)
+                terms = [
+                    hat(place, channel[g]) * (fine[x, g] - 0.5 * on_grid(made[g][odd], n, parity)) for g in range(2)
+                ]
+                parts.append(terms[0] + terms[1])
+        sums[start : start + 8, :] = eight_totals(parts)
+
+    for start in (4, 12):
+        coefficient_b(b4, b5, e4, c4, start, 4, parity_four)
+    for start in (10, 18, 26):
+        coefficient_b(b3, b4, e3, c3, start, 2, parity_three)
 
     def raise_rows(src, dst, start, count, index=()):
         above = src[index + (pl.ds(start - 1, count), slice(None))]
@@ -363,71 +377,84 @@
     base_s = column_s // 2 - 128 + 12
     odd_column = (lane % 2) != 0
     clip = lambda x: jnp.clip(x, 0, 127)
-    three_a = [clip(base_a + d) for d in (-1, 0, 1)]
-    three_s = [clip(base_s + d) for d in (-1, 0, 1)]
+    base_a, base_s = clip(base_a), clip(base_s)
     upper_half = lane >= 64
 
-    def expand(y, three):
-        m, c, p = [pick(y, t) for t in three]
-        return jnp.where(odd_column, 0.5 * (c + p), 0.125 * (m + p) + 0.75 * c)
-
-    scale_two = 1.0 / (BETA * 2.0**16)
-
-    def coefficient_two(i, carry):
-        made = [rows_up(b3[i - 1, g], b3[i, g], b3[i + 1, g]) for g in range(2)]
-        for odd in range(2):
-            x = 2 * i + odd
-            place = spread(k2, x) * 15.0
-            acc = None
-            for g in range(2):
-                part = hat(place, channel[g]) * (
-                    f2[x, 3 * g + 1] * scale_two - 0.5 * expand(made[g][odd], three_a)
-                )
-                acc = part if acc is None else acc + part
-            c2a[pl.ds(x, 1), :] = total(acc)
-            place = spread(h2, 0, x) * 15.0
-            wide = jnp.where(upper_half, expand(made[1][odd], three_s), expand(made[0][odd], three_s))
-            acc = hat(place, split) * (s2[x, 0] * scale_two - 0.5 * wide)
-            acc = acc + right(acc, 64)
-            c2s[pl.ds(x, 1), :] = total(acc)
-        return carry
-
-    lax.fori_loop(11, 29, coefficient_two, 0)
+    def expand(y, at):
+        even, odd = 0.125 * (right(y) + left(y)) + 0.75 * y, 0.5 * (y + left(y))
+        return jnp.where(odd_column, pick(odd, at), pick(even, at))
+
+    scale_two = 2.0 / (BETA * 2.0**16)
+
+    def widen(i, carry):
+        for g in range(2):
+            wide3[i, g] = expand(b3[i, g], base_a)
+        wide3[i, 2] = jnp.where(upper_half, expand(b3[i, 1], base_s), expand(b3[i, 0], base_s))
+        return carry
+
+    loop(10, 32, 11, widen)
+
+    def coefficient_two(t, carry):
+        parts, side = [], []
+        for n in range(4):
+            i = 4 * t + 11 + n
+            made = [rows_up(wide3[i - 1, g], wide3[i, g], wide3[i + 1, g]) for g in range(3)]
+            for odd in range(2):
+                x = 2 * i + odd
+                place = spread(k2, x) * 15.0
+                terms = [
+                    hat(place, channel[g]) * (f2[x, 3 * g + 1] * scale_two - made[g][odd]) for g in range(2)
+                ]
+                parts.append(terms[0] + terms[1])
+                place = spread(h2, 0, x) * 15.0
+                side.append(hat(place, split) * (s2[x, 0] * scale_two - made[2][odd]))
+        rows = pl.ds(8 * t + 22, 8)
+        c2a[rows, :] = 0.5 * eight_totals(parts)
+        both = eight_totals(side)
+        c2s[rows, :] = 0.5 * (both + right(both, 64))
+        return carry
+
+    lax.fori_loop(0, 5, coefficient_two, 0)
     for start in (8, 16, 24):
         raise_rows(r3, w2, start, 8)
     for t in range(2, 8):
         rows = slice(8 * t, 8 * t + 8)
         coarse = w2[rows, :]
-        value = gains[2] * (0.5 * k2[rows, :] + c2a[rows, :]) + expand(coarse, three_a)
+        value = gains[2] * (0.5 * k2[rows, :] + c2a[rows, :]) + expand(coarse, base_a)
         r2a[rows, :] = value - (0.5 * gains[1]) * k2[rows, :]
         guide = h2[0, rows, :]
-        value = gains[2] * (0.5 * guide + c2s[rows, :]) + expand(coarse, three_s)
+        value = gains[2] * (0.5 * guide + c2s[rows, :]) + expand(coarse, base_s)
         r2s[rows, :] = value - (0.5 * gains[1]) * guide
 
     def two_phases(m, y, p):
         return y + 0.25 * ((m + y) + (y + p)), y + p
 
-    def coefficient_one(i, carry):
-        made = [[rows_up(f2[i - 1, n], f2[i, n], f2[i + 1, n]) for n in range(3 * g, 3 * g + 3)] for g in range(2)]
-        made_s = rows_up(s2[i - 1, 0], s2[i, 0], s2[i + 1, 0])
-        for odd in range(2):
-            x = 2 * i + odd
-            places = [spread(k1, c, x) * 15.0 for c in range(2)]
-            acc = [None, None]
-            for g in range(2):
-                ups = two_phases(*[made[g][n][odd] for n in range(3)])
+    def coefficient_one(t, carry):
+        parts, side = [[], []], [[], []]
+        for n in range(4):
+            i = 4 * t + 23 + n
+            made = [
+                [rows_up(f2[i - 1, m], f2[i, m], f2[i + 1, m]) for m in range(3 * g, 3 * g + 3)] for g in range(2)
+            ]
+            made_s = rows_up(s2[i - 1, 0], s2[i, 0], s2[i + 1, 0])
+            for odd in range(2):
+                x = 2 * i + odd
+                ups = [two_phases(*[made[g][m][odd] for m in range(3)]) for g in range(2)]
+                ups_s = two_phases(right(made_s[odd]), made_s[odd], left(made_s[odd]))
                 for c in range(2):
-                    part = hat(places[c], channel[g]) * (f1[x, 4 * g + 1 + c] * 1024.0 - ups[c])
-                    acc[c] = part if acc[c] is None else acc[c] + part
-            for c in range(2):
-                c1a[c, pl.ds(x, 1), :] = total(acc[c])
-            ups = two_phases(right(made_s[odd]), made_s[odd], left(made_s[odd]))
-            for c in range(2):
-                part = hat(spread(h1, c, x) * 15.0, split) * (s1[x, c] * 1024.0 - ups[c])
-                c1s[c, pl.ds(x, 1), :] = total(part + right(part, 64))
-        return carry
-
-    lax.fori_loop(23, 57, coefficient_one, 0)
+                    place = spread(k1, c, x) * 15.0
+                    terms = [hat(place, channel[g]) * (f1[x, 4 * g + 1 + c] * 1024.0 - ups[g][c]) for g in range(2)]
+                    parts[c].append(terms[0] + terms[1])
+                    place = spread(h1, c, x) * 15.0
+                    side[c].append(hat(place, split) * (s1[x, c] * 1024.0 - ups_s[c]))
+        rows = pl.ds(8 * t + 46, 8)
+        for c in range(2):
+            c1a[c, rows, :] = eight_totals(parts[c])
+            both = eight_totals(side[c])
+            c1s[c, rows, :] = both + right(both, 64)
+        return carry
+
+    lax.fori_loop(0, 9, coefficient_one, 0)
     scale_one = gains[1] * (1.0 / (BETA * 2.0**18))
     for start in (20, 28, 36, 44, 52):
         raise_rows(r2a, wide_a, start, 8)
@@ -455,7 +482,7 @@
         return carry
 
     rest_in = lum
-    lax.fori_loop(5, 15, collapse_one, 0)
+    loop(5, 15, 5, collapse_one)
 
     scale_zero = gains[0] * (1.0 / (BETA * 2.0**10))
 
@@ -463,18 +490,23 @@
         t0, t1, tm = q0 + q1, q1 + p, m + q0
         return q0 + 0.25 * (tm + t0), t0, q1 + 0.25 * (t0 + t1), t1
 
-    def coefficient_zero(i, carry):
-        made = [[rows_up(f1[i - 1, n], f1[i, n], f1[i + 1, n]) for n in range(4 * g, 4 * g + 4)] for g in range(2)]
-        for odd in range(2):
-            x = 2 * (i - 48) + odd
-            ups = [four_phases(*[made[g][n][odd] for n in range(4)]) for g in range(2)]
-            for c in range(4):
-                place = spread(x15, c, x)
-                acc = hat(place, channel[0]) * ups[0][c] + hat(place, channel[1]) * ups[1][c]
-                rest[c, pl.ds(x, 1), :] = total(acc)
-        return carry
-
-    lax.fori_loop(48, 112, coefficient_zero, 0)
+    def coefficient_zero(t, carry):
+        parts = [[] for c in range(4)]
+        for n in range(4):
+            i = 4 * t + 48 + n
+            made = [
+                [rows_up(f1[i - 1, m], f1[i, m], f1[i + 1, m]) for m in range(4 * g, 4 * g + 4)] for g in range(2)
+            ]
+            for odd in range(2):
+                ups = [four_phases(*[made[g][m][odd] for m in range(4)]) for g in range(2)]
+                for c in range(4):
+                    place = spread(x15, c, 8 * t + 2 * n + odd)
+                    parts[c].append(hat(place, channel[0]) * ups[0][c] + hat(place, channel[1]) * ups[1][c])
+        for c in range(4):
+            rest[c, pl.ds(pl.multiple_of(8 * t, 8), 8), :] = eight_totals(parts[c])
+        return carry
+
+    lax.fori_loop(0, 16, coefficient_zero, 0)
 
     inverse = jnp.where(target == 4 * (source % LANES) + source // LANES, 1.0, 0.0).astype(jnp.bfloat16)
     for start in range(0, 64, 32):
@@ -555,6 +587,7 @@
             vmem(24, LANES),
             vmem(40, LANES),
             vmem(40, LANES),
+            vmem(40, 3, HALF, LANES),
             vmem(80, LANES),
             vmem(80, LANES),
             vmem(80, LANES),

time: 92.7 us -> 42.9 us (0.46)
  Pallas kernels: 76.3 us -> 26.2 us
    pallas_call x1, Pallas kernels: 55.7 us -> 18.9 us  [run_b(): pl.pallas_call(kernel_b, out_shape=shape(128, 512), in_specs=[pl.BlockSpe...]
    pallas_call x1, Pallas kernels: 20.7 us -> 7.3 us  [run_a(): pl.pallas_call(kernel_a, out_shape=(shape(160, 4, HALF, LANES), shape(80,...]
  transfers between devices with their start and end apart: 4 -> 4, of which waited for: 2 -> 3; matrix products, arithmetic and copies ran while one was open for 1% -> 2% of each run, Pallas kernels for 22% -> 17%
where the time goes in v2:
time: 42.9 us; the launch traced here: 42.7 us
  Pallas kernels  26.2 us (61%)
  starting transfers between devices  8.97 us (21%)
  waiting for transfers between devices  4.57 us (11%)
  local copies, waits for them, and re-layouts  2.89 us (7%)
    pallas_call x1, Pallas kernels, run_b(): pl.pallas_call(kernel_b, out_shape=shape(128, 512), in_specs=[pl.BlockSpe...  18.9 us
    pallas_call x1, Pallas kernels, run_a(): pl.pallas_call(kernel_a, out_shape=(shape(160, 4, HALF, LANES), shape(80,...  7.3 us
    ppermute x1, starting transfers between devices, local(): far_right = lax.ppermute(near[0], 'col', ring('col', -1))  6.28 us
    ppermute x1, starting transfers between devices, local(): top = lax.ppermute(luminance[32:], 'row', ring('row', 1))  2.61 us
    ppermute x1, waiting for transfers between devices, local(): bottom = lax.ppermute(luminance[:96], 'row', ring('row', -1))  2.47 us
    ppermute x1, waiting for transfers between devices, local(): top = lax.ppermute(luminance[32:], 'row', ring('row', 1))  1.73 us
    slice x1, local copies, waits for them, and re-layouts, local(): top = lax.ppermute(luminance[32:], 'row', ring('row', 1))  1.05 us
    unnamed x4, local copies, waits for them, and re-layouts  0.95 us
  transfers between devices with their start and end apart: 4, of which 3 were waited for; matrix products, arithmetic and copies ran while one was open for 2% of the time, Pallas kernels for 17%

profile of v2, /device:TPU:1, one launch (start us, length us, event | category | flops | bytes accessed | tf_op | source)
XLA Modules:
  0.0 42.7 jit_solution(13841768410190290140)
XLA Ops:
  0.0 1.0 %fusion.1 = (f32[96,512]{1,0:T(8,128)S(1)}, f32[96,512]{1,0:T(8,128)S(1)}) fusion(f32[128,512]{1,0:T(8,128)} %mid.1), kind=kLoop, calls=%fused_computation.3 | loop fusion | bytes 786432 | tf_op jit(solution)/shard_map/slice | solution.py:611
  1.1 2.6 %collective-permute-start = (f32[96,512]{1,0:T(8,128)S(1)}, f32[96,512]{1,0:T(8,128)S(1)}, u32[]{:S(2)}, u32[]{:S(2)}) collective-permute-start(f32[96,512]{1,0:T(8,128)S(1)} %get-tuple-element.23), channel_id=1, source_target_pairs={{0,16},{16,32},{32,48},{48,64},{64,80},{80,96},{96,112},{112,0},{1... | collective-permute-start | bytes 589832 | tf_op jit(solution)/shard_map/ppermute | solution.py:611
  3.7 0.0 collective-permute-start.1
  3.7 0.9 %fusion = (f32[128,128]{1,0:T(8,128)S(1)}, f32[128,128]{1,0:T(8,128)S(1)}) fusion(f32[128,512]{1,0:T(8,128)} %mid.1), kind=kLoop, calls=%fused_computation.2 | loop fusion | bytes 262144 | tf_op jit(solution)/shard_map/slice | solution.py:615
  4.6 1.7 %collective-permute-done.top = f32[96,512]{1,0:T(8,128)S(1)} collective-permute-done((f32[96,512]{1,0:T(8,128)S(1)}, f32[96,512]{1,0:T(8,128)S(1)}, u32[]{:S(2)}, u32[]{:S(2)}) %collective-permute-start) | collective-permute-done | bytes 196640 | tf_op jit(solution)/shard_map/ppermute | solution.py:611
  6.3 2.5 %collective-permute-done.1.bottom = f32[96,512]{1,0:T(8,128)S(1)} collective-permute-done((f32[96,512]{1,0:T(8,128)S(1)}, f32[96,512]{1,0:T(8,128)S(1)}, u32[]{:S(2)}, u32[]{:S(2)}) %collective-permute-start.1) | collective-permute-done | bytes 196640 | tf_op jit(solution)/shard_map/ppermute | solution.py:612
  8.8 6.3 %collective-permute-start.3 = (f32[320,128]{1,0:T(8,128)S(1)}, f32[320,128]{1,0:T(8,128)S(1)}, u32[]{:S(2)}, u32[]{:S(2)}) collective-permute-start(f32[320,128]{1,0:T(8,128)S(1)} %pad_maximum_fusion.1.near_left), channel_id=1, source_target_pairs={{0,15},{1,0},{2,1},{3,2},{4,3},{5,4},{6,5},{7,6},{8,7},{9,8},{10,9... | collective-permute-start | bytes 491528 | tf_op jit(solution)/shard_map/ppermute | solution.py:617
  15.1 0.0 copy-start.1
  15.1 0.1 collective-permute-start.2
  15.2 0.0 copy-start
  15.2 0.9 %copy-done = f32[128,512]{1,0:T(8,128)S(1)} copy-done((f32[128,512]{1,0:T(8,128)S(1)}, f32[128,512]{1,0:T(8,128)}, u32[]{:S(2)}) %copy-start) | copy-done | bytes 262168
  16.1 7.3 %shard_map.28 = (f32[160,4,8,128]{3,2,1,0:T(8,128)S(1)}, f32[80,2,8,128]{3,2,1,0:T(8,128)S(1)}, f32[40,2,8,128]{3,2,1,0:T(8,128)S(1)}, f32[4,128,128]{2,1,0:T(8,...) custom-call(f32[96,512]{1,0:T(8,128)S(1)} %collective-permute-done.t, ...), custom_call_target="tpu_custom_call" | custom-call | flops 60000000 | bytes 6000000 | tf_op jit(solution)/shard_map/pallas_call | solution.py:536
  23.4 0.0 collective-permute-done.3.far_right
  23.4 0.4 collective-permute-done.2.far_left
  23.8 0.0 copy-done.1
  23.8 18.9 %shard_map.29 = f32[128,512]{1,0:T(8,128)} custom-call(f32[5]{0:T(128)S(1)} %copy-done.1, f32[320,128]{1,0:T(8,128)S(1)} %collective-permute-done.2.far_left, f32[320,128]{1,0:T(8,128)S(1)} %pad_maximum_fusion.1.near_left, f32[320,128]{1,0:T(8,128)S(1)} %pad_maximum_fusion.near_right, f32[320,128]{1,0:T(8,128)S(1)} %collective-permute-done.3.far_right, ...), custom_call_target="tpu_custom_call" | custom-call | flops 60000000 | bytes 6000000 | tf_op jit(solution)/shard_map/pallas_call | solution.py:558
  (4 shorter events, 0.0 us)
Async XLA Ops:
  1.1 5.2 %collective-permute-start = (f32[96,512]{1,0:T(8,128)S(1)}, f32[96,512]{1,0:T(8,128)S(1)}, u32[]{:S(2)}, u32[]{:S(2)}) collective-permute-start(f32[96,512]{1,0:T(8,128)S(1)} %get-tuple-element.23), channel_id=1, source_target_pairs={{0,16},{16,32},{32,48},{48,64},{64,80},{80,96},{96,112},{112,0},{1... | collective-permute-start | bytes 589832 | tf_op jit(solution)/shard_map/ppermute | solution.py:611
  3.7 5.1 %collective-permute-start.1 = (f32[96,512]{1,0:T(8,128)S(1)}, f32[96,512]{1,0:T(8,128)S(1)}, u32[]{:S(2)}, u32[]{:S(2)}) collective-permute-start(f32[96,512]{1,0:T(8,128)S(1)} %get-tuple-element.24), channel_id=1, source_target_pairs={{0,112},{16,0},{32,16},{48,32},{64,48},{80,64},{96,80},{112,96},{1... | collective-permute-start | bytes 589832 | tf_op jit(solution)/shard_map/ppermute | solution.py:612
  8.8 14.6 %collective-permute-start.3 = (f32[320,128]{1,0:T(8,128)S(1)}, f32[320,128]{1,0:T(8,128)S(1)}, u32[]{:S(2)}, u32[]{:S(2)}) collective-permute-start(f32[320,128]{1,0:T(8,128)S(1)} %pad_maximum_fusion.1.near_left), channel_id=1, source_target_pairs={{0,15},{1,0},{2,1},{3,2},{4,3},{5,4},{6,5},{7,6},{8,7},{9,8},{10,9... | collective-permute-start | bytes 491528 | tf_op jit(solution)/shard_map/ppermute | solution.py:617
  15.1 8.7 %copy-start.1 = (f32[5]{0:T(128)S(1)}, f32[5]{0:T(128)}, u32[]{:S(2)}) copy-start(f32[5]{0:T(128)} %gain_ref.1) | copy-start | bytes 64
  15.1 8.7 %collective-permute-start.2 = (f32[320,128]{1,0:T(8,128)S(1)}, f32[320,128]{1,0:T(8,128)S(1)}, u32[]{:S(2)}, u32[]{:S(2)}) collective-permute-start(f32[320,128]{1,0:T(8,128)S(1)} %pad_maximum_fusion.near_right), channel_id=1, source_target_pairs={{0,1},{1,2},{2,3},{3,4},{4,5},{5,6},{6,7},{7,8},{8,9},{9,10},{10,1... | collective-permute-start | bytes 491528 | tf_op jit(solution)/shard_map/ppermute | solution.py:616
  15.2 1.0 %copy-start = (f32[128,512]{1,0:T(8,128)S(1)}, f32[128,512]{1,0:T(8,128)}, u32[]{:S(2)}) copy-start(f32[128,512]{1,0:T(8,128)} %mid.1) | copy-start | bytes 786436

commit v3 on v2

v3 whole, which is shorter than its diff:
```python
import math

import jax
import jax.numpy as jnp
from jax import lax
from jax.experimental import pallas as pl
from jax.experimental.pallas import tpu as pltpu
from jax.sharding import PartitionSpec as P


ROWS = 320
LANES = 128
HALF = 8
STEP = 1.0 / 15.0
BETA = math.sqrt(800.0 * math.log2(math.e))
F32 = jnp.float32
UNROLL = {1: 53, 2: 26}
UNROLL_TWO = {1: 39, 2: 26}
UNROLL_SUMS = 4


def iota(shape, dim):
    return lax.broadcasted_iota(jnp.int32, shape, dim)


def left(x, n=1):
    return pltpu.roll(x, LANES - n, axis=x.ndim - 1)


def right(x, n=1):
    return pltpu.roll(x, n, axis=x.ndim - 1)


def pick(x, idx):
    return jnp.take_along_axis(x, idx, axis=1)


def select_columns(x, table):
    hi = x.astype(jnp.bfloat16)
    rest = x - hi.astype(F32)
    mid = rest.astype(jnp.bfloat16)
    low = (rest - mid.astype(F32)).astype(jnp.bfloat16)
    count = x.shape[0]
    out = jnp.dot(jnp.concatenate([hi, mid, low], axis=0), table, preferred_element_type=F32)
    return out[:count] + out[count : 2 * count] + out[2 * count :]


def spread(ref, *index):
    return ref[index[:-1] + (pl.ds(index[-1], HALF, stride=0), slice(None))]


def fold(y0, y1, y2, y3, y4):
    return (y0 + y4) + 6.0 * y2 + 4.0 * (y1 + y3)


def bump(lum, anchor, power):
    u = lum - anchor
    return u * jnp.exp2(power - u * u)


def columns_from_four(y):
    y0, y1, y2, y3 = y
    return (
        (right(y2) + y2) + 6.0 * y0 + (right(y3) + y1),
        (y0 + left(y0)) + 6.0 * y2 + (y1 + y3),
    )


def columns_from_two(y):
    y0, y1 = y
    return fold(right(y0), right(y1), y0, y1, left(y0))


def columns_strided(y, n):
    return fold(right(y, 2 * n), right(y, n), y, left(y, n), left(y, 2 * n))


def loop(low, high, size, body, state=()):
    whole = (high - low) // size

    def several(t, state):
        for n in range(size):
            state = body(low + size * t + n, state)
        return state

    state = lax.fori_loop(0, whole, several, state)
    for i in range(low + size * whole, high):
        state = body(i, state)
    return state


def channel_chain(lum, anchors, d1, d2, d3):
    groups = len(anchors)

    def row(e, odd):
        values = [spread(lum, c, e) for c in range(4)]
        return [[bump(v, a, 2.0 * odd + 2.0 * (c % 2)) for c, v in enumerate(values)] for a in anchors]

    def step(i, state):
        even_before, even, odd_before = state
        odd = row(2 * i + 1, 1)
        even_next = row(2 * i + 2, 0)
        for g in range(groups):
            y = [
                (even_before[g][c] + even_next[g][c]) + 6.0 * even[g][c] + (odd_before[g][c] + odd[g][c])
                for c in range(4)
            ]
            out = columns_from_four(y)
            d1[i, 2 * g] = out[0]
            d1[i, 2 * g + 1] = out[1]
        return even, even_next, odd

    loop(2, 159, UNROLL[groups], step, (row(2, 0), row(4, 0), row(3, 1)))

    def second_level(i, carry):
        for g in range(groups):
            y = [fold(*[d1[2 * i + s - 2, 2 * g + c] for s in range(5)]) for c in range(2)]
            d2[i, g] = columns_from_two(y)
        return carry

    loop(2, 79, UNROLL_TWO[groups], second_level)

    def third_level(i, carry):
        for g in range(groups):
            d3[i, g] = columns_strided(fold(*[d2[2 * i + s - 2, g] for s in range(5)]), 1)
        return carry

    loop(2, 39, UNROLL_TWO[groups], third_level)


def rows_blurred(ref, c, base, count):
    return fold(*[ref[c, pl.ds(base + s - 2, count, stride=2), :] for s in range(5)])


def guide_chain(lum, scale, g1, g2, g3):
    def first(t, carry):
        i = pl.multiple_of(8 * t, 8) + 8
        y = [rows_blurred(lum, c, 2 * i, 8) * (1.0 + 3.0 * (c % 2)) for c in range(4)]
        out = columns_from_four(y)
        g1[0, pl.ds(i, 8), :] = out[0] * (scale / 256.0)
        g1[1, pl.ds(i, 8), :] = out[1] * (scale / 256.0)
        return carry

    loop(0, 18, 6, first)
    for i in (1, 151):
        y = [rows_blurred(lum, c, 2 * i, 8) * (1.0 + 3.0 * (c % 2)) for c in range(4)]
        out = columns_from_four(y)
        g1[0, i : i + 8, :] = out[0] * (scale / 256.0)
        g1[1, i : i + 8, :] = out[1] * (scale / 256.0)
    for i in (2, 8, 16, 24, 32, 40, 48, 56, 64, 71):
        y = [rows_blurred(g1, c, 2 * i, 8) for c in range(2)]
        g2[0, i : i + 8, :] = columns_from_two(y) * (1.0 / 256.0)
    for i in (2, 8, 16, 24, 31):
        g3[i : i + 8, :] = columns_strided(rows_blurred(g2, 0, 2 * i, 8), 1) * (1.0 / 256.0)


def anchor_tile(base):
    return (iota((HALF, LANES), 0) + base).astype(F32)


def kernel_a(top, mid, bottom, d1, d2, d3, x15, g1, g2, g3, base_term, lum):
    source = iota((256, 256), 0)
    target = iota((256, 256), 1)
    table = jnp.where(source == 4 * (target % 64) + target // 64, 1.0, 0.0).astype(jnp.bfloat16)
    for ref, skip, start, count in ((top, 32, 0, 96), (mid, 0, 96, 128), (bottom, 0, 224, 96)):
        both = jnp.concatenate([ref[skip : skip + count, :256], ref[skip : skip + count, 256:]], axis=0)
        split = select_columns(both, table)
        low_half = iota((count, LANES), 1) < 64
        for pair in range(2):
            a = split[:count, pair * LANES : (pair + 1) * LANES]
            b = split[count:, pair * LANES : (pair + 1) * LANES]
            for c, part in (
                (2 * pair, jnp.where(low_half, a, right(b, 64))),
                (2 * pair + 1, jnp.where(low_half, right(a, 64), b)),
            ):
                lum[c, start : start + count, :] = part * BETA
                if start == 96:
                    x15[c] = part * 15.0
    guide_chain(lum, 1.0 / BETA, g1, g2, g3)
    anchors = [anchor_tile(HALF * g) * (BETA * STEP) for g in range(2)]
    channel_chain(lum, anchors, d1, d2, d3)

    def natural(t, carry):
        rows = pl.ds(pl.multiple_of(8 * t, 8), 8)
        value = mid[rows, :]
        place = value * 15.0
        lower = jnp.floor(place)
        part = place - lower
        near = value - lower * STEP
        far = value - (lower + 1.0) * STEP
        bend = (1.0 - part) * near * jnp.exp(near * near * -800.0) + part * far * jnp.exp(far * far * -800.0)
        base_term[rows, :] = 0.5 * value + bend
        return carry

    loop(0, 16, 4, natural)


def hat(place, channel):
    return jnp.maximum(0.0, 1.0 - jnp.abs(place - channel))


def eight_totals(parts):
    sublane = iota((HALF, LANES), 0)

    def join(a, b, offset, span):
        mine = (sublane - offset + HALF) % (2 * span) < span
        return jnp.where(mine, a, b) + pltpu.roll(jnp.where(mine, b, a), HALF - span, axis=0)

    def four(a, b, c, d, offset):
        return join(join(a, b, offset, 4), join(c, d, offset + 2, 4), offset, 2)

    x = parts
    return join(four(x[0], x[4], x[2], x[6], 0), four(x[1], x[5], x[3], x[7], 1), 0, 1)


def rows_up(before, here, after):
    later = here + after
    return here + 0.25 * ((before + here) + later), later


def raised(rows):
    sums = [a + b for a, b in zip(rows, rows[1:])]
    out = []
    for n in range(1, len(rows) - 1):
        out += [rows[n] + 0.25 * (sums[n - 1] + sums[n]), sums[n]]
    return out


def two_phases(m, y, p):
    return y + 0.25 * ((m + y) + (y + p)), y + p


def four_phases(m, q0, q1, p):
    t0, t1, tm = q0 + q1, q1 + p, m + q0
    return q0 + 0.25 * (tm + t0), t0, q1 + 0.25 * (t0 + t1), t1


def kernel_c(d1, d2, x15, g1, sums, c1a):
    channel = [anchor_tile(HALF * g) for g in range(2)]

    def level_one(t, carry):
        parts = [[None] * 8 for c in range(2)]
        for g in range(2):
            rows = [d2[4 * t + 22 + n, g] for n in range(6)]
            fine = [raised(y) for y in ([right(y) for y in rows], rows, [left(y) for y in rows])]
            for n in range(8):
                ups = two_phases(*[f[n] for f in fine])
                for c in range(2):
                    x = 8 * t + 46 + n
                    part = hat(spread(g1, c, x) * 15.0, channel[g]) * (d1[x, 2 * g + c] * 1024.0 - ups[c])
                    parts[c][n] = part if g == 0 else parts[c][n] + part
        for c in range(2):
            c1a[c, pl.ds(8 * t + 46, 8), :] = eight_totals(parts[c])
        return carry

    loop(0, 9, UNROLL_SUMS, level_one)

    def level_zero(t, carry):
        parts = [[None] * 8 for c in range(4)]
        for g in range(2):
            rows = [[d1[4 * t + 47 + n, 2 * g + c] for n in range(6)] for c in range(2)]
            fine = [raised(y) for y in ([right(y) for y in rows[1]], rows[0], rows[1], [left(y) for y in rows[0]])]
            for n in range(8):
                ups = four_phases(*[f[n] for f in fine])
                for c in range(4):
                    part = hat(spread(x15, c, 8 * t + n), channel[g]) * ups[c]
                    parts[c][n] = part if g == 0 else parts[c][n] + part
        for c in range(4):
            sums[c, pl.ds(pl.multiple_of(8 * t, 8), 8), :] = eight_totals(parts[c])
        return carry

    loop(0, 16, UNROLL_SUMS, level_zero)


def kernel_b(
    gain_ref, top, mid, bottom, far_left, far_right, far_top, far_bottom,
    d2, d3, g1, g2, g3, base_term, sums, c1a, out,
    lum, s1, s2, s3, h1, h2, h3, b3, b4, b5, e3, e4, e5,
    c4, c3, c2a, c2s, c1s, sums_s, r5, r4, u4, r3, u3, wide3, w2, r2a, r2s, wide_a, wide_s, rest,
):
    gains = [gain_ref[i] for i in range(5)]
    lane = iota((HALF, LANES), 1)
    channel = [anchor_tile(HALF * g) for g in range(2)]
    split = anchor_tile(0) + jnp.where(lane >= 64, 8.0, 0.0)

    source = iota((512, 256), 0)
    target = iota((512, 256), 1)
    wanted = 32 + 320 * ((target // 32) % 2) + 4 * (target % 32) + target // 64
    table = jnp.where(source == wanted, 1.0, 0.0).astype(jnp.bfloat16)
    for natural, start, count in (
        ([far_top[:, :LANES], top[32:, :LANES], top[32:, 384:], far_top[:, LANES:]], 0, 96),
        ([far_left[...], mid[:, :LANES], mid[:, 384:], far_right[...]], 96, 128),
        ([far_bottom[:, :LANES], bottom[:96, :LANES], bottom[:96, 384:], far_bottom[:, LANES:]], 224, 96),
    ):
        pieces = select_columns(jnp.concatenate(natural, axis=1), table)
        low_half = iota((count, LANES), 1) < 64
        for pair in range(2):
            a = pieces[:, pair * LANES : (pair + 1) * LANES] * BETA
            b = right(a, 64)
            lum[2 * pair, start : start + count, :] = jnp.where(low_half, a, b)
            lum[2 * pair + 1, start : start + count, :] = jnp.where(low_half, b, a)
    guide_chain(lum, 1.0 / BETA, h1, h2, h3)
    channel_chain(lum, [split * (BETA * STEP)], s1, s2, s3)

    first, last = lane == 0, lane == 127
    turn = lambda x, source, to: pltpu.roll(x, (to - source) % LANES, axis=1)

    def ends(x, t, low, high):
        return jnp.where(lane >= high, turn(t, 39, 127), jnp.where(lane <= low, turn(t, 24, 0), x))

    def edges_one(q0, q1, t0, t1):
        q0, q1 = ends(q0, t0, 2, 126), ends(q1, t1, 2, 126)
        return jnp.where(first, turn(t1, 23, 0), right(q1)), q0, q1, jnp.where(last, turn(t0, 40, 127), left(q0))

    def edges_two(y, t):
        y = ends(y, t, 1, 127)
        return jnp.where(first, turn(t, 23, 0), right(y)), y, jnp.where(last, turn(t, 40, 127), left(y))

    from_a = (lane >= 14) & (lane <= 74)
    index_a = jnp.clip(2 * (lane - 12), 0, 127)
    index_s = [jnp.clip(64 * g + jnp.where(lane < 14, 2 * lane, 2 * lane - 112), 0, 127) for g in range(2)]

    def merge(i, carry):
        for g in range(2):
            b3[i, g] = jnp.where(from_a, pick(d3[i, g], index_a), pick(s3[i, 0], index_s[g])) * (
                1.0 / (BETA * 2.0**24)
            )
        return carry

    loop(2, 39, 8, merge)
    for t in range(5):
        rows = slice(8 * t, 8 * t + 8)
        e3[rows, :] = jnp.where(from_a, pick(g3[rows, :], index_a), pick(h3[rows, :], index_s[0]))

    def fourth_level(i, carry):
        for g in range(2):
            b4[i, g] = columns_strided(fold(*[b3[2 * i + s - 2, g] for s in range(5)]), 1) * (1.0 / 256.0)
        return carry

    loop(2, 19, 17, fourth_level)

    def fifth_level(i, carry):
        for g in range(2):
            b5[i, g] = columns_strided(fold(*[b4[2 * i + s - 2, g] for s in range(5)]), 2) * (1.0 / 256.0)
        return carry

    loop(2, 9, 7, fifth_level)
    blur = lambda ref, i: fold(*[ref[pl.ds(2 * i + s - 2, 8, stride=2), :] for s in range(5)])
    for i in (2, 8, 11):
        e4[i : i + 8, :] = columns_strided(blur(e3, i), 1) * (1.0 / 256.0)
    e5[2:10, :] = columns_strided(blur(e4, 2), 2) * (1.0 / 256.0)

    def lanes_up(y, n):
        even = 0.125 * (right(y, n) + left(y, n)) + 0.75 * y
        odd = 0.5 * (right(y, n // 2) + left(y, n // 2))
        return even, odd

    def on_grid(y, n, parity):
        even, odd = lanes_up(y, n)
        return jnp.where(parity, odd, even)

    parity_four = (lane % 4) != 0
    parity_three = (lane % 2) != 0

    def coefficient_b(fine, coarse, guide, sums, start, n, parity):
        parts = []
        for i in range(start // 2, start // 2 + 4):
            made = [rows_up(coarse[i - 1, g], coarse[i, g], coarse[i + 1, g]) for g in range(2)]
            for odd in range(2):
                x = 2 * i + odd
                place = spread(guide, x) * 15.0
                terms = [
                    hat(place, channel[g]) * (fine[x, g] - 0.5 * on_grid(made[g][odd], n, parity)) for g in range(2)
                ]
                parts.append(terms[0] + terms[1])
        sums[start : start + 8, :] = eight_totals(parts)

    for start in (4, 12):
        coefficient_b(b4, b5, e4, c4, start, 4, parity_four)
    for start in (10, 18, 26):
        coefficient_b(b3, b4, e3, c3, start, 2, parity_three)

    def raise_rows(src, dst, start, count, index=()):
        above = src[index + (pl.ds(start - 1, count), slice(None))]
        here = src[index + (pl.ds(start, count), slice(None))]
        below = src[index + (pl.ds(start + 1, count), slice(None))]
        even, odd = rows_up(above, here, below)
        dst[index + (pl.ds(2 * start, count, stride=2), slice(None))] = 0.5 * even
        dst[index + (pl.ds(2 * start + 1, count, stride=2), slice(None))] = 0.5 * odd

    r5[...] = e5[...] * (1.0 - 0.5 * gains[4])
    raise_rows(r5, u4, 1, 8)
    for t in range(3):
        rows = slice(8 * t, 8 * t + 8)
        value = gains[4] * (0.5 * e4[rows, :] + c4[rows, :]) + on_grid(u4[rows, :], 4, parity_four)
        r4[rows, :] = value - (0.5 * gains[3]) * e4[rows, :]
    raise_rows(r4, u3, 4, 8)
    raise_rows(r4, u3, 8, 8)
    for t in range(1, 4):
        rows = slice(8 * t, 8 * t + 8)
        value = gains[3] * (0.5 * e3[rows, :] + c3[rows, :]) + on_grid(u3[rows, :], 2, parity_three)
        r3[rows, :] = value - (0.5 * gains[2]) * e3[rows, :]

    base_a = lane // 2 + 12
    column_s = jnp.where((lane // 32) % 2 == 0, lane % 32 - 24 + 256, lane % 32 + 120 + 256)
    base_s = column_s // 2 - 128 + 12
    odd_column = (lane % 2) != 0
    clip = lambda x: jnp.clip(x, 0, 127)
    base_a, base_s = clip(base_a), clip(base_s)

    def expand(y, at):
        even, odd = 0.125 * (right(y) + left(y)) + 0.75 * y, 0.5 * (y + left(y))
        return jnp.where(odd_column, pick(odd, at), pick(even, at))

    scale_two = 2.0 / (BETA * 2.0**16)

    def widen(i, carry):
        for g in range(2):
            wide3[i, g] = expand(b3[i, g], base_a)
        wide3[i, 2] = on_grid(s3[i, 0], 2, odd_column) * (1.0 / (BETA * 2.0**24))
        return carry

    loop(10, 32, 11, widen)

    def coefficient_two(t, carry):
        fine = [raised([wide3[4 * t + 10 + n, g] for n in range(6)]) for g in range(3)]
        parts, side = [], []
        for n in range(8):
            x = 8 * t + 22 + n
            place = spread(g2, 0, x) * 15.0
            terms = [hat(place, channel[g]) * (d2[x, g] * scale_two - fine[g][n]) for g in range(2)]
            parts.append(terms[0] + terms[1])
            place = spread(h2, 0, x) * 15.0
            side.append(hat(place, split) * (s2[x, 0] * scale_two - fine[2][n]))
        rows = pl.ds(8 * t + 22, 8)
        c2a[rows, :] = 0.5 * eight_totals(parts)
        both = eight_totals(side)
        c2s[rows, :] = 0.5 * (both + right(both, 64))
        return carry

    loop(0, 5, UNROLL_SUMS, coefficient_two)
    for start in (8, 16, 24):
        raise_rows(r3, w2, start, 8)
    for t in range(2, 8):
        rows = slice(8 * t, 8 * t + 8)
        coarse = w2[rows, :]
        value = gains[2] * (0.5 * g2[0, rows, :] + c2a[rows, :]) + expand(coarse, base_a)
        r2a[rows, :] = value - (0.5 * gains[1]) * g2[0, rows, :]
        guide = h2[0, rows, :]
        value = gains[2] * (0.5 * guide + c2s[rows, :]) + expand(coarse, base_s)
        r2s[rows, :] = value - (0.5 * gains[1]) * guide

    def side_one(t, carry):
        rows = [s2[4 * t + 22 + n, 0] for n in range(6)]
        fine = [raised(y) for y in ([right(y) for y in rows], rows, [left(y) for y in rows])]
        parts = [[], []]
        for n in range(8):
            ups = two_phases(*[f[n] for f in fine])
            for c in range(2):
                x = 8 * t + 46 + n
                parts[c].append(hat(spread(h1, c, x) * 15.0, split) * (s1[x, c] * 1024.0 - ups[c]))
        for c in range(2):
            both = eight_totals(parts[c])
            c1s[c, pl.ds(8 * t + 46, 8), :] = both + right(both, 64)
        return carry

    loop(0, 9, UNROLL_SUMS, side_one)

    def side_zero(t, carry):
        rows = [[s1[4 * t + 47 + n, c] for n in range(6)] for c in range(2)]
        fine = [raised(y) for y in ([right(y) for y in rows[1]], rows[0], rows[1], [left(y) for y in rows[0]])]
        parts = [[] for c in range(4)]
        for n in range(8):
            ups = four_phases(*[f[n] for f in fine])
            for c in range(4):
                place = spread(lum, c, 8 * t + 96 + n) * (15.0 / BETA)
                parts[c].append(hat(place, split) * ups[c])
        for c in range(4):
            both = eight_totals(parts[c])
            both = both + right(both, 64)
            sums_s[c, pl.ds(pl.multiple_of(8 * t, 8), 8), :] = both
        return carry

    loop(0, 16, UNROLL_SUMS, side_zero)
    scale_one = gains[1] * (1.0 / (BETA * 2.0**18))
    for start in (20, 28, 36, 44, 52):
        raise_rows(r2a, wide_a, start, 8)
        raise_rows(r2s, wide_s, start, 8)

    def collapse_one(t, carry):
        rows = pl.ds(pl.multiple_of(8 * t, 8), 8)
        y, z = wide_a[rows, :], wide_s[rows, :]
        m, y, p = edges_two(y, z)
        ups_a = two_phases(m, y, p)
        ups_s = two_phases(right(z), z, left(z))
        found = []
        for c in range(2):
            guide = g1[c, rows, :]
            found.append(
                (0.5 * (gains[1] - gains[0])) * guide + scale_one * c1a[c, rows, :] + 0.5 * ups_a[c]
            )
        side = []
        for c in range(2):
            guide = h1[c, rows, :]
            side.append((0.5 * (gains[1] - gains[0])) * guide + scale_one * c1s[c, rows, :] + 0.5 * ups_s[c])
        found = edges_one(found[0], found[1], side[0], side[1])
        for n in range(4):
            rest_in[n, rows, :] = found[n]
        return carry

    rest_in = lum
    loop(5, 15, 5, collapse_one)

    scale_zero = gains[0] * (1.0 / (BETA * 2.0**10))
    source = iota((256, 256), 0)
    target = iota((256, 256), 1)
    inverse = jnp.where(target == 4 * (source % 64) + source // 64, 1.0, 0.0).astype(jnp.bfloat16)

    def collapse_zero(t, carry):
        start = pl.multiple_of(8 * t, 8)
        fine = []
        for n in range(4):
            rows = [rest_in[n, pl.ds(start + 47 + k, 8), :] for k in range(3)]
            fine.append(rows_up(*rows))
        for odd in range(2):
            ups = four_phases(*[f[odd] for f in fine])
            for c in range(4):
                rest[c, pl.ds(2 * start + odd, 8, stride=2), :] = 0.25 * ups[c]
        for c in range(4):
            for k in range(2):
                rows = pl.ds(pl.multiple_of(2 * start, 16) + 8 * k, 8)
                total = ends(sums[c, rows, :], sums_s[c, rows, :], 0, 127)
                rest[c, rows, :] = rest[c, rows, :] - scale_zero * total
        return carry

    loop(0, 8, 4, collapse_zero)
    low_half = iota((128, LANES), 1) < 64
    halves = [[], []]
    for pair in range(2):
        a, b = rest[2 * pair], rest[2 * pair + 1]
        halves[0].append(jnp.where(low_half, a, right(b, 64)))
        halves[1].append(jnp.where(low_half, right(a, 64), b))
    both = jnp.concatenate([jnp.concatenate(h, axis=1) for h in halves], axis=0)
    natural = select_columns(both, inverse)
    out[:, :256] = natural[:128] + gains[0] * base_term[:, :256]
    out[:, 256:] = natural[128:] + gains[0] * base_term[:, 256:]


def shape(*dims):
    return jax.ShapeDtypeStruct(dims, F32)


def vmem(*dims):
    return pltpu.VMEM(dims, F32)


def run_a(top, mid, bottom):
    whole = pl.BlockSpec(memory_space=pltpu.VMEM)
    return pl.pallas_call(
        kernel_a,
        out_shape=(
            shape(160, 4, HALF, LANES),
            shape(80, 2, HALF, LANES),
            shape(40, 2, HALF, LANES),
            shape(4, 128, LANES),
            shape(2, 160, LANES),
            shape(1, 80, LANES),
            shape(40, LANES),
            shape(128, 512),
        ),
        in_specs=[whole] * 3,
        out_specs=(whole,) * 8,
        scratch_shapes=[vmem(4, ROWS, LANES)],
        compiler_params=pltpu.CompilerParams(vmem_limit_bytes=40 << 20),
        cost_estimate=pl.CostEstimate(flops=60_000_000, transcendentals=2_600_000, bytes_accessed=6_000_000),
    )(top, mid, bottom)


def run_c(d1, d2, x15, g1):
    whole = pl.BlockSpec(memory_space=pltpu.VMEM)
    return pl.pallas_call(
        kernel_c,
        out_shape=(shape(4, 128, LANES), shape(2, 160, LANES)),
        in_specs=[whole] * 4,
        out_specs=(whole, whole),
        compiler_params=pltpu.CompilerParams(vmem_limit_bytes=40 << 20),
        cost_estimate=pl.CostEstimate(flops=30_000_000, transcendentals=0, bytes_accessed=3_000_000),
    )(d1, d2, x15, g1)


def run_b(gain, *arrays):
    whole = pl.BlockSpec(memory_space=pltpu.VMEM)
    return pl.pallas_call(
        kernel_b,
        out_shape=shape(128, 512),
        in_specs=[pl.BlockSpec(memory_space=pltpu.SMEM)] + [whole] * len(arrays),
        out_specs=whole,
        scratch_shapes=[
            vmem(4, ROWS, LANES),
            vmem(160, 2, HALF, LANES),
            vmem(80, 1, HALF, LANES),
            vmem(40, 1, HALF, LANES),
            vmem(2, 160, LANES),
            vmem(1, 80, LANES),
            vmem(40, LANES),
            vmem(40, 2, HALF, LANES),
            vmem(24, 2, HALF, LANES),
            vmem(16, 2, HALF, LANES),
            vmem(40, LANES),
            vmem(24, LANES),
            vmem(16, LANES),
            vmem(24, LANES),
            vmem(40, LANES),
            vmem(80, LANES),
            vmem(80, LANES),
            vmem(2, 160, LANES),
            vmem(4, 128, LANES),
            vmem(16, LANES),
            vmem(24, LANES),
            vmem(24, LANES),
            vmem(40, LANES),
            vmem(40, LANES),
            vmem(40, 3, HALF, LANES),
            vmem(80, LANES),
            vmem(80, LANES),
            vmem(80, LANES),
            vmem(160, LANES),
            vmem(160, LANES),
            vmem(4, 128, LANES),
        ],
        compiler_params=pltpu.CompilerParams(vmem_limit_bytes=48 << 20),
        cost_estimate=pl.CostEstimate(flops=60_000_000, transcendentals=1_300_000, bytes_accessed=6_000_000),
    )(gain, *arrays)


def ring(axis, shift):
    count = lax.axis_size(axis)
    return [(i, (i + shift) % count) for i in range(count)]


def local(luminance, level_gain):
    down = lambda x: lax.ppermute(x, "row", ring("row", 1))
    up = lambda x: lax.ppermute(x, "row", ring("row", -1))
    top, bottom = down(luminance), up(luminance)
    far_left = lax.ppermute(luminance[:, 384:], "col", ring("col", 1))
    far_right = lax.ppermute(luminance[:, :LANES], "col", ring("col", -1))
    d1, d2, d3, x15, g1, g2, g3, base_term = run_a(top, luminance, bottom)
    far_left, far_right, d3 = lax.optimization_barrier((far_left, far_right, d3))
    far = jnp.concatenate([far_left, far_right], axis=1)
    far_top, far_bottom = down(far[32:]), up(far[:96])
    sums, c1a = run_c(d1, d2, x15, g1)
    return run_b(
        level_gain, top, luminance, bottom, far_left, far_right, far_top, far_bottom,
        d2, d3, g1, g2, g3, base_term, sums, c1a,
    )


def solution(mesh):
    return jax.shard_map(
        local, mesh=mesh, in_specs=(P("row", "col"), P()), out_specs=P("row", "col"), check_vma=False
    )
```

time: 42.9 us -> 33.5 us (0.78)
  Pallas kernels: 26.2 us -> 18.1 us
  waiting for transfers between devices: 4.57 us -> 1.83 us
  starting transfers between devices: 8.97 us -> 11.1 us
  local copies, waits for them, and re-layouts: 2.89 us -> 1.91 us
    pallas_call x1, Pallas kernels: 18.9 us -> 10.1 us  [run_b(): pl.pallas_call(kernel_b, out_shape=shape(128, 512), in_specs=[pl.BlockSpe...]
    ppermute x4 -> x6, waiting for transfers between devices: 4.57 us -> 1.83 us  [the longest x2 1.82 us: local(): up = lambda x: lax.ppermute(x, 'row', ring('row', -1))]
    pallas_call x0 -> x1, Pallas kernels: none -> 2.36 us  [run_c(): pl.pallas_call(kernel_c, out_shape=(shape(4, 128, LANES), shape(2, 160, L...]
    ppermute x4 -> x6, starting transfers between devices: 8.97 us -> 11.1 us  [the longest x1 4.99 us: local(): far_right = lax.ppermute(luminance[:, :LANES], 'col', ring('col', -1))]
    pallas_call x1, Pallas kernels: 7.3 us -> 5.59 us  [run_a(): pl.pallas_call(kernel_a, out_shape=(shape(160, 4, HALF, LANES), shape(80,...]
    slice x4 -> x2, local copies, waits for them, and re-layouts: 1.94 us -> 0.93 us  [the longest x1 0.92 us: local(): far_right = lax.ppermute(luminance[:, :LANES], 'col', ring('col', -1))]
    unnamed x4 -> x7, local copies, waits for them, and re-layouts: 0.95 us -> 0.97 us
  transfers between devices with their start and end apart: 4 -> 6, of which waited for: 3 -> 1; matrix products, arithmetic and copies ran while one was open for 2% -> 3% of each run, Pallas kernels for 17% -> 24%
where the time goes in v3:
time: 33.5 us; the launch traced here: 33 us
  Pallas kernels  18.1 us (54%)
  starting transfers between devices  11.1 us (33%)
  local copies, waits for them, and re-layouts  1.91 us (6%)
  waiting for transfers between devices  1.83 us (5%)
    pallas_call x1, Pallas kernels, run_b(): pl.pallas_call(kernel_b, out_shape=shape(128, 512), in_specs=[pl.BlockSpe...  10.1 us
    pallas_call x1, Pallas kernels, run_a(): pl.pallas_call(kernel_a, out_shape=(shape(160, 4, HALF, LANES), shape(80,...  5.59 us
    ppermute x1, starting transfers between devices, local(): far_right = lax.ppermute(luminance[:, :LANES], 'col', ring('col', -1))  4.99 us
    ppermute x2, starting transfers between devices, local(): down = lambda x: lax.ppermute(x, 'row', ring('row', 1))  4.6 us
    pallas_call x1, Pallas kernels, run_c(): pl.pallas_call(kernel_c, out_shape=(shape(4, 128, LANES), shape(2, 160, L...  2.36 us
    ppermute x2, waiting for transfers between devices, local(): up = lambda x: lax.ppermute(x, 'row', ring('row', -1))  1.82 us
    ppermute x1, starting transfers between devices, local(): far_left = lax.ppermute(luminance[:, 384:], 'col', ring('col', 1))  1.37 us
    unnamed x7, local copies, waits for them, and re-layouts  0.97 us
  transfers between devices with their start and end apart: 6, of which 1 were waited for; matrix products, arithmetic and copies ran while one was open for 3% of the time, Pallas kernels for 24%

profile of v3, /device:TPU:1, one launch (start us, length us, event | category | flops | bytes accessed | tf_op | source)
XLA Modules:
  0.0 33.0 jit_solution(1369434693794324344)
XLA Ops:
  0.0 2.6 %collective-permute-start = (f32[128,512]{1,0:T(8,128)}, f32[128,512]{1,0:T(8,128)S(1)}, u32[]{:S(2)}, u32[]{:S(2)}) collective-permute-start(f32[128,512]{1,0:T(8,128)} %mid.3), channel_id=1, source_target_pairs={{0,16},{16,32},{32,48},{48,64},{64,80},{80,96},{96,112},{112,0},{1... | collective-permute-start | bytes 786440 | tf_op jit(solution)/shard_map/ppermute | solution.py:642
  2.6 0.0 collective-permute-start.1
  2.6 0.9 %fusion = (f32[128,128]{1,0:T(8,128)S(1)}, f32[128,128]{1,0:T(8,128)S(1)}) fusion(f32[128,512]{1,0:T(8,128)} %mid.3), kind=kLoop, calls=%fused_computation.2 | loop fusion | bytes 262144 | tf_op jit(solution)/shard_map/slice | solution.py:646
  3.5 1.4 %collective-permute-start.2 = (f32[128,128]{1,0:T(8,128)S(1)}, f32[128,128]{1,0:T(8,128)S(1)}, u32[]{:S(2)}, u32[]{:S(2)}) collective-permute-start(f32[128,128]{1,0:T(8,128)S(1)} %get-tuple-element.32), channel_id=1, source_target_pairs={{0,1},{1,2},{2,3},{3,4},{4,5},{5,6},{6,7},{7,8},{8,9},{9,10},{10,1... | collective-permute-start | bytes 196616 | tf_op jit(solution)/shard_map/ppermute | solution.py:645
  4.9 5.0 %collective-permute-start.3 = (f32[128,128]{1,0:T(8,128)S(1)}, f32[128,128]{1,0:T(8,128)S(1)}, u32[]{:S(2)}, u32[]{:S(2)}) collective-permute-start(f32[128,128]{1,0:T(8,128)S(1)} %get-tuple-element.31), channel_id=1, source_target_pairs={{0,15},{1,0},{2,1},{3,2},{4,3},{5,4},{6,5},{7,6},{8,7},{9,8},{10,9... | collective-permute-start | bytes 196616 | tf_op jit(solution)/shard_map/ppermute | solution.py:646
  9.9 0.0 collective-permute-done.top
  9.9 0.0 collective-permute-done.1.bottom
  9.9 0.0 copy-start
  9.9 0.9 %copy-done = f32[128,512]{1,0:T(8,128)S(1)} copy-done((f32[128,512]{1,0:T(8,128)S(1)}, f32[128,512]{1,0:T(8,128)}, u32[]{:S(2)}) %copy-start) | copy-done | bytes 262168
  10.8 5.6 %shard_map.28 = (f32[160,4,8,128]{3,2,1,0:T(8,128)S(1)}, f32[80,2,8,128]{3,2,1,0:T(8,128)S(1)}, f32[40,2,8,128]{3,2,1,0:T(8,128)S(1)}, f32[4,128,128]{2,1,0:T(8,...) custom-call(f32[128,512]{1,0:T(8,128)S(1)} %collective-permute-done., ...), custom_call_target="tpu_custom_call" | custom-call | flops 60000000 | bytes 6000000 | tf_op jit(solution)/shard_map/pallas_call | solution.py:559
  16.4 0.0 copy-start.1
  16.5 0.0 copy-start.2
  16.5 0.0 collective-permute-done.2.far_left
  16.5 0.0 collective-permute-done.3.far_right
  16.5 2.0 %collective-permute-start.4 = (f32[96,256]{1,0:T(8,128)S(1)}, f32[96,256]{1,0:T(8,128)S(1)}, u32[]{:S(2)}, u32[]{:S(2)}) collective-permute-start(f32[96,256]{1,0:T(8,128)S(1)} %get-tuple-element.34), channel_id=1, source_target_pairs={{0,16},{16,32},{32,48},{48,64},{64,80},{80,96},{96,112},{112,0},{1... | collective-permute-start | bytes 294920 | tf_op jit(solution)/shard_map/ppermute | solution.py:642
  18.5 0.1 collective-permute-start.5
  18.7 2.4 %shard_map.29 = (f32[4,128,128]{2,1,0:T(8,128)S(1)}, f32[2,160,128]{2,1,0:T(8,128)S(1)}) custom-call(f32[160,4,8,128]{3,2,1,0:T(8,128)S(1)} %get-tuple-element.27.d1, f32[80,2,8,128]{3,2,1,0:T(8,128)S(1)} %get-tuple-element.21.d2, f32[4,128,128]{2,1,0:T(8,128)S(1)} %get-tuple-element.28.x15, f32[2,160,128]{2,1,0:T(8,128)S(1)} %get-tuple-element.23.g1), custom_call_target="tpu_custom_call" | custom-call | flops 30000000 | bytes 3000000 | tf_op jit(solution)/shard_map/pallas_call | solution.py:581
  21.1 0.0 collective-permute-done.4.far_top
  21.1 1.8 %collective-permute-done.5.far_bottom = f32[96,256]{1,0:T(8,128)S(1)} collective-permute-done((f32[96,256]{1,0:T(8,128)S(1)}, f32[96,256]{1,0:T(8,128)S(1)}, u32[]{:S(2)}, u32[]{:S(2)}) %collective-permute-start.5) | collective-permute-done | bytes 98336 | tf_op jit(solution)/shard_map/ppermute | solution.py:643
  22.9 0.0 copy-done.1
  22.9 0.0 copy-done.2
  22.9 10.1 %shard_map.30 = f32[128,512]{1,0:T(8,128)} custom-call(f32[5]{0:T(128)S(1)} %copy-done.2, f32[128,512]{1,0:T(8,128)S(1)} %collective-permute-done.top, f32[128,512]{1,0:T(8,128)S(1)} %copy-done.1, f32[128,512]{1,0:T(8,128)S(1)} %collective-permute-done.1.bottom, f32[128,128]{1,0:T(8,128)S(1)} %collective-permute-done.2.far_left, ...), custom_call_target="tpu_custom_call" | custom-call | flops 60000000 | bytes 6000000 | tf_op jit(solution)/shard_map/pallas_call | solution.py:593
  (3 shorter events, 0.0 us)
Async XLA Ops:
  0.0 9.9 %collective-permute-start = (f32[128,512]{1,0:T(8,128)}, f32[128,512]{1,0:T(8,128)S(1)}, u32[]{:S(2)}, u32[]{:S(2)}) collective-permute-start(f32[128,512]{1,0:T(8,128)} %mid.3), channel_id=1, source_target_pairs={{0,16},{16,32},{32,48},{48,64},{64,80},{80,96},{96,112},{112,0},{1... | collective-permute-start | bytes 786440 | tf_op jit(solution)/shard_map/ppermute | solution.py:642
  2.6 7.3 %collective-permute-start.1 = (f32[128,512]{1,0:T(8,128)}, f32[128,512]{1,0:T(8,128)S(1)}, u32[]{:S(2)}, u32[]{:S(2)}) collective-permute-start(f32[128,512]{1,0:T(8,128)} %mid.3), channel_id=1, source_target_pairs={{0,112},{16,0},{32,16},{48,32},{64,48},{80,64},{96,80},{112,96},{1... | collective-permute-start | bytes 786440 | tf_op jit(solution)/shard_map/ppermute | solution.py:643
  3.5 12.9 %collective-permute-start.2 = (f32[128,128]{1,0:T(8,128)S(1)}, f32[128,128]{1,0:T(8,128)S(1)}, u32[]{:S(2)}, u32[]{:S(2)}) collective-permute-start(f32[128,128]{1,0:T(8,128)S(1)} %get-tuple-element.32), channel_id=1, source_target_pairs={{0,1},{1,2},{2,3},{3,4},{4,5},{5,6},{6,7},{7,8},{8,9},{9,10},{10,1... | collective-permute-start | bytes 196616 | tf_op jit(solution)/shard_map/ppermute | solution.py:645
  4.9 11.6 %collective-permute-start.3 = (f32[128,128]{1,0:T(8,128)S(1)}, f32[128,128]{1,0:T(8,128)S(1)}, u32[]{:S(2)}, u32[]{:S(2)}) collective-permute-start(f32[128,128]{1,0:T(8,128)S(1)} %get-tuple-element.31), channel_id=1, source_target_pairs={{0,15},{1,0},{2,1},{3,2},{4,3},{5,4},{6,5},{7,6},{8,7},{9,8},{10,9... | collective-permute-start | bytes 196616 | tf_op jit(solution)/shard_map/ppermute | solution.py:646
  9.9 1.0 %copy-start = (f32[128,512]{1,0:T(8,128)S(1)}, f32[128,512]{1,0:T(8,128)}, u32[]{:S(2)}) copy-start(f32[128,512]{1,0:T(8,128)} %mid.3) | copy-start | bytes 786436
  16.4 6.4 %copy-start.1 = (f32[128,512]{1,0:T(8,128)S(1)}, f32[128,512]{1,0:T(8,128)}, u32[]{:S(2)}) copy-start(f32[128,512]{1,0:T(8,128)} %mid.3) | copy-start | bytes 786436
  16.5 6.4 %copy-start.2 = (f32[5]{0:T(128)S(1)}, f32[5]{0:T(128)}, u32[]{:S(2)}) copy-start(f32[5]{0:T(128)} %gain_ref.1) | copy-start | bytes 64
  16.5 4.5 %collective-permute-start.4 = (f32[96,256]{1,0:T(8,128)S(1)}, f32[96,256]{1,0:T(8,128)S(1)}, u32[]{:S(2)}, u32[]{:S(2)}) collective-permute-start(f32[96,256]{1,0:T(8,128)S(1)} %get-tuple-element.34), channel_id=1, source_target_pairs={{0,16},{16,32},{32,48},{48,64},{64,80},{80,96},{96,112},{112,0},{1... | collective-permute-start | bytes 294920 | tf_op jit(solution)/shard_map/ppermute | solution.py:642
  18.5 4.3 %collective-permute-start.5 = (f32[96,256]{1,0:T(8,128)S(1)}, f32[96,256]{1,0:T(8,128)S(1)}, u32[]{:S(2)}, u32[]{:S(2)}) collective-permute-start(f32[96,256]{1,0:T(8,128)S(1)} %get-tuple-element.33), channel_id=1, source_target_pairs={{0,112},{16,0},{32,16},{48,32},{64,48},{80,64},{96,80},{112,96},{1... | collective-permute-start | bytes 294920 | tf_op jit(solution)/shard_map/ppermute | solution.py:643

commit v4 on v3

--- a/solution.py
+++ b/solution.py
@@ -14,9 +14,8 @@
 STEP = 1.0 / 15.0
 BETA = math.sqrt(800.0 * math.log2(math.e))
 F32 = jnp.float32
-UNROLL = {1: 53, 2: 26}
-UNROLL_TWO = {1: 39, 2: 26}
-UNROLL_SUMS = 4
+UNROLL_TWO = {1: 77, 2: 39}
+UNROLL_SUMS = 8
 
 
 def iota(shape, dim):
@@ -89,11 +88,11 @@
     return state
 
 
-def channel_chain(lum, anchors, d1, d2, d3):
+def first_level(lum, anchors, d1, low, high, size, above=0):
     groups = len(anchors)
 
     def row(e, odd):
-        values = [spread(lum, c, e) for c in range(4)]
+        values = [spread(lum, c, e - above) for c in range(4)]
         return [[bump(v, a, 2.0 * odd + 2.0 * (c % 2)) for c, v in enumerate(values)] for a in anchors]
 
     def step(i, state):
@@ -110,8 +109,10 @@
             d1[i, 2 * g + 1] = out[1]
         return even, even_next, odd
 
-    loop(2, 159, UNROLL[groups], step, (row(2, 0), row(4, 0), row(3, 1)))
-
+    loop(low, high, size, step, (row(2 * low - 2, 0), row(2 * low, 0), row(2 * low - 1, 1)))
+
+
+def next_levels(d1, d2, d3, groups):
     def second_level(i, carry):
         for g in range(groups):
             y = [fold(*[d1[2 * i + s - 2, 2 * g + c] for s in range(5)]) for c in range(2)]
@@ -158,41 +159,22 @@
     return (iota((HALF, LANES), 0) + base).astype(F32)
 
 
-def kernel_a(top, mid, bottom, d1, d2, d3, x15, g1, g2, g3, base_term, lum):
+def phase_table():
     source = iota((256, 256), 0)
     target = iota((256, 256), 1)
-    table = jnp.where(source == 4 * (target % 64) + target // 64, 1.0, 0.0).astype(jnp.bfloat16)
-    for ref, skip, start, count in ((top, 32, 0, 96), (mid, 0, 96, 128), (bottom, 0, 224, 96)):
-        both = jnp.concatenate([ref[skip : skip + count, :256], ref[skip : skip + count, 256:]], axis=0)
-        split = select_columns(both, table)
-        low_half = iota((count, LANES), 1) < 64
-        for pair in range(2):
-            a = split[:count, pair * LANES : (pair + 1) * LANES]
-            b = split[count:, pair * LANES : (pair + 1) * LANES]
-            for c, part in (
-                (2 * pair, jnp.where(low_half, a, right(b, 64))),
-                (2 * pair + 1, jnp.where(low_half, right(a, 64), b)),
-            ):
-                lum[c, start : start + count, :] = part * BETA
-                if start == 96:
-                    x15[c] = part * 15.0
-    guide_chain(lum, 1.0 / BETA, g1, g2, g3)
-    anchors = [anchor_tile(HALF * g) * (BETA * STEP) for g in range(2)]
-    channel_chain(lum, anchors, d1, d2, d3)
-
-    def natural(t, carry):
-        rows = pl.ds(pl.multiple_of(8 * t, 8), 8)
-        value = mid[rows, :]
-        place = value * 15.0
-        lower = jnp.floor(place)
-        part = place - lower
-        near = value - lower * STEP
-        far = value - (lower + 1.0) * STEP
-        bend = (1.0 - part) * near * jnp.exp(near * near * -800.0) + part * far * jnp.exp(far * far * -800.0)
-        base_term[rows, :] = 0.5 * value + bend
-        return carry
-
-    loop(0, 16, 4, natural)
+    return jnp.where(source == 4 * (target % 64) + target // 64, 1.0, 0.0).astype(jnp.bfloat16)
+
+
+def phases_of(block, table):
+    count = block.shape[0]
+    split = select_columns(jnp.concatenate([block[:, :256], block[:, 256:]], axis=0), table)
+    low_half = iota((count, LANES), 1) < 64
+    found = []
+    for pair in range(2):
+        a = split[:count, pair * LANES : (pair + 1) * LANES]
+        b = split[count:, pair * LANES : (pair + 1) * LANES]
+        found += [jnp.where(low_half, a, right(b, 64)), jnp.where(low_half, right(a, 64), b)]
+    return found
 
 
 def hat(place, channel):
@@ -235,7 +217,27 @@
     return q0 + 0.25 * (tm + t0), t0, q1 + 0.25 * (t0 + t1), t1
 
 
-def kernel_c(d1, d2, x15, g1, sums, c1a):
+def sums_of_level_zero(d1, x15, sums):
+    channel = [anchor_tile(HALF * g) for g in range(2)]
+
+    def level_zero(t, carry):
+        parts = [[None] * 8 for c in range(4)]
+        for g in range(2):
+            rows = [[d1[4 * t + 47 + n, 2 * g + c] for n in range(6)] for c in range(2)]
+            fine = [raised(y) for y in ([right(y) for y in rows[1]], rows[0], rows[1], [left(y) for y in rows[0]])]
+            for n in range(8):
+                ups = four_phases(*[f[n] for f in fine])
+                for c in range(4):
+                    part = hat(spread(x15, c, 8 * t + n), channel[g]) * ups[c]
+                    parts[c][n] = part if g == 0 else parts[c][n] + part
+        for c in range(4):
+            sums[c, pl.ds(8 * t, 8), :] = eight_totals(parts[c])
+        return carry
+
+    return level_zero
+
+
+def sums_in_a(d1, d2, x15, g1, sums, c1a):
     channel = [anchor_tile(HALF * g) for g in range(2)]
 
     def level_one(t, carry):
@@ -255,25 +257,53 @@
 
     loop(0, 9, UNROLL_SUMS, level_one)
 
-    def level_zero(t, carry):
-        parts = [[None] * 8 for c in range(4)]
-        for g in range(2):
-            rows = [[d1[4 * t + 47 + n, 2 * g + c] for n in range(6)] for c in range(2)]
-            fine = [raised(y) for y in ([right(y) for y in rows[1]], rows[0], rows[1], [left(y) for y in rows[0]])]
-            for n in range(8):
-                ups = four_phases(*[f[n] for f in fine])
-                for c in range(4):
-                    part = hat(spread(x15, c, 8 * t + n), channel[g]) * ups[c]
-                    parts[c][n] = part if g == 0 else parts[c][n] + part
-        for c in range(4):
-            sums[c, pl.ds(pl.multiple_of(8 * t, 8), 8), :] = eight_totals(parts[c])
-        return carry
-
-    loop(0, 16, UNROLL_SUMS, level_zero)
+    level_zero = sums_of_level_zero(d1, x15, sums)
+    level_zero(0, ())
+    level_zero(15, ())
+
+
+def kernel_z(mid, x15, base_term, near_left, near_right, d1, sums, lum):
+    for c, part in enumerate(phases_of(mid[...], phase_table())):
+        x15[c] = part * 15.0
+        lum[c] = part * BETA
+    near_left[...] = mid[:, :LANES]
+    near_right[...] = mid[:, 384:]
+
+    def natural(t, carry):
+        rows = pl.ds(pl.multiple_of(8 * t, 8), 8)
+        value = mid[rows, :]
+        place = value * 15.0
+        lower = jnp.floor(place)
+        part = place - lower
+        near = value - lower * STEP
+        far = value - (lower + 1.0) * STEP
+        bend = (1.0 - part) * near * jnp.exp(near * near * -800.0) + part * far * jnp.exp(far * far * -800.0)
+        base_term[rows, :] = 0.5 * value + bend
+        return carry
+
+    loop(0, 16, 8, natural)
+    anchors = [anchor_tile(HALF * g) * (BETA * STEP) for g in range(2)]
+    first_level(lum, anchors, d1, 49, 111, 31, above=96)
+    loop(1, 15, 7, sums_of_level_zero(d1, x15, sums))
+
+
+def kernel_a(top, bottom, x15, d1_in, sums_in, d1, d2, d3, g1, g2, g3, sums, c1a, lum):
+    table = phase_table()
+    for ref, skip, start in ((top, 32, 0), (bottom, 0, 224)):
+        for c, part in enumerate(phases_of(ref[skip : skip + 96, :], table)):
+            lum[c, start : start + 96, :] = part * BETA
+    for c in range(4):
+        lum[c, 96:224, :] = x15[c] * (BETA * STEP)
+    guide_chain(lum, 1.0 / BETA, g1, g2, g3)
+    anchors = [anchor_tile(HALF * g) * (BETA * STEP) for g in range(2)]
+    first_level(lum, anchors, d1, 2, 49, 24)
+    first_level(lum, anchors, d1, 111, 159, 24)
+    next_levels(d1, d2, d3, 2)
+    sums_in_a(d1, d2, x15, g1, sums, c1a)
 
 
 def kernel_b(
-    gain_ref, top, mid, bottom, far_left, far_right, far_top, far_bottom,
+    gain_ref, far_left, near_left, near_right, far_right,
     d2, d3, g1, g2, g3, base_term, sums, c1a, out,
     lum, s1, s2, s3, h1, h2, h3, b3, b4, b5, e3, e4, e5,
     c4, c3, c2a, c2s, c1s, sums_s, r5, r4, u4, r3, u3, wide3, w2, r2a, r2s, wide_a, wide_s, rest,
@@ -287,11 +317,10 @@
     target = iota((512, 256), 1)
     wanted = 32 + 320 * ((target // 32) % 2) + 4 * (target % 32) + target // 64
     table = jnp.where(source == wanted, 1.0, 0.0).astype(jnp.bfloat16)
-    for natural, start, count in (
-        ([far_top[:, :LANES], top[32:, :LANES], top[32:, 384:], far_top[:, LANES:]], 0, 96),
-        ([far_left[...], mid[:, :LANES], mid[:, 384:], far_right[...]], 96, 128),
-        ([far_bottom[:, :LANES], bottom[:96, :LANES], bottom[:96, 384:], far_bottom[:, LANES:]], 224, 96),
-    ):
+    count = 160
+    for start in range(0, ROWS, count):
+        part = slice(start, start + count)
+        natural = [ref[part, :] for ref in (far_left, near_left, near_right, far_right)]
         pieces = select_columns(jnp.concatenate(natural, axis=1), table)
         low_half = iota((count, LANES), 1) < 64
         for pair in range(2):
@@ -300,7 +329,8 @@
             lum[2 * pair, start : start + count, :] = jnp.where(low_half, a, b)
             lum[2 * pair + 1, start : start + count, :] = jnp.where(low_half, b, a)
     guide_chain(lum, 1.0 / BETA, h1, h2, h3)
-    channel_chain(lum, [split * (BETA * STEP)], s1, s2, s3)
+    first_level(lum, [split * (BETA * STEP)], s1, 2, 159, 53)
+    next_levels(s1, s2, s3, 1)
 
     first, last = lane == 0, lane == 127
     turn = lambda x, source, to: pltpu.roll(x, (to - source) % LANES, axis=1)
@@ -554,7 +584,27 @@
     return pltpu.VMEM(dims, F32)
 
 
-def run_a(top, mid, bottom):
+def run_z(mid):
+    whole = pl.BlockSpec(memory_space=pltpu.VMEM)
+    return pl.pallas_call(
+        kernel_z,
+        out_shape=(
+            shape(4, 128, LANES),
+            shape(128, 512),
+            shape(128, LANES),
+            shape(128, LANES),
+            shape(160, 4, HALF, LANES),
+            shape(4, 128, LANES),
+        ),
+        in_specs=[whole],
+        out_specs=(whole,) * 6,
+        scratch_shapes=[vmem(4, 128, LANES)],
+        compiler_params=pltpu.CompilerParams(vmem_limit_bytes=40 << 20),
+        cost_estimate=pl.CostEstimate(flops=30_000_000, transcendentals=1_100_000, bytes_accessed=2_000_000),
+    )(mid)
+
+
+def run_a(top, bottom, x15, d1, sums):
     whole = pl.BlockSpec(memory_space=pltpu.VMEM)
     return pl.pallas_call(
         kernel_a,
@@ -562,30 +612,19 @@
             shape(160, 4, HALF, LANES),
             shape(80, 2, HALF, LANES),
             shape(40, 2, HALF, LANES),
-            shape(4, 128, LANES),
             shape(2, 160, LANES),
             shape(1, 80, LANES),
             shape(40, LANES),
-            shape(128, 512),
+            shape(4, 128, LANES),
+            shape(2, 160, LANES),
         ),
-        in_specs=[whole] * 3,
+        in_specs=[whole] * 5,
         out_specs=(whole,) * 8,
+        input_output_aliases={3: 0, 4: 6},
         scratch_shapes=[vmem(4, ROWS, LANES)],
         compiler_params=pltpu.CompilerParams(vmem_limit_bytes=40 << 20),
         cost_estimate=pl.CostEstimate(flops=60_000_000, transcendentals=2_600_000, bytes_accessed=6_000_000),
-    )(top, mid, bottom)
-
-
-def run_c(d1, d2, x15, g1):
-    whole = pl.BlockSpec(memory_space=pltpu.VMEM)
-    return pl.pallas_call(
-        kernel_c,
-        out_shape=(shape(4, 128, LANES), shape(2, 160, LANES)),
-        in_specs=[whole] * 4,
-        out_specs=(whole, whole),
-        compiler_params=pltpu.CompilerParams(vmem_limit_bytes=40 << 20),
-        cost_estimate=pl.CostEstimate(flops=30_000_000, transcendentals=0, bytes_accessed=3_000_000),
-    )(d1, d2, x15, g1)
+    )(top, bottom, x15, d1, sums)
 
 
 def run_b(gain, *arrays):
@@ -639,19 +678,16 @@
 
 
 def local(luminance, level_gain):
-    down = lambda x: lax.ppermute(x, "row", ring("row", 1))
-    up = lambda x: lax.ppermute(x, "row", ring("row", -1))
-    top, bottom = down(luminance), up(luminance)
-    far_left = lax.ppermute(luminance[:, 384:], "col", ring("col", 1))
-    far_right = lax.ppermute(luminance[:, :LANES], "col", ring("col", -1))
-    d1, d2, d3, x15, g1, g2, g3, base_term = run_a(top, luminance, bottom)
-    far_left, far_right, d3 = lax.optimization_barrier((far_left, far_right, d3))
-    far = jnp.concatenate([far_left, far_right], axis=1)
-    far_top, far_bottom = down(far[32:]), up(far[:96])
-    sums, c1a = run_c(d1, d2, x15, g1)
+    top = lax.ppermute(luminance, "row", ring("row", 1))
+    bottom = lax.ppermute(luminance, "row", ring("row", -1))
+    x15, base_term, mid_left, mid_right, d1, sums = run_z(luminance)
+    near_left = jnp.concatenate([top[32:, :LANES], mid_left, bottom[:96, :LANES]], axis=0)
+    near_right = jnp.concatenate([top[32:, 384:], mid_right, bottom[:96, 384:]], axis=0)
+    far_left = lax.ppermute(near_right, "col", ring("col", 1))
+    far_right = lax.ppermute(near_left, "col", ring("col", -1))
+    d1, d2, d3, g1, g2, g3, sums, c1a = run_a(top, bottom, x15, d1, sums)
     return run_b(
-        level_gain, top, luminance, bottom, far_left, far_right, far_top, far_bottom,
-        d2, d3, g1, g2, g3, base_term, sums, c1a,
+        level_gain, far_left, near_left, near_right, far_right, d2, d3, g1, g2, g3, base_term, sums, c1a
     )
 
 

time: 33.5 us -> 29.3 us (0.87); the launches traced: 33 us -> 29.2 us
  starting transfers between devices: 11.1 us -> 8.98 us
  local copies, waits for them, and re-layouts: 1.91 us -> 1 us
  Pallas kernels: 18.1 us -> 17.5 us
    ppermute x6 -> x4, starting transfers between devices: 11.1 us -> 8.98 us  [the longest x1 5.01 us: local(): far_right = lax.ppermute(near_left, 'col', ring('col', -1))]
    pallas_call x1, Pallas kernels: 5.59 us -> 4.46 us  [run_a(): pl.pallas_call(kernel_a, out_shape=(shape(160, 4, HALF, LANES), shape(80,...]
    pallas_call x1, Pallas kernels: 2.36 us -> 3.34 us  [run_z(): pl.pallas_call(kernel_z, out_shape=(shape(4, 128, LANES), shape(128, 512)...]
    slice x2, local copies, waits for them, and re-layouts: 0.93 us -> 0.02 us  [the longest x1 0.01 us: local(): top[32:, :LANES]]
    pallas_call x1, Pallas kernels: 10.1 us -> 9.66 us  [run_b(): pl.pallas_call(kernel_b, out_shape=shape(128, 512), in_specs=[pl.BlockSpe...]
    ppermute x6 -> x4, waiting for transfers between devices: 1.83 us -> 1.66 us  [the longest x1 1.65 us: local(): bottom = lax.ppermute(luminance, 'row', ring('row', -1))]
    unnamed x7 -> x4, local copies, waits for them, and re-layouts: 0.97 us -> 0.98 us
  transfers between devices with their start and end apart: 6 -> 4, of which waited for: 1 -> 1; matrix products, arithmetic and copies ran while one was open for 3% -> 0% of each run, Pallas kernels for 24% -> 27%
where the time goes in v4:
time: 29.3 us; the launch traced here: 29.2 us
  Pallas kernels  17.5 us (60%)
  starting transfers between devices  8.98 us (31%)
  waiting for transfers between devices  1.66 us (6%)
  local copies, waits for them, and re-layouts  1 us (3%)
    pallas_call x1, Pallas kernels, run_b(): pl.pallas_call(kernel_b, out_shape=shape(128, 512), in_specs=[pl.BlockSpe...  9.66 us
    ppermute x1, starting transfers between devices, local(): far_right = lax.ppermute(near_left, 'col', ring('col', -1))  5.01 us
    pallas_call x1, Pallas kernels, run_a(): pl.pallas_call(kernel_a, out_shape=(shape(160, 4, HALF, LANES), shape(80,...  4.46 us
    pallas_call x1, Pallas kernels, run_z(): pl.pallas_call(kernel_z, out_shape=(shape(4, 128, LANES), shape(128, 512)...  3.34 us
    ppermute x1, starting transfers between devices, local(): top = lax.ppermute(luminance, 'row', ring('row', 1))  2.6 us
    ppermute x1, waiting for transfers between devices, local(): bottom = lax.ppermute(luminance, 'row', ring('row', -1))  1.65 us
    ppermute x1, starting transfers between devices, local(): far_left = lax.ppermute(near_right, 'col', ring('col', 1))  1.37 us
    unnamed x4, local copies, waits for them, and re-layouts  0.98 us
  transfers between devices with their start and end apart: 4, of which 1 were waited for; matrix products, arithmetic and copies ran while one was open for 0% of the time, Pallas kernels for 27%

profile of v4, /device:TPU:1, one launch (start us, length us, event | category | flops | bytes accessed | tf_op | source)
XLA Modules:
  0.0 29.2 jit_solution(11878218323011573167)
XLA Ops:
  0.0 2.6 %collective-permute-start = (f32[128,512]{1,0:T(8,128)}, f32[128,512]{1,0:T(8,128)S(1)}, u32[]{:S(2)}, u32[]{:S(2)}) collective-permute-start(f32[128,512]{1,0:T(8,128)} %mid.1), channel_id=1, source_target_pairs={{0,16},{16,32},{32,48},{48,64},{64,80},{80,96},{96,112},{112,0},{1... | collective-permute-start | bytes 786440 | tf_op jit(solution)/shard_map/ppermute | solution.py:681
  2.6 0.0 collective-permute-start.1
  2.6 0.0 copy-start.1
  2.6 1.0 %copy-done.1 = f32[128,512]{1,0:T(8,128)S(1)} copy-done((f32[128,512]{1,0:T(8,128)S(1)}, f32[128,512]{1,0:T(8,128)}, u32[]{:S(2)}) %copy-start.1) | copy-done | bytes 262168
  3.6 3.3 %shard_map.28 = (f32[4,128,128]{2,1,0:T(8,128)S(1)}, f32[128,512]{1,0:T(8,128)S(1)}, f32[128,128]{1,0:T(8,128)S(1)}, f32[128,128]{1,0:T(8,128)S(1)}, f32[160,4,8...) custom-call(f32[128,512]{1,0:T(8,128)S(1)} %copy-done.1), custom_call_target="tpu_custom_call" | custom-call | flops 30000000 | bytes 2000000 | tf_op jit(solution)/shard_map/pallas_call | solution.py:589
  6.9 0.0 collective-permute-done.top
  7.0 1.6 %collective-permute-done.1.bottom = f32[128,512]{1,0:T(8,128)S(1)} collective-permute-done((f32[128,512]{1,0:T(8,128)}, f32[128,512]{1,0:T(8,128)S(1)}, u32[]{:S(2)}, u32[]{:S(2)}) %collective-permute-start.1) | collective-permute-done | bytes 262176 | tf_op jit(solution)/shard_map/ppermute | solution.py:682
  8.6 1.4 %collective-permute-start.2 = (f32[320,128]{1,0:T(8,128)S(1)}, f32[320,128]{1,0:T(8,128)S(1)}, u32[]{:S(2)}, u32[]{:S(2)}) collective-permute-start(f32[320,128]{1,0:T(8,128)S(1)} %pad_maximum_fusion.near_right), channel_id=1, source_target_pairs={{0,1},{1,2},{2,3},{3,4},{4,5},{5,6},{6,7},{7,8},{8,9},{9,10},{10,1... | collective-permute-start | bytes 491528 | tf_op jit(solution)/shard_map/ppermute | solution.py:686
  10.0 0.0 copy-start
  10.0 5.0 %collective-permute-start.3 = (f32[320,128]{1,0:T(8,128)S(1)}, f32[320,128]{1,0:T(8,128)S(1)}, u32[]{:S(2)}, u32[]{:S(2)}) collective-permute-start(f32[320,128]{1,0:T(8,128)S(1)} %pad_maximum_fusion.1.near_left), channel_id=1, source_target_pairs={{0,15},{1,0},{2,1},{3,2},{4,3},{5,4},{6,5},{7,6},{8,7},{9,8},{10,9... | collective-permute-start | bytes 491528 | tf_op jit(solution)/shard_map/ppermute | solution.py:687
  15.0 4.5 %shard_map.29 = (f32[160,4,8,128]{3,2,1,0:T(8,128)S(1)}, f32[80,2,8,128]{3,2,1,0:T(8,128)S(1)}, f32[40,2,8,128]{3,2,1,0:T(8,128)S(1)}, f32[2,160,128]{2,1,0:T(8,...) custom-call(f32[128,512]{1,0:T(8,128)S(1)} %collective-permute-done., ...), custom_call_target="tpu_custom_call", output_to_operand_aliasing={{0}: (3, {}), {6}: (4, {})} | custom-call | flops 60000000 | bytes 6000000 | tf_op jit(solution)/shard_map/pallas_call | solution.py:609
  19.5 0.0 collective-permute-done.2.far_left
  19.5 0.0 collective-permute-done.3.far_right
  19.5 0.0 copy-done
  19.5 9.7 %shard_map.30 = f32[128,512]{1,0:T(8,128)} custom-call(f32[5]{0:T(128)S(1)} %copy-done, f32[320,128]{1,0:T(8,128)S(1)} %collective-permute-done.2.far_left, f32[320,128]{1,0:T(8,128)S(1)} %pad_maximum_fusion.1.near_left, f32[320,128]{1,0:T(8,128)S(1)} %pad_maximum_fusion.near_right, f32[320,128]{1,0:T(8,128)S(1)} %collective-permute-done.3.far_right, ...), custom_call_target="tpu_custom_call" | custom-call | flops 60000000 | bytes 6000000 | tf_op jit(solution)/shard_map/pallas_call | solution.py:632
  (4 shorter events, 0.0 us)
Async XLA Ops:
  0.0 6.9 %collective-permute-start = (f32[128,512]{1,0:T(8,128)}, f32[128,512]{1,0:T(8,128)S(1)}, u32[]{:S(2)}, u32[]{:S(2)}) collective-permute-start(f32[128,512]{1,0:T(8,128)} %mid.1), channel_id=1, source_target_pairs={{0,16},{16,32},{32,48},{48,64},{64,80},{80,96},{96,112},{112,0},{1... | collective-permute-start | bytes 786440 | tf_op jit(solution)/shard_map/ppermute | solution.py:681
  2.6 6.0 %collective-permute-start.1 = (f32[128,512]{1,0:T(8,128)}, f32[128,512]{1,0:T(8,128)S(1)}, u32[]{:S(2)}, u32[]{:S(2)}) collective-permute-start(f32[128,512]{1,0:T(8,128)} %mid.1), channel_id=1, source_target_pairs={{0,112},{16,0},{32,16},{48,32},{64,48},{80,64},{96,80},{112,96},{1... | collective-permute-start | bytes 786440 | tf_op jit(solution)/shard_map/ppermute | solution.py:682
  2.6 1.0 %copy-start.1 = (f32[128,512]{1,0:T(8,128)S(1)}, f32[128,512]{1,0:T(8,128)}, u32[]{:S(2)}) copy-start(f32[128,512]{1,0:T(8,128)} %mid.1) | copy-start | bytes 786436
  8.6 10.9 %collective-permute-start.2 = (f32[320,128]{1,0:T(8,128)S(1)}, f32[320,128]{1,0:T(8,128)S(1)}, u32[]{:S(2)}, u32[]{:S(2)}) collective-permute-start(f32[320,128]{1,0:T(8,128)S(1)} %pad_maximum_fusion.near_right), channel_id=1, source_target_pairs={{0,1},{1,2},{2,3},{3,4},{4,5},{5,6},{6,7},{7,8},{8,9},{9,10},{10,1... | collective-permute-start | bytes 491528 | tf_op jit(solution)/shard_map/ppermute | solution.py:686
  10.0 9.5 %copy-start = (f32[5]{0:T(128)S(1)}, f32[5]{0:T(128)}, u32[]{:S(2)}) copy-start(f32[5]{0:T(128)} %gain_ref.1) | copy-start | bytes 64
  10.0 9.5 %collective-permute-start.3 = (f32[320,128]{1,0:T(8,128)S(1)}, f32[320,128]{1,0:T(8,128)S(1)}, u32[]{:S(2)}, u32[]{:S(2)}) collective-permute-start(f32[320,128]{1,0:T(8,128)S(1)} %pad_maximum_fusion.1.near_left), channel_id=1, source_target_pairs={{0,15},{1,0},{2,1},{3,2},{4,3},{5,4},{6,5},{7,6},{8,7},{9,8},{10,9... | collective-permute-start | bytes 491528 | tf_op jit(solution)/shard_map/ppermute | solution.py:687

commit v5 on v4

--- a/solution.py
+++ b/solution.py
@@ -16,6 +16,7 @@
 F32 = jnp.float32
 UNROLL_TWO = {1: 77, 2: 39}
 UNROLL_SUMS = 8
+EARLY = 28
 
 
 def iota(shape, dim):
@@ -262,12 +263,24 @@
     level_zero(15, ())
 
 
-def kernel_z(mid, x15, base_term, near_left, near_right, d1, sums, lum):
-    for c, part in enumerate(phases_of(mid[...], phase_table())):
+def kernel_z(block, x15, base_term, near_left, near_right, piece_left, piece_right, d1, sums, lum, mid, arrived):
+    copies = []
+    for q in range(4):
+        rows = pl.ds(32 * q, 32)
+        copies.append(pltpu.make_async_copy(block.at[rows, :], mid.at[rows, :], arrived.at[q]))
+        copies[-1].start()
+    table = phase_table()
+    for copy in copies:
+        copy.wait()
+    for c, part in enumerate(phases_of(mid[...], table)):
         x15[c] = part * 15.0
         lum[c] = part * BETA
     near_left[...] = mid[:, :LANES]
     near_right[...] = mid[:, 384:]
+    for n in range(3):
+        rows = slice(80 * n, 80 * n + 80)
+        piece_left[rows, :] = right(mid[48:, :LANES], 96 - 32 * n)
+        piece_right[rows, :] = right(mid[48:, 384:], 96 - 32 * n)
 
     def natural(t, carry):
         rows = pl.ds(pl.multiple_of(8 * t, 8), 8)
@@ -287,16 +300,40 @@
     loop(1, 15, 7, sums_of_level_zero(d1, x15, sums))
 
 
-def kernel_a(top, bottom, x15, d1_in, sums_in, d1, d2, d3, g1, g2, g3, sums, c1a, lum):
+def outer_phases(top, bottom, lum):
     table = phase_table()
-    for ref, skip, start in ((top, 32, 0), (bottom, 0, 224)):
-        for c, part in enumerate(phases_of(ref[skip : skip + 96, :], table)):
-            lum[c, start : start + 96, :] = part * BETA
+    outer = jnp.concatenate([top[32:, :], bottom[:96, :]], axis=0)
+    for c, part in enumerate(phases_of(outer, table)):
+        lum[c, :96, :] = part[:96] * BETA
+        lum[c, 224:, :] = part[96:] * BETA
+
+
+def upper_rows(lum, d1):
+    first_level(lum, [anchor_tile(HALF * g) * (BETA * STEP) for g in range(2)], d1, 2, 2 + EARLY, EARLY)
+
+
+def kernel_p(early, top, bottom, middle, piece, d1_in, send_left, lum, d1):
+    lane = iota((240, LANES), 1)
+    direct = jnp.concatenate([top[32:, :LANES], middle[:48, :], bottom[:96, :LANES]], axis=0)
+    send_left[...] = jnp.where(lane < 96, direct, piece[...])
+
+    @pl.when(early[0] == 1)
+    def _():
+        outer_phases(top, bottom, lum)
+        upper_rows(lum, d1)
+
+
+def kernel_a(early, top, bottom, x15, lum_in, d1_in, sums_in, lum, d1, d2, d3, g1, g2, g3, sums, c1a):
+    @pl.when(early[0] == 0)
+    def _():
+        outer_phases(top, bottom, lum)
+        upper_rows(lum, d1)
+
     for c in range(4):
         lum[c, 96:224, :] = x15[c] * (BETA * STEP)
     guide_chain(lum, 1.0 / BETA, g1, g2, g3)
     anchors = [anchor_tile(HALF * g) * (BETA * STEP) for g in range(2)]
-    first_level(lum, anchors, d1, 2, 49, 24)
+    first_level(lum, anchors, d1, 2 + EARLY, 49, 47 - EARLY)
     first_level(lum, anchors, d1, 111, 159, 24)
     next_levels(d1, d2, d3, 2)
     sums_in_a(d1, d2, x15, g1, sums, c1a)
@@ -317,10 +354,17 @@
     target = iota((512, 256), 1)
     wanted = 32 + 320 * ((target // 32) % 2) + 4 * (target % 32) + target // 64
     table = jnp.where(source == wanted, 1.0, 0.0).astype(jnp.bfloat16)
+    def unpacked(ref, low, high):
+        a, b, c = [right(ref[80 * n : 80 * n + 80, :], 32 + 32 * n) for n in range(3)]
+        at_lane = iota((80, LANES), 1)
+        inner = jnp.where(at_lane < low, a, jnp.where(at_lane < high, b, c))
+        return jnp.concatenate([ref[:144, :], inner, ref[144:, :]], axis=0)
+
+    whole_left, whole_right = unpacked(far_left, 64, 96), unpacked(far_right, 32, 64)
     count = 160
     for start in range(0, ROWS, count):
         part = slice(start, start + count)
-        natural = [ref[part, :] for ref in (far_left, near_left, near_right, far_right)]
+        natural = [whole_left[part], near_left[part, :], near_right[part, :], whole_right[part]]
         pieces = select_columns(jnp.concatenate(natural, axis=1), table)
         low_half = iota((count, LANES), 1) < 64
         for pair in range(2):
@@ -539,7 +583,7 @@
         return carry
 
     rest_in = lum
-    loop(5, 15, 5, collapse_one)
+    loop(5, 15, 10, collapse_one)
 
     scale_zero = gains[0] * (1.0 / (BETA * 2.0**10))
     source = iota((256, 256), 0)
@@ -563,7 +607,7 @@
                 rest[c, rows, :] = rest[c, rows, :] - scale_zero * total
         return carry
 
-    loop(0, 8, 4, collapse_zero)
+    loop(0, 8, 8, collapse_zero)
     low_half = iota((128, LANES), 1) < 64
     halves = [[], []]
     for pair in range(2):
@@ -593,22 +637,38 @@
             shape(128, 512),
             shape(128, LANES),
             shape(128, LANES),
+            shape(240, LANES),
+            shape(240, LANES),
             shape(160, 4, HALF, LANES),
             shape(4, 128, LANES),
         ),
-        in_specs=[whole],
-        out_specs=(whole,) * 6,
-        scratch_shapes=[vmem(4, 128, LANES)],
+        in_specs=[pl.BlockSpec(memory_space=pltpu.HBM)],
+        out_specs=(whole,) * 8,
+        scratch_shapes=[vmem(4, 128, LANES), vmem(128, 512), pltpu.SemaphoreType.DMA((4,))],
         compiler_params=pltpu.CompilerParams(vmem_limit_bytes=40 << 20),
         cost_estimate=pl.CostEstimate(flops=30_000_000, transcendentals=1_100_000, bytes_accessed=2_000_000),
     )(mid)
 
 
-def run_a(top, bottom, x15, d1, sums):
+def run_p(early, top, bottom, middle, piece, d1):
+    whole = pl.BlockSpec(memory_space=pltpu.VMEM)
+    return pl.pallas_call(
+        kernel_p,
+        out_shape=(shape(240, LANES), shape(4, ROWS, LANES), shape(160, 4, HALF, LANES)),
+        in_specs=[pl.BlockSpec(memory_space=pltpu.SMEM)] + [whole] * 5,
+        out_specs=(whole,) * 3,
+        input_output_aliases={5: 2},
+        compiler_params=pltpu.CompilerParams(vmem_limit_bytes=40 << 20),
+        cost_estimate=pl.CostEstimate(flops=30_000_000, transcendentals=1_000_000, bytes_accessed=3_000_000),
+    )(early, top, bottom, middle, piece, d1)
+
+
+def run_a(early, top, bottom, x15, lum, d1, sums):
     whole = pl.BlockSpec(memory_space=pltpu.VMEM)
     return pl.pallas_call(
         kernel_a,
         out_shape=(
+            shape(4, ROWS, LANES),
             shape(160, 4, HALF, LANES),
             shape(80, 2, HALF, LANES),
             shape(40, 2, HALF, LANES),
@@ -618,13 +678,12 @@
             shape(4, 128, LANES),
             shape(2, 160, LANES),
         ),
-        in_specs=[whole] * 5,
-        out_specs=(whole,) * 8,
-        input_output_aliases={3: 0, 4: 6},
-        scratch_shapes=[vmem(4, ROWS, LANES)],
+        in_specs=[pl.BlockSpec(memory_space=pltpu.SMEM)] + [whole] * 6,
+        out_specs=(whole,) * 9,
+        input_output_aliases={4: 0, 5: 1, 6: 7},
         compiler_params=pltpu.CompilerParams(vmem_limit_bytes=40 << 20),
-        cost_estimate=pl.CostEstimate(flops=60_000_000, transcendentals=2_600_000, bytes_accessed=6_000_000),
-    )(top, bottom, x15, d1, sums)
+        cost_estimate=pl.CostEstimate(flops=1_000, transcendentals=0, bytes_accessed=1_000),
+    )(early, top, bottom, x15, lum, d1, sums)
 
 
 def run_b(gain, *arrays):
@@ -680,12 +739,21 @@
 def local(luminance, level_gain):
     top = lax.ppermute(luminance, "row", ring("row", 1))
     bottom = lax.ppermute(luminance, "row", ring("row", -1))
-    x15, base_term, mid_left, mid_right, d1, sums = run_z(luminance)
-    near_left = jnp.concatenate([top[32:, :LANES], mid_left, bottom[:96, :LANES]], axis=0)
-    near_right = jnp.concatenate([top[32:, 384:], mid_right, bottom[:96, 384:]], axis=0)
-    far_left = lax.ppermute(near_right, "col", ring("col", 1))
-    far_right = lax.ppermute(near_left, "col", ring("col", -1))
-    d1, d2, d3, g1, g2, g3, sums, c1a = run_a(top, bottom, x15, d1, sums)
+    x15, base_term, mid_left, mid_right, piece_left, piece_right, d1, sums = run_z(pltpu.with_memory_space_constraint(luminance, pltpu.HBM))
+    lane = lax.broadcasted_iota(jnp.int32, (240, LANES), 1)
+
+    def strip(columns, middle):
+        return [top[32:, columns], middle, bottom[:96, columns]]
+
+    first, last = slice(0, LANES), slice(384, 512)
+    near_left, near_right = [jnp.concatenate(strip(*x), axis=0) for x in ((first, mid_left), (last, mid_right))]
+    send_right = jnp.where(lane >= 32, jnp.concatenate(strip(last, mid_right[:48]), axis=0), piece_right)
+    far_left = lax.ppermute(send_right, "col", ring("col", 1))
+    piece_left, send_right = lax.optimization_barrier((piece_left, send_right))
+    early = (lax.axis_index("col") == 0).astype(jnp.int32)[None]
+    send_left, lum, d1 = run_p(early, top, bottom, mid_left, piece_left, d1)
+    far_right = lax.ppermute(send_left, "col", ring("col", -1))
+    _, d1, d2, d3, g1, g2, g3, sums, c1a = run_a(early, top, bottom, x15, lum, d1, sums)
     return run_b(
         level_gain, far_left, near_left, near_right, far_right, d2, d3, g1, g2, g3, base_term, sums, c1a
     )

time: 29.3 us -> 27.9 us (0.952)
  starting transfers between devices: 8.98 us -> 8.01 us
  local copies, waits for them, and re-layouts: 1 us -> 0.03 us
  Pallas kernels: 17.5 us -> 18 us
    unnamed x4 -> x2, local copies, waits for them, and re-layouts: 0.98 us -> 0.01 us
    ppermute x2, starting transfers between devices: 6.37 us -> 5.41 us  [the longest x1 4.04 us: local(): far_right = lax.ppermute(send_left, 'col', ring('col', -1))]
    pallas_call x1, Pallas kernels: 3.34 us -> 4.3 us  [run_z(): pl.pallas_call(kernel_z, out_shape=(shape(4, 128, LANES), shape(128, 512)...]
    pallas_call x1, Pallas kernels: 9.66 us -> 9.22 us  [run_b(): pl.pallas_call(kernel_b, out_shape=shape(128, 512), in_specs=[pl.BlockSpe...]
    pallas_call x1 -> x2, Pallas kernels: 4.46 us -> 4.43 us  [the longest x1 3.45 us: run_a(): pl.pallas_call(kernel_a, out_shape=(shape(4, ROWS, LANES), shape(160, 4,...]
  transfers between devices with their start and end apart: 4 -> 4, of which waited for: 1 -> 1; matrix products, arithmetic and copies ran while one was open for 0% -> 0% of each run, Pallas kernels for 27% -> 31%
where the time goes in v5:
time: 27.9 us; the launch traced here: 27.8 us
  Pallas kernels  18 us (65%)
  starting transfers between devices  8.01 us (29%)
  waiting for transfers between devices  1.66 us (6%)
    pallas_call x1, Pallas kernels, run_b(): pl.pallas_call(kernel_b, out_shape=shape(128, 512), in_specs=[pl.BlockSpe...  9.22 us
    pallas_call x1, Pallas kernels, run_z(): pl.pallas_call(kernel_z, out_shape=(shape(4, 128, LANES), shape(128, 512)...  4.3 us
    ppermute x1, starting transfers between devices, local(): far_right = lax.ppermute(send_left, 'col', ring('col', -1))  4.04 us
    pallas_call x1, Pallas kernels, run_a(): pl.pallas_call(kernel_a, out_shape=(shape(4, ROWS, LANES), shape(160, 4,...  3.45 us
    ppermute x1, starting transfers between devices, local(): top = lax.ppermute(luminance, 'row', ring('row', 1))  2.6 us
    ppermute x1, waiting for transfers between devices, local(): bottom = lax.ppermute(luminance, 'row', ring('row', -1))  1.65 us
    ppermute x1, starting transfers between devices, local(): far_left = lax.ppermute(send_right, 'col', ring('col', 1))  1.37 us
    pallas_call x1, Pallas kernels, run_p(): pl.pallas_call(kernel_p, out_shape=(shape(240, LANES), shape(4, ROWS, LAN...  0.98 us
  transfers between devices with their start and end apart: 4, of which 1 were waited for; matrix products, arithmetic and copies ran while one was open for 0% of the time, Pallas kernels for 31%

profile of v5, /device:TPU:1, one launch (start us, length us, event | category | flops | bytes accessed | tf_op | source)
XLA Modules:
  0.0 27.8 jit_solution(17475539033739236032)
XLA Ops:
  0.0 2.6 %collective-permute-start = (f32[128,512]{1,0:T(8,128)}, f32[128,512]{1,0:T(8,128)S(1)}, u32[]{:S(2)}, u32[]{:S(2)}) collective-permute-start(f32[128,512]{1,0:T(8,128)} %block.1), channel_id=1, source_target_pairs={{0,16},{16,32},{32,48},{48,64},{64,80},{80,96},{96,112},{112,0},{1... | collective-permute-start | bytes 786440 | tf_op jit(solution)/shard_map/ppermute | solution.py:740
  2.6 0.0 collective-permute-start.1
  2.6 4.3 %shard_map.28 = (f32[4,128,128]{2,1,0:T(8,128)S(1)}, f32[128,512]{1,0:T(8,128)S(1)}, f32[128,128]{1,0:T(8,128)S(1)}, f32[128,128]{1,0:T(8,128)S(1)}, f32[240,128...) custom-call(f32[128,512]{1,0:T(8,128)} %block.1), custom_call_target="tpu_custom_call" | custom-call | flops 30000000 | bytes 2000000 | tf_op jit(solution)/shard_map/pallas_call | solution.py:633
  6.9 0.0 collective-permute-done.top
  7.0 1.6 %collective-permute-done.1.bottom = f32[128,512]{1,0:T(8,128)S(1)} collective-permute-done((f32[128,512]{1,0:T(8,128)}, f32[128,512]{1,0:T(8,128)S(1)}, u32[]{:S(2)}, u32[]{:S(2)}) %collective-permute-start.1) | collective-permute-done | bytes 262176 | tf_op jit(solution)/shard_map/ppermute | solution.py:741
  8.6 1.4 %collective-permute-start.2 = (f32[240,128]{1,0:T(8,128)S(1)}, f32[240,128]{1,0:T(8,128)S(1)}, u32[]{:S(2)}, u32[]{:S(2)}) collective-permute-start(f32[240,128]{1,0:T(8,128)S(1)} %maximum_select_fusion), channel_id=1, source_target_pairs={{0,1},{1,2},{2,3},{3,4},{4,5},{5,6},{6,7},{7,8},{8,9},{9,10},{10,1... | collective-permute-start | bytes 368648 | tf_op jit(solution)/shard_map/ppermute | solution.py:751
  10.0 1.0 %shard_map.29 = (f32[240,128]{1,0:T(8,128)S(1)}, f32[4,320,128]{2,1,0:T(8,128)S(1)}, f32[160,4,8,128]{3,2,1,0:T(8,128)S(1)}) custom-call(s32[1]{0:T(128)} %bitcast.early, f32[128,512]{1,0:T(8,128)S(1)} %collective-permute-done.top, f32[128,512]{1,0:T(8,128)S(1)} %collective-permute-done.1.bottom, ...), custom_call_target="tpu_custom_call", output_to_operand_aliasing={{2}: (5, {})} | custom-call | flops 30000000 | bytes 3000000 | tf_op jit(solution)/shard_map/pallas_call | solution.py:655
  11.0 0.0 copy-start
  11.0 4.0 %collective-permute-start.3 = (f32[240,128]{1,0:T(8,128)S(1)}, f32[240,128]{1,0:T(8,128)S(1)}, u32[]{:S(2)}, u32[]{:S(2)}) collective-permute-start(f32[240,128]{1,0:T(8,128)S(1)} %get-tuple-element.30), channel_id=1, source_target_pairs={{0,15},{1,0},{2,1},{3,2},{4,3},{5,4},{6,5},{7,6},{8,7},{9,8},{10,9... | collective-permute-start | bytes 368648 | tf_op jit(solution)/shard_map/ppermute | solution.py:755
  15.1 3.5 %shard_map.30 = (f32[4,320,128]{2,1,0:T(8,128)S(1)}, f32[160,4,8,128]{3,2,1,0:T(8,128)S(1)}, f32[80,2,8,128]{3,2,1,0:T(8,128)S(1)}, f32[40,2,8,128]{3,2,1,0:T(8,...) custom-call(s32[1]{0:T(128)} %bitcast.early, ...), custom_call_target="tpu_custom_call", output_to_operand_aliasing={{0}: (4, {}), {1}: (5, {}), {7}: (6, {})} | custom-call | flops 1000 | bytes 1000 | tf_op jit(solution)/shard_map/pallas_call | solution.py:668
  18.5 0.0 collective-permute-done.2.far_left
  18.6 0.0 collective-permute-done.3.far_right
  18.6 0.0 copy-done
  18.6 9.2 %shard_map.31 = f32[128,512]{1,0:T(8,128)} custom-call(f32[5]{0:T(128)S(1)} %copy-done, f32[240,128]{1,0:T(8,128)S(1)} %collective-permute-done.2.far_left, f32[320,128]{1,0:T(8,128)S(1)} %get-tuple-element.47.near_left, f32[320,128]{1,0:T(8,128)S(1)} %get-tuple-element.48.near_right, f32[240,128]{1,0:T(8,128)S(1)} %collective-permute-done.3.far_right, ...), custom_call_target="tpu_custom_call" | custom-call | flops 60000000 | bytes 6000000 | tf_op jit(solution)/shard_map/pallas_call | solution.py:691
  (6 shorter events, 0.1 us)
Async XLA Ops:
  0.0 6.9 %collective-permute-start = (f32[128,512]{1,0:T(8,128)}, f32[128,512]{1,0:T(8,128)S(1)}, u32[]{:S(2)}, u32[]{:S(2)}) collective-permute-start(f32[128,512]{1,0:T(8,128)} %block.1), channel_id=1, source_target_pairs={{0,16},{16,32},{32,48},{48,64},{64,80},{80,96},{96,112},{112,0},{1... | collective-permute-start | bytes 786440 | tf_op jit(solution)/shard_map/ppermute | solution.py:740
  2.6 6.0 %collective-permute-start.1 = (f32[128,512]{1,0:T(8,128)}, f32[128,512]{1,0:T(8,128)S(1)}, u32[]{:S(2)}, u32[]{:S(2)}) collective-permute-start(f32[128,512]{1,0:T(8,128)} %block.1), channel_id=1, source_target_pairs={{0,112},{16,0},{32,16},{48,32},{64,48},{80,64},{96,80},{112,96},{1... | collective-permute-start | bytes 786440 | tf_op jit(solution)/shard_map/ppermute | solution.py:741
  8.6 9.9 %collective-permute-start.2 = (f32[240,128]{1,0:T(8,128)S(1)}, f32[240,128]{1,0:T(8,128)S(1)}, u32[]{:S(2)}, u32[]{:S(2)}) collective-permute-start(f32[240,128]{1,0:T(8,128)S(1)} %maximum_select_fusion), channel_id=1, source_target_pairs={{0,1},{1,2},{2,3},{3,4},{4,5},{5,6},{6,7},{7,8},{8,9},{9,10},{10,1... | collective-permute-start | bytes 368648 | tf_op jit(solution)/shard_map/ppermute | solution.py:751
  11.0 7.6 %copy-start = (f32[5]{0:T(128)S(1)}, f32[5]{0:T(128)}, u32[]{:S(2)}) copy-start(f32[5]{0:T(128)} %gain_ref.1) | copy-start | bytes 64
  11.0 7.5 %collective-permute-start.3 = (f32[240,128]{1,0:T(8,128)S(1)}, f32[240,128]{1,0:T(8,128)S(1)}, u32[]{:S(2)}, u32[]{:S(2)}) collective-permute-start(f32[240,128]{1,0:T(8,128)S(1)} %get-tuple-element.30), channel_id=1, source_target_pairs={{0,15},{1,0},{2,1},{3,2},{4,3},{5,4},{6,5},{7,6},{8,7},{9,8},{10,9... | collective-permute-start | bytes 368648 | tf_op jit(solution)/shard_map/ppermute | solution.py:755

commit v6 on v5

--- a/solution.py
+++ b/solution.py
@@ -373,7 +373,7 @@
             lum[2 * pair, start : start + count, :] = jnp.where(low_half, a, b)
             lum[2 * pair + 1, start : start + count, :] = jnp.where(low_half, b, a)
     guide_chain(lum, 1.0 / BETA, h1, h2, h3)
-    first_level(lum, [split * (BETA * STEP)], s1, 2, 159, 53)
+    first_level(lum, [split * (BETA * STEP)], s1, 2, 159, 79)
     next_levels(s1, s2, s3, 1)
 
     first, last = lane == 0, lane == 127

time: 27.9 us -> 27.8 us (level)
  transfers between devices with their start and end apart: 4 -> 4, of which waited for: 1 -> 1; matrix products, arithmetic and copies ran while one was open for 0% -> 0% of each run, Pallas kernels for 31% -> 32%
where the time goes in v6:
time: 27.8 us; the launch traced here: 27.6 us
  Pallas kernels  17.8 us (64%)
  starting transfers between devices  8.01 us (29%)
  waiting for transfers between devices  1.66 us (6%)
    pallas_call x1, Pallas kernels, run_b(): pl.pallas_call(kernel_b, out_shape=shape(128, 512), in_specs=[pl.BlockSpe...  9.03 us
    pallas_call x1, Pallas kernels, run_z(): pl.pallas_call(kernel_z, out_shape=(shape(4, 128, LANES), shape(128, 512)...  4.3 us
    ppermute x1, starting transfers between devices, local(): far_right = lax.ppermute(send_left, 'col', ring('col', -1))  4.04 us
    pallas_call x1, Pallas kernels, run_a(): pl.pallas_call(kernel_a, out_shape=(shape(4, ROWS, LANES), shape(160, 4,...  3.45 us
    ppermute x1, starting transfers between devices, local(): top = lax.ppermute(luminance, 'row', ring('row', 1))  2.6 us
    ppermute x1, waiting for transfers between devices, local(): bottom = lax.ppermute(luminance, 'row', ring('row', -1))  1.65 us
    ppermute x1, starting transfers between devices, local(): far_left = lax.ppermute(send_right, 'col', ring('col', 1))  1.37 us
    pallas_call x1, Pallas kernels, run_p(): pl.pallas_call(kernel_p, out_shape=(shape(240, LANES), shape(4, ROWS, LAN...  0.98 us
  transfers between devices with their start and end apart: 4, of which 1 were waited for; matrix products, arithmetic and copies ran while one was open for 0% of the time, Pallas kernels for 32%

profile of v6, /device:TPU:1, one launch (start us, length us, event | category | flops | bytes accessed | tf_op | source)
XLA Modules:
  0.0 27.6 jit_solution(10544801294064025853)
XLA Ops:
  0.0 2.6 %collective-permute-start = (f32[128,512]{1,0:T(8,128)}, f32[128,512]{1,0:T(8,128)S(1)}, u32[]{:S(2)}, u32[]{:S(2)}) collective-permute-start(f32[128,512]{1,0:T(8,128)} %block.1), channel_id=1, source_target_pairs={{0,16},{16,32},{32,48},{48,64},{64,80},{80,96},{96,112},{112,0},{1... | collective-permute-start | bytes 786440 | tf_op jit(solution)/shard_map/ppermute | solution.py:740
  2.6 0.0 collective-permute-start.1
  2.6 4.3 %shard_map.28 = (f32[4,128,128]{2,1,0:T(8,128)S(1)}, f32[128,512]{1,0:T(8,128)S(1)}, f32[128,128]{1,0:T(8,128)S(1)}, f32[128,128]{1,0:T(8,128)S(1)}, f32[240,128...) custom-call(f32[128,512]{1,0:T(8,128)} %block.1), custom_call_target="tpu_custom_call" | custom-call | flops 30000000 | bytes 2000000 | tf_op jit(solution)/shard_map/pallas_call | solution.py:633
  6.9 0.0 collective-permute-done.top
  7.0 1.6 %collective-permute-done.1.bottom = f32[128,512]{1,0:T(8,128)S(1)} collective-permute-done((f32[128,512]{1,0:T(8,128)}, f32[128,512]{1,0:T(8,128)S(1)}, u32[]{:S(2)}, u32[]{:S(2)}) %collective-permute-start.1) | collective-permute-done | bytes 262176 | tf_op jit(solution)/shard_map/ppermute | solution.py:741
  8.6 1.4 %collective-permute-start.2 = (f32[240,128]{1,0:T(8,128)S(1)}, f32[240,128]{1,0:T(8,128)S(1)}, u32[]{:S(2)}, u32[]{:S(2)}) collective-permute-start(f32[240,128]{1,0:T(8,128)S(1)} %maximum_select_fusion), channel_id=1, source_target_pairs={{0,1},{1,2},{2,3},{3,4},{4,5},{5,6},{6,7},{7,8},{8,9},{9,10},{10,1... | collective-permute-start | bytes 368648 | tf_op jit(solution)/shard_map/ppermute | solution.py:751
  10.0 1.0 %shard_map.29 = (f32[240,128]{1,0:T(8,128)S(1)}, f32[4,320,128]{2,1,0:T(8,128)S(1)}, f32[160,4,8,128]{3,2,1,0:T(8,128)S(1)}) custom-call(s32[1]{0:T(128)} %bitcast.early, f32[128,512]{1,0:T(8,128)S(1)} %collective-permute-done.top, f32[128,512]{1,0:T(8,128)S(1)} %collective-permute-done.1.bottom, ...), custom_call_target="tpu_custom_call", output_to_operand_aliasing={{2}: (5, {})} | custom-call | flops 30000000 | bytes 3000000 | tf_op jit(solution)/shard_map/pallas_call | solution.py:655
  11.0 0.0 copy-start
  11.0 4.0 %collective-permute-start.3 = (f32[240,128]{1,0:T(8,128)S(1)}, f32[240,128]{1,0:T(8,128)S(1)}, u32[]{:S(2)}, u32[]{:S(2)}) collective-permute-start(f32[240,128]{1,0:T(8,128)S(1)} %get-tuple-element.30), channel_id=1, source_target_pairs={{0,15},{1,0},{2,1},{3,2},{4,3},{5,4},{6,5},{7,6},{8,7},{9,8},{10,9... | collective-permute-start | bytes 368648 | tf_op jit(solution)/shard_map/ppermute | solution.py:755
  15.1 3.5 %shard_map.30 = (f32[4,320,128]{2,1,0:T(8,128)S(1)}, f32[160,4,8,128]{3,2,1,0:T(8,128)S(1)}, f32[80,2,8,128]{3,2,1,0:T(8,128)S(1)}, f32[40,2,8,128]{3,2,1,0:T(8,...) custom-call(s32[1]{0:T(128)} %bitcast.early, ...), custom_call_target="tpu_custom_call", output_to_operand_aliasing={{0}: (4, {}), {1}: (5, {}), {7}: (6, {})} | custom-call | flops 1000 | bytes 1000 | tf_op jit(solution)/shard_map/pallas_call | solution.py:668
  18.5 0.0 collective-permute-done.2.far_left
  18.6 0.0 collective-permute-done.3.far_right
  18.6 0.0 copy-done
  18.6 9.0 %shard_map.31 = f32[128,512]{1,0:T(8,128)} custom-call(f32[5]{0:T(128)S(1)} %copy-done, f32[240,128]{1,0:T(8,128)S(1)} %collective-permute-done.2.far_left, f32[320,128]{1,0:T(8,128)S(1)} %get-tuple-element.47.near_left, f32[320,128]{1,0:T(8,128)S(1)} %get-tuple-element.48.near_right, f32[240,128]{1,0:T(8,128)S(1)} %collective-permute-done.3.far_right, ...), custom_call_target="tpu_custom_call" | custom-call | flops 60000000 | bytes 6000000 | tf_op jit(solution)/shard_map/pallas_call | solution.py:691
  (6 shorter events, 0.1 us)
Async XLA Ops:
  0.0 6.9 %collective-permute-start = (f32[128,512]{1,0:T(8,128)}, f32[128,512]{1,0:T(8,128)S(1)}, u32[]{:S(2)}, u32[]{:S(2)}) collective-permute-start(f32[128,512]{1,0:T(8,128)} %block.1), channel_id=1, source_target_pairs={{0,16},{16,32},{32,48},{48,64},{64,80},{80,96},{96,112},{112,0},{1... | collective-permute-start | bytes 786440 | tf_op jit(solution)/shard_map/ppermute | solution.py:740
  2.6 6.0 %collective-permute-start.1 = (f32[128,512]{1,0:T(8,128)}, f32[128,512]{1,0:T(8,128)S(1)}, u32[]{:S(2)}, u32[]{:S(2)}) collective-permute-start(f32[128,512]{1,0:T(8,128)} %block.1), channel_id=1, source_target_pairs={{0,112},{16,0},{32,16},{48,32},{64,48},{80,64},{96,80},{112,96},{1... | collective-permute-start | bytes 786440 | tf_op jit(solution)/shard_map/ppermute | solution.py:741
  8.6 9.9 %collective-permute-start.2 = (f32[240,128]{1,0:T(8,128)S(1)}, f32[240,128]{1,0:T(8,128)S(1)}, u32[]{:S(2)}, u32[]{:S(2)}) collective-permute-start(f32[240,128]{1,0:T(8,128)S(1)} %maximum_select_fusion), channel_id=1, source_target_pairs={{0,1},{1,2},{2,3},{3,4},{4,5},{5,6},{6,7},{7,8},{8,9},{9,10},{10,1... | collective-permute-start | bytes 368648 | tf_op jit(solution)/shard_map/ppermute | solution.py:751
  11.0 7.6 %copy-start = (f32[5]{0:T(128)S(1)}, f32[5]{0:T(128)}, u32[]{:S(2)}) copy-start(f32[5]{0:T(128)} %gain_ref.1) | copy-start | bytes 64
  11.0 7.5 %collective-permute-start.3 = (f32[240,128]{1,0:T(8,128)S(1)}, f32[240,128]{1,0:T(8,128)S(1)}, u32[]{:S(2)}, u32[]{:S(2)}) collective-permute-start(f32[240,128]{1,0:T(8,128)S(1)} %get-tuple-element.30), channel_id=1, source_target_pairs={{0,15},{1,0},{2,1},{3,2},{4,3},{5,4},{6,5},{7,6},{8,7},{9,8},{10,9... | collective-permute-start | bytes 368648 | tf_op jit(solution)/shard_map/ppermute | solution.py:755
